TPU v7x, 32 devices: a whole 2x2x4 slice. The times are simulated.
32 devices in a mesh: dp: 4 (over z), tensor: 8 (over y, x, core).
Axes of the slice: x: 2, y: 2, z: 4, core: 2. Of those that a mesh axis runs over, the one named last changes fastest.
Arguments:
- hidden_input: bfloat16 [16384, 2048], P(('dp', 'tensor')), may hold values from -6 to 6
- first_gain: bfloat16 [2048], replicated, may hold values from 0.5 to 1.5
- first_shift: bfloat16 [2048], replicated, may hold values from -3 to 3
- qkv_weight: bfloat16 [2048, 6144], P('dp', 'tensor'), may hold values from -0.125 to 0.125
- query_bias: bfloat16 [2048], P('tensor'), may hold values from -3 to 3
- value_bias: bfloat16 [2048], P('tensor'), may hold values from -3 to 3
- dense_weight: bfloat16 [2048, 2048], P('tensor', 'dp'), may hold values from -0.5 to 0.5
- dense_bias: bfloat16 [2048], replicated, may hold values from -3 to 3
- second_gain: bfloat16 [2048], replicated, may hold values from 0.5 to 1.5
- second_shift: bfloat16 [2048], replicated, may hold values from -3 to 3
- up_weight: bfloat16 [2048, 8192], P('dp', 'tensor'), may hold values from -0.125 to 0.125
- up_bias: bfloat16 [8192], P('tensor'), may hold values from -3 to 3
- down_weight: bfloat16 [8192, 2048], P('tensor', 'dp'), may hold values from -0.0625 to 0.0625
- down_bias: bfloat16 [2048], replicated, may hold values from -3 to 3
- segments: int32 [16384], P('dp'), may hold values from 0 to 17, as said below
- document_lengths: int32 [16, 18], P('dp'), may hold values from 0 to 800, as said below
- cotangent: bfloat16 [16384, 2048], P(('dp', 'tensor')), may hold values from -6 to 6
Outputs:
- hidden_output: bfloat16 [16384, 2048], P(('dp', 'tensor'))
- grad_input: float32 [16384, 2048], P(('dp', 'tensor'))
- grad_first_gain: float32 [2048], replicated
- grad_first_shift: float32 [2048], replicated
- grad_qkv_weight: float32 [2048, 6144], P('dp', 'tensor')
- grad_query_bias: float32 [2048], P('tensor')
- grad_value_bias: float32 [2048], P('tensor')
- grad_dense_weight: float32 [2048, 2048], P('tensor', 'dp')
- grad_dense_bias: float32 [2048], replicated
- grad_second_gain: float32 [2048], replicated
- grad_second_shift: float32 [2048], replicated
- grad_up_weight: float32 [2048, 8192], P('dp', 'tensor')
- grad_up_bias: float32 [8192], P('tensor')
- grad_down_weight: float32 [8192, 2048], P('tensor', 'dp')
- grad_down_bias: float32 [2048], replicated
Inputs may be any that keep to these rules, and one draw needn't show every extreme that they name: `segments`: within each packed sequence the numbers start at 0 and never fall, each document's run matches its entry of document_lengths, and tokens after the last document carry the next number. `document_lengths`: each row holds documents of 60 to 800 tokens first, then zeros; a row's sum is at most 1024.
All inputs are finite; a program needn't handle non-finite values.
Results may differ from a plain program's by a relative error of at most 0.02.
Values may be sent and summed in bfloat16 or wider, within the bound.
A program may use at most 256 MiB of HBM per device.

v0:
```python
import math

import jax
import jax.numpy as jnp
from jax import lax
from jax.sharding import PartitionSpec as P

HEADS = 16
HEAD_DIM = 128


def gelu_tanh(value):
    return (
        0.5
        * value
        * (1.0 + jnp.tanh(0.7978845608028654 * (value + 0.044715 * value * value * value)))
    )


def normalize(rows):
    center = rows - jnp.mean(rows, axis=1, keepdims=True)
    factor = lax.rsqrt(jnp.mean(center * center, axis=1, keepdims=True) + 1e-05)
    return (center * factor, factor)


def norm_back(grad_out, normed, factor, gain):
    scaled = grad_out * gain
    return factor * (
        scaled
        - jnp.mean(scaled, axis=1, keepdims=True)
        - normed * jnp.mean(scaled * normed, axis=1, keepdims=True)
    )


def allowed_mask(labels, lengths):
    length = labels.shape[0]
    position = lax.broadcasted_iota(jnp.int32, (length, length), 0)
    other = lax.broadcasted_iota(jnp.int32, (length, length), 1)
    filled = jnp.sum(lengths)
    same = labels[:, None] == labels[None, :]
    allowed = same & (other <= position) & ((other < filled) | (other == position))
    return (allowed, (other - position).astype(jnp.float32))


def head_scores(queries, keys, slopes, labels, lengths):
    allowed, distance = allowed_mask(labels, lengths)
    raw = jnp.einsum("qhd,khd->hqk", queries, keys, preferred_element_type=jnp.float32) * (
        1.0 / math.sqrt(HEAD_DIM)
    )
    raw = raw + slopes[:, None, None] * distance[None]
    return jnp.where(allowed[None], raw, -1e30)


def attend_forward(item, slopes):
    queries, keys, values, labels, lengths = item
    masked = head_scores(queries, keys, slopes, labels, lengths)
    top = jnp.max(masked, axis=2, keepdims=True)
    expo = jnp.exp(masked - top)
    total = jnp.sum(expo, axis=2, keepdims=True)
    probs = (expo / total).astype(jnp.bfloat16)
    mixed = jnp.einsum("hqk,khd->qhd", probs, values, preferred_element_type=jnp.float32)
    return (mixed.astype(jnp.bfloat16), (top + jnp.log(total))[:, :, 0])


def attend_backward(item, slopes):
    queries, keys, values, labels, lengths, logsum, grad_mixed = item
    masked = head_scores(queries, keys, slopes, labels, lengths)
    probs = jnp.exp(masked - logsum[:, :, None])
    rounded = probs.astype(jnp.bfloat16)
    grad_probs = jnp.einsum("qhd,khd->hqk", grad_mixed, values, preferred_element_type=jnp.float32)
    grad_scores = (
        probs * (grad_probs - jnp.sum(probs * grad_probs, axis=2, keepdims=True))
    ).astype(jnp.bfloat16)
    factor = 1.0 / math.sqrt(HEAD_DIM)
    grad_queries = (
        jnp.einsum("hqk,khd->qhd", grad_scores, keys, preferred_element_type=jnp.float32) * factor
    ).astype(jnp.bfloat16)
    grad_keys = (
        jnp.einsum("hqk,qhd->khd", grad_scores, queries, preferred_element_type=jnp.float32)
        * factor
    ).astype(jnp.bfloat16)
    grad_values = jnp.einsum(
        "hqk,qhd->khd", rounded, grad_mixed, preferred_element_type=jnp.float32
    ).astype(jnp.bfloat16)
    return (grad_queries, grad_keys, grad_values)


def on_device(
    hidden_input,
    first_gain,
    first_shift,
    qkv_weight,
    query_bias,
    value_bias,
    dense_weight,
    dense_bias,
    second_gain,
    second_shift,
    up_weight,
    up_bias,
    down_weight,
    down_bias,
    segments,
    document_lengths,
    cotangent,
):
    heads_local = query_bias.shape[0] // HEAD_DIM
    first_gain32 = first_gain.astype(jnp.float32)
    second_gain32 = second_gain.astype(jnp.float32)
    inputs = hidden_input.astype(jnp.float32)
    normed_first, factor_first = normalize(inputs)
    attn_input = (normed_first * first_gain32 + first_shift.astype(jnp.float32)).astype(
        jnp.bfloat16
    )
    attn_rows = lax.all_gather(attn_input, "tensor", axis=0, tiled=True)
    project_full, dense_full, expand_full, shrink_full = (
        lax.all_gather(qkv_weight, "dp", axis=0, tiled=True),
        lax.all_gather(dense_weight, "dp", axis=1, tiled=True),
        lax.all_gather(up_weight, "dp", axis=0, tiled=True),
        lax.all_gather(down_weight, "dp", axis=1, tiled=True),
    )
    group_rows = attn_rows.shape[0]
    sequences = document_lengths.shape[0]
    length = group_rows // sequences
    heads_index = lax.axis_index("tensor") * heads_local + lax.broadcasted_iota(
        jnp.int32, (heads_local,), 0
    )
    slopes = jnp.exp2(-8.0 * (heads_index.astype(jnp.float32) + 1.0) / HEADS)
    projected = jnp.dot(attn_rows, project_full, preferred_element_type=jnp.float32).reshape(
        group_rows, heads_local, 3, HEAD_DIM
    )
    queries = (
        projected[:, :, 0] + query_bias.astype(jnp.float32).reshape(heads_local, HEAD_DIM)
    ).astype(jnp.bfloat16)
    keys = projected[:, :, 1].astype(jnp.bfloat16)
    values = (
        projected[:, :, 2] + value_bias.astype(jnp.float32).reshape(heads_local, HEAD_DIM)
    ).astype(jnp.bfloat16)
    shape_four = (sequences, length, heads_local, HEAD_DIM)
    query_seq = queries.reshape(shape_four)
    key_seq = keys.reshape(shape_four)
    value_seq = values.reshape(shape_four)
    label_seq = segments.reshape(sequences, length)
    mixed, logsum = lax.map(
        lambda item: attend_forward(item, slopes),
        (query_seq, key_seq, value_seq, label_seq, document_lengths),
    )
    mixed = mixed.reshape(group_rows, heads_local * HEAD_DIM)
    attn_out = lax.psum_scatter(
        jnp.dot(mixed, dense_full, preferred_element_type=jnp.float32).astype(jnp.bfloat16),
        "tensor",
        scatter_dimension=0,
        tiled=True,
    ).astype(jnp.float32)
    residual = inputs + attn_out + dense_bias.astype(jnp.float32)
    normed_second, factor_second = normalize(residual)
    mlp_input = (normed_second * second_gain32 + second_shift.astype(jnp.float32)).astype(
        jnp.bfloat16
    )
    mlp_rows = lax.all_gather(mlp_input, "tensor", axis=0, tiled=True)
    pre_act = jnp.dot(mlp_rows, expand_full, preferred_element_type=jnp.float32) + up_bias.astype(
        jnp.float32
    )
    activated = gelu_tanh(pre_act).astype(jnp.bfloat16)
    mlp_out = lax.psum_scatter(
        jnp.dot(activated, shrink_full, preferred_element_type=jnp.float32).astype(jnp.bfloat16),
        "tensor",
        scatter_dimension=0,
        tiled=True,
    ).astype(jnp.float32)
    hidden_output = (residual + mlp_out + down_bias.astype(jnp.float32)).astype(jnp.bfloat16)
    grad_rows = lax.all_gather(cotangent, "tensor", axis=0, tiled=True)
    grad_down = jnp.einsum("tf,td->fd", activated, grad_rows, preferred_element_type=jnp.float32)
    grad_act = jnp.einsum("td,fd->tf", grad_rows, shrink_full, preferred_element_type=jnp.float32)
    grad_pre = jax.vjp(gelu_tanh, pre_act)[1](grad_act)[0].astype(jnp.bfloat16)
    grad_up = jnp.einsum("td,tf->df", mlp_rows, grad_pre, preferred_element_type=jnp.float32)
    sum_up_bias = jnp.sum(grad_pre.astype(jnp.float32), axis=0)
    grad_mlp_in = lax.psum_scatter(
        jnp.einsum("tf,df->td", grad_pre, expand_full, preferred_element_type=jnp.float32).astype(
            jnp.bfloat16
        ),
        "tensor",
        scatter_dimension=0,
        tiled=True,
    ).astype(jnp.float32)
    cotangent32 = cotangent.astype(jnp.float32)
    grad_residual = cotangent32 + norm_back(
        grad_mlp_in, normed_second, factor_second, second_gain32
    )
    sum_second_gain = jnp.sum(grad_mlp_in * normed_second, axis=0)
    sum_second_shift = jnp.sum(grad_mlp_in, axis=0)
    sum_down_bias = jnp.sum(cotangent32, axis=0)
    sum_dense_bias = jnp.sum(grad_residual, axis=0)
    grad_attn_rows = lax.all_gather(
        grad_residual.astype(jnp.bfloat16), "tensor", axis=0, tiled=True
    )
    grad_dense = jnp.einsum("tc,td->cd", mixed, grad_attn_rows, preferred_element_type=jnp.float32)
    grad_mixed = jnp.einsum(
        "td,cd->tc", grad_attn_rows, dense_full, preferred_element_type=jnp.float32
    ).astype(jnp.bfloat16)
    grad_queries, grad_keys, grad_values = lax.map(
        lambda item: attend_backward(item, slopes),
        (
            query_seq,
            key_seq,
            value_seq,
            label_seq,
            document_lengths,
            logsum,
            grad_mixed.reshape(shape_four),
        ),
    )
    grad_proj = jnp.stack((grad_queries, grad_keys, grad_values), axis=3).reshape(
        group_rows, heads_local * 3 * HEAD_DIM
    )
    sum_query_bias = jnp.sum(grad_queries.astype(jnp.float32), axis=(0, 1)).reshape(
        heads_local * HEAD_DIM
    )
    sum_value_bias = jnp.sum(grad_values.astype(jnp.float32), axis=(0, 1)).reshape(
        heads_local * HEAD_DIM
    )
    grad_project = jnp.einsum("td,tc->dc", attn_rows, grad_proj, preferred_element_type=jnp.float32)
    grad_attn_in = lax.psum_scatter(
        jnp.einsum("tc,dc->td", grad_proj, project_full, preferred_element_type=jnp.float32).astype(
            jnp.bfloat16
        ),
        "tensor",
        scatter_dimension=0,
        tiled=True,
    ).astype(jnp.float32)
    grad_input = grad_residual + norm_back(grad_attn_in, normed_first, factor_first, first_gain32)
    sum_first_gain = jnp.sum(grad_attn_in * normed_first, axis=0)
    sum_first_shift = jnp.sum(grad_attn_in, axis=0)
    grad_qkv_weight, grad_dense_weight, grad_up_weight, grad_down_weight = (
        lax.psum_scatter(
            grad_project.astype(jnp.bfloat16), "dp", scatter_dimension=0, tiled=True
        ).astype(jnp.float32),
        lax.psum_scatter(
            grad_dense.astype(jnp.bfloat16), "dp", scatter_dimension=1, tiled=True
        ).astype(jnp.float32),
        lax.psum_scatter(
            grad_up.astype(jnp.bfloat16), "dp", scatter_dimension=0, tiled=True
        ).astype(jnp.float32),
        lax.psum_scatter(
            grad_down.astype(jnp.bfloat16), "dp", scatter_dimension=1, tiled=True
        ).astype(jnp.float32),
    )
    grad_query_bias, grad_value_bias, grad_up_bias = lax.psum(
        (sum_query_bias, sum_value_bias, sum_up_bias), "dp"
    )
    (
        grad_first_gain,
        grad_first_shift,
        grad_second_gain,
        grad_second_shift,
        grad_dense_bias,
        grad_down_bias,
    ) = lax.psum(
        (
            sum_first_gain,
            sum_first_shift,
            sum_second_gain,
            sum_second_shift,
            sum_dense_bias,
            sum_down_bias,
        ),
        ("dp", "tensor"),
    )
    return (
        hidden_output,
        grad_input,
        grad_first_gain,
        grad_first_shift,
        grad_qkv_weight,
        grad_query_bias,
        grad_value_bias,
        grad_dense_weight,
        grad_dense_bias,
        grad_second_gain,
        grad_second_shift,
        grad_up_weight,
        grad_up_bias,
        grad_down_weight,
        grad_down_bias,
    )


def solution(mesh):
    return jax.shard_map(
        on_device,
        mesh=mesh,
        in_specs=(
            P(("dp", "tensor"), None),
            P(),
            P(),
            P("dp", "tensor"),
            P("tensor"),
            P("tensor"),
            P("tensor", "dp"),
            P(),
            P(),
            P(),
            P("dp", "tensor"),
            P("tensor"),
            P("tensor", "dp"),
            P(),
            P("dp"),
            P("dp", None),
            P(("dp", "tensor"), None),
        ),
        out_specs=(
            P(("dp", "tensor"), None),
            P(("dp", "tensor"), None),
            P(),
            P(),
            P("dp", "tensor"),
            P("tensor"),
            P("tensor"),
            P("tensor", "dp"),
            P(),
            P(),
            P(),
            P("dp", "tensor"),
            P("tensor"),
            P("tensor", "dp"),
            P(),
        ),
        check_vma=False,
    )
```

profile of v0, /device:TPU:0, one launch (start us, length us, event | category | flops | bytes accessed | tf_op | source)
XLA Modules:
  0.0 1625.5 jit_solution(15093619472249127329)
XLA Ops:
  15.7 60.0 %all-gather.11.cloned.1.call-done = bf16[2048,768]{1,0:T(8,128)(2,1)} async-done(((bf16[512,768]{1,0:T(8,128)(2,1)}), bf16[2048,768]{1,0:T(8,128)(2,1)}) %all-gather.11.cloned.1.call-update) | async-done | bytes 3145744 | tf_op jit(solution)/shard_map/all_gather | solution.py:117
  75.8 90.9 %all-gather.9.cloned.1.call-done = bf16[4096,2048]{1,0:T(8,128)(2,1)} async-done(((bf16[512,2048]{1,0:T(8,128)(2,1)}), bf16[4096,2048]{1,0:T(8,128)(2,1)}) %all-gather.9.cloned.1.call-update) | async-done | bytes 16777232 | tf_op jit(solution)/shard_map/all_gather | solution.py:115
  166.6 20.4 %fusion.97 = f32[4096,768]{0,1:T(8,128)} fusion(bf16[4096,2048]{1,0:T(8,128)(2,1)} %all-gather.9.cloned.1.call-done, bf16[2048,768]{1,0:T(8,128)(2,1)} %all-gather.11.cloned.1.call-done), kind=kOutput, calls=%fused_computation.160 | convolution fusion | flops 12884901888 | bytes 32505856 | tf_op jit(solution)/shard_map/dot_general | solution.py:129
  224.8 67.4 %while.28 = (s32[]{:T(128)}, bf16[4,1024,2,128]{3,2,1,0:T(2,128)(2,1)S(1)}, f32[4,2,1024]{2,1,0:T(2,128)}, bf16[4,1024,2,128]{3,1,0,2:T(8,128)(2,1)}, s32[4,1024...) while((s32[]{:T(128)}, ...), condition=%wide.region_6.7_spmd.clone, body=%wide.region_2.6_spmd.clone.sunk | while | flops 1120140288 | bytes 50412788 | solution.py:144
  303.6 115.1 %reduce-scatter.9.cloned.1.call-done = bf16[512,2048]{1,0:T(8,128)(2,1)} async-done(((bf16[4096,2048]{1,0:T(8,128)(2,1)}), bf16[512,2048]{1,0:T(8,128)(2,1)}) %reduce-scatter.9.cloned.1.call-update) | async-done | bytes 2097168 | tf_op jit(solution)/shard_map/reduce_scatter | solution.py:149
  427.1 73.8 %all-gather.17.cloned.1.call-done = bf16[2048,1024]{1,0:T(8,128)(2,1)} async-done(((bf16[512,1024]{1,0:T(8,128)(2,1)}), bf16[2048,1024]{1,0:T(8,128)(2,1)}) %all-gather.17.cloned.1.call-update) | async-done | bytes 4194320 | tf_op jit(solution)/shard_map/all_gather | solution.py:119
  500.9 90.6 %all-gather.15.cloned.1.call-done = bf16[4096,2048]{1,0:T(8,128)(2,1)} async-done(((bf16[512,2048]{1,0:T(8,128)(2,1)}), bf16[4096,2048]{1,0:T(8,128)(2,1)}) %all-gather.15.cloned.1.call-update) | async-done | bytes 16777232 | tf_op jit(solution)/shard_map/all_gather | solution.py:160
  591.5 23.4 %fusion.98 = f32[4096,1024]{1,0:T(8,128)} fusion(bf16[4096,2048]{1,0:T(8,128)(2,1)} %all-gather.15.cloned.1.call-done, bf16[2048,1024]{1,0:T(8,128)(2,1)} %all-gather.17.cloned.1.call-done), kind=kOutput, calls=%fused_computation.161 | convolution fusion | flops 17179869184 | bytes 37748736 | tf_op jit(solution)/shard_map/dot_general | solution.py:161
  614.9 58.9 %all-gather.19.cloned.1.call-done = bf16[1024,2048]{1,0:T(8,128)(2,1)} async-done(((bf16[1024,512]{1,0:T(8,128)(2,1)}), bf16[1024,2048]{1,0:T(8,128)(2,1)}) %all-gather.19.cloned.1.call-update) | async-done | bytes 4194320 | tf_op jit(solution)/shard_map/all_gather | solution.py:120
  673.8 90.1 %all-gather.21.cloned.1.call-done = bf16[4096,2048]{1,0:T(8,128)(2,1)} async-done(((bf16[512,2048]{1,0:T(8,128)(2,1)}), bf16[4096,2048]{1,0:T(8,128)(2,1)}) %all-gather.21.cloned.1.call-update) | async-done | bytes 16777232 | tf_op jit(solution)/shard_map/all_gather | solution.py:172
  763.9 39.2 %convert_reduce_fusion = (f32[1024]{0:T(1024)}, bf16[4096,1024]{1,0:T(8,128)(2,1)}) fusion(f32[4096,1024]{1,0:T(8,128)} %fusion.98, f32[1024]{0:T(1024)S(1)} %convert_element_type.184, bf16[4096,2048]{1,0:T(8,128)(2,1)} %all-gather.21.cloned.1.call-done, bf16[1024,2048]{1,0:T(8,128)(2,1)} %all-gather.19.cloned.1.call-done), kind=kOutput, calls=%fused_computation.89 | convolution fusion | flops 17293115392 | bytes 46145536 | tf_op jit(solution)/shard_map/td,fd->tf/dot_general | solution.py:174
  803.1 23.9 %convolution_convert_fusion.1 = bf16[4096,2048]{1,0:T(8,128)(2,1)} fusion(bf16[4096,1024]{1,0:T(8,128)(2,1)} %get-tuple-element.282, bf16[2048,1024]{1,0:T(8,128)(2,1)S(1)} %copy-done.38), kind=kOutput, calls=%fused_computation.92 | convolution fusion | flops 17188257792 | bytes 29360128 | tf_op jit(solution)/shard_map/tf,df->td/dot_general | solution.py:179
  827.1 26.7 %convolution_convert_fusion.2 = bf16[4096,2048]{1,0:T(8,128)(2,1)} fusion(bf16[1024,2048]{1,0:T(8,128)(2,1)} %all-gather.19.cloned.1.call-done, f32[4096,1024]{1,0:T(8,128)} %fusion.98, f32[1024]{0:T(1024)S(1)} %convert_element_type.184), kind=kOutput, calls=%fused_computation.93 | convolution fusion | flops 17230200832 | bytes 37752832 | tf_op jit(solution)/shard_map/dot_general | solution.py:166
  854.5 88.9 %reduce-scatter.13.cloned.1.call-done = bf16[512,2048]{1,0:T(8,128)(2,1)} async-done(((bf16[4096,2048]{1,0:T(8,128)(2,1)}), bf16[512,2048]{1,0:T(8,128)(2,1)}) %reduce-scatter.13.cloned.1.call-update) | async-done | bytes 2097168 | tf_op jit(solution)/shard_map/reduce_scatter | solution.py:178
  948.7 114.3 %reduce-scatter.11.cloned.1.call-done = bf16[512,2048]{1,0:T(8,128)(2,1)} async-done(((bf16[4096,2048]{1,0:T(8,128)(2,1)}), bf16[512,2048]{1,0:T(8,128)(2,1)}) %reduce-scatter.11.cloned.1.call-update) | async-done | bytes 2097168 | tf_op jit(solution)/shard_map/reduce_scatter | solution.py:165
  1074.3 27.4 %convolution_convert_fusion.5 = bf16[1024,2048]{1,0:T(8,128)(2,1)} fusion(bf16[4096,2048]{1,0:T(8,128)(2,1)} %all-gather.21.cloned.1.call-done, f32[4096,1024]{1,0:T(8,128)} %fusion.98, f32[1024]{0:T(1024)S(1)} %convert_element_type.184), kind=kOutput, calls=%fused_computation.139 | convolution fusion | flops 17223909376 | bytes 37752832 | tf_op jit(solution)/shard_map/tf,td->fd/dot_general | solution.py:173
  1101.9 23.8 %convolution_convert_fusion.6 = bf16[2048,1024]{1,0:T(8,128)(2,1)} fusion(bf16[4096,2048]{1,0:T(8,128)(2,1)} %all-gather.15.cloned.1.call-done, bf16[4096,1024]{1,0:T(8,128)(2,1)} %get-tuple-element.282), kind=kOutput, calls=%fused_computation.140 | convolution fusion | flops 17181966336 | bytes 29360128 | tf_op jit(solution)/shard_map/td,tf->df/dot_general | solution.py:176
  1125.7 38.4 %all-gather.23.cloned.1.call-done = bf16[4096,2048]{1,0:T(8,128)(2,1)} async-done(((bf16[512,2048]{1,0:T(8,128)(2,1)}), bf16[4096,2048]{1,0:T(8,128)(2,1)}) %all-gather.23.cloned.1.call-update) | async-done | bytes 16777232 | tf_op jit(solution)/shard_map/all_gather | solution.py:194
  1174.6 156.0 %while.29 = (s32[]{:T(128)}, bf16[4,1024,2,128]{1,3,2,0:T(8,128)(2,1)}, bf16[4,1024,2,128]{1,3,2,0:T(8,128)(2,1)}, bf16[4,1024,2,128]{1,3,2,0:T(8,128)(2,1)}, bf...) while((s32[]{:T(128)}, ...), condition=%wide.region_17.18_spmd.clone, body=%wide.region_14.17_spmd.clone.sunk | while | flops 2717121536 | bytes 130082144 | solution.py:201
  1361.1 20.0 %convolution_convert_fusion.7 = bf16[2048,768]{1,0:T(8,128)(2,1)} fusion(bf16[4096,2048]{1,0:T(8,128)(2,1)} %all-gather.9.cloned.1.call-done, bf16[4096,768]{0,1:T(8,128)(2,1)} %bitcast.164), kind=kOutput, calls=%fused_computation.141 | convolution fusion | flops 12886474752 | bytes 26214400 | tf_op jit(solution)/shard_map/td,tc->dc/dot_general | solution.py:222
  1381.2 19.0 %convolution_convert_fusion = bf16[4096,2048]{1,0:T(8,128)(2,1)} fusion(bf16[4096,768]{0,1:T(8,128)(2,1)} %bitcast.165, bf16[2048,768]{1,0:T(8,128)(2,1)S(1)} %copy-done.39), kind=kOutput, calls=%fused_computation.91 | convolution fusion | flops 12893290496 | bytes 26214400 | tf_op jit(solution)/shard_map/tc,dc->td/dot_general | solution.py:224
  1425.5 24.7 %reduce-scatter.17.cloned.1.call-done = bf16[512,768]{1,0:T(8,128)(2,1)} async-done(((bf16[2048,768]{1,0:T(8,128)(2,1)}), bf16[512,768]{1,0:T(8,128)(2,1)}) %reduce-scatter.17.cloned.1.call-update) | async-done | bytes 786448 | tf_op jit(solution)/shard_map/reduce_scatter | solution.py:235
  1452.6 117.1 %reduce-scatter.15.cloned.1.call-done = bf16[512,2048]{1,0:T(8,128)(2,1)} async-done(((bf16[4096,2048]{1,0:T(8,128)(2,1)}), bf16[512,2048]{1,0:T(8,128)(2,1)}) %reduce-scatter.15.cloned.1.call-update) | async-done | bytes 2097168 | tf_op jit(solution)/shard_map/reduce_scatter | solution.py:223
  1573.3 40.6 %all-reduce = (f32[2048]{0:T(1024)}, f32[2048]{0:T(1024)}, f32[2048]{0:T(1024)}, f32[2048]{0:T(1024)}, f32[2048]{0:T(1024)}, /*index=5*/f32[2048]{0:T(1024)}) all-reduce(f32[2048]{0:T(1024)S(1)} %get-tuple-element.224, f32[2048]{0:T(1024)S(1)} %get-tuple-element.229, ...), channel_id=1, replica_groups=mesh['dp'=4,'tensor'=8] {'dp','tensor'}, use_global_device_ids=true, to_apply=%region_22.23 | all-reduce | flops 12288 | bytes 98304 | tf_op jit(solution)/shard_map/psum | solution.py:258
  (298 shorter events, 382.3 us)
Async XLA Ops:
  7.2 68.6 %all-gather.11.cloned.1.call-start = ((), (), s32[]{:S(2)}) async-start(), calls=%async_computation.9 | async-start | bytes 3932160 | tf_op jit(solution)/shard_map/all_gather | solution.py:117
  7.9 158.7 %all-gather.9.cloned.1.call-start = ((), (), s32[]{:S(2)}) async-start(), calls=%async_computation.8 | async-start | bytes 18874368 | tf_op jit(solution)/shard_map/all_gather | solution.py:115
  14.8 277.4 %all-gather.13.cloned.1.call-start = ((), (), s32[]{:S(2)}) async-start(), calls=%async_computation.10 | async-start | bytes 1310720 | tf_op jit(solution)/shard_map/all_gather | solution.py:118
  15.6 403.1 %reduce-scatter.9.cloned.1.call-start = ((), (), s32[]{:S(2)}) async-start(), calls=%async_computation.11 | async-start | bytes 18874368 | tf_op jit(solution)/shard_map/reduce_scatter | solution.py:149
  302.4 198.5 %all-gather.17.cloned.1.call-start = ((), (), s32[]{:S(2)}) async-start(), calls=%async_computation.13 | async-start | bytes 5242880 | tf_op jit(solution)/shard_map/all_gather | solution.py:119
  303.0 288.5 %all-gather.15.cloned.1.call-start = ((), (), s32[]{:S(2)}) async-start(), calls=%async_computation.12 | async-start | bytes 18874368 | tf_op jit(solution)/shard_map/all_gather | solution.py:160
  425.5 248.3 %all-gather.19.cloned.1.call-start = ((), (), s32[]{:S(2)}) async-start(), calls=%async_computation.14 | async-start | bytes 5242880 | tf_op jit(solution)/shard_map/all_gather | solution.py:120
  426.2 337.7 %all-gather.21.cloned.1.call-start = ((), (), s32[]{:S(2)}) async-start(), calls=%async_computation.16 | async-start | bytes 18874368 | tf_op jit(solution)/shard_map/all_gather | solution.py:172
  427.0 516.4 %reduce-scatter.13.cloned.1.call-start = ((), (), s32[]{:S(2)}) async-start(), calls=%async_computation.17 | async-start | bytes 18874368 | tf_op jit(solution)/shard_map/reduce_scatter | solution.py:178
  827.1 236.0 %reduce-scatter.11.cloned.1.call-start = ((), (), s32[]{:S(2)}) async-start(), calls=%async_computation.15 | async-start | bytes 18874368 | tf_op jit(solution)/shard_map/reduce_scatter | solution.py:165
  853.9 310.3 %all-gather.23.cloned.1.call-start = ((), (), s32[]{:S(2)}) async-start(), calls=%async_computation.18 | async-start | bytes 18874368 | tf_op jit(solution)/shard_map/all_gather | solution.py:194
  1074.3 326.0 %reduce-scatter.23.cloned.1.call-start = ((), (), s32[]{:S(2)}) async-start(), calls=%async_computation.23 | async-start | bytes 5242880 | tf_op jit(solution)/shard_map/reduce_scatter | solution.py:244
  1101.8 301.3 %reduce-scatter.21.cloned.1.call-start = ((), (), s32[]{:S(2)}) async-start(), calls=%async_computation.22 | async-start | bytes 5242880 | tf_op jit(solution)/shard_map/reduce_scatter | solution.py:241
  1125.7 298.1 %reduce-scatter.19.cloned.1.call-start = ((), (), s32[]{:S(2)}) async-start(), calls=%async_computation.21 | async-start | bytes 1310720 | tf_op jit(solution)/shard_map/reduce_scatter | solution.py:238
  1361.1 89.2 %reduce-scatter.17.cloned.1.call-start = ((), (), s32[]{:S(2)}) async-start(), calls=%async_computation.20 | async-start | bytes 3932160 | tf_op jit(solution)/shard_map/reduce_scatter | solution.py:235
  1381.2 188.6 %reduce-scatter.15.cloned.1.call-start = ((), (), s32[]{:S(2)}) async-start(), calls=%async_computation.19 | async-start | bytes 18874368 | tf_op jit(solution)/shard_map/reduce_scatter | solution.py:223
  1405.9 163.8 %copy-start.4 = (bf16[512,2048]{1,0:T(8,128)(2,1)S(1)}, bf16[512,2048]{1,0:T(8,128)(2,1)}, u32[]{:S(2)}) copy-start(bf16[512,2048]{1,0:T(8,128)(2,1)} %param.21) | copy-start | bytes 6291460
  1405.9 163.8 %copy-start.18 = (f32[2048]{0:T(1024)S(1)}, f32[2048]{0:T(1024)}, u32[]{:S(2)}) copy-start(f32[2048]{0:T(1024)} %copy-done.17) | copy-start | bytes 24580
  1405.9 163.8 %copy-start.22 = (f32[512]{0:T(512)S(1)}, f32[512]{0:T(512)}, u32[]{:S(2)}) copy-start(f32[512]{0:T(512)} %copy-done.21) | copy-start | bytes 6148
  1405.9 163.8 %copy-start.26 = (f32[512]{0:T(512)S(1)}, f32[512]{0:T(512)}, u32[]{:S(2)}) copy-start(f32[512]{0:T(512)} %copy-done.25) | copy-start | bytes 6148
  1410.0 163.2 %copy-start.23 = (f32[2048]{0:T(1024)S(1)}, f32[2048]{0:T(1024)}, u32[]{:S(2)}) copy-start(f32[2048]{0:T(1024)} %get-tuple-element.283) | copy-start | bytes 24580
  1410.0 163.2 %copy-start.24 = (f32[2048]{0:T(1024)S(1)}, f32[2048]{0:T(1024)}, u32[]{:S(2)}) copy-start(f32[2048]{0:T(1024)} %get-tuple-element.292) | copy-start | bytes 24580
  1410.0 163.2 %copy-start.29 = (f32[2048]{0:T(1024)S(1)}, f32[2048]{0:T(1024)}, u32[]{:S(2)}) copy-start(f32[2048]{0:T(1024)} %get-tuple-element.222) | copy-start | bytes 24580
  1410.1 163.2 %copy-start.30 = (f32[2048]{0:T(1024)S(1)}, f32[2048]{0:T(1024)}, u32[]{:S(2)}) copy-start(f32[2048]{0:T(1024)} %get-tuple-element.228) | copy-start | bytes 24580
  (43 other events, 1024.4 us)
Sparse Core Ops, SparseCore 0:
  9.6 66.1 all-gather.10
  78.2 88.3 all-gather.8
  168.2 27.9 all-gather.12
  302.5 116.1 reduce-scatter.8
  420.1 80.7 all-gather.16
  503.2 88.2 all-gather.14
  593.0 80.7 all-gather.18
  675.7 88.2 all-gather.20
  827.2 116.1 reduce-scatter.12
  946.8 116.1 reduce-scatter.10
  1074.4 89.7 all-gather.22
  1166.3 76.7 reduce-scatter.22
  1245.4 77.2 reduce-scatter.20
  1361.2 27.4 reduce-scatter.18
  1390.8 59.3 reduce-scatter.16
  1453.7 116.0 reduce-scatter.14
where the time goes:
time: 1640 us; the launch traced here: 1630 us
  waiting for transfers between devices  966 us (59%)
  matrix products  373 us (23%)
  other arithmetic  140 us (9%)
  local copies, waits for them, and re-layouts  74.4 us (5%)
  blocking collectives  54.2 us (3%)
    reduce_scatter x1, waiting for transfers between devices, on_device(): lax.psum_scatter(jnp.einsum('tc,dc->td', grad_proj, project_full, preferr...  117 us
    reduce_scatter x1, waiting for transfers between devices, on_device(): lax.psum_scatter(jnp.dot(mixed, dense_full, preferred_element_type=jnp.fl...  115 us
    reduce_scatter x1, waiting for transfers between devices, on_device(): lax.psum_scatter(jnp.dot(activated, shrink_full, preferred_element_type=j...  114 us
    all_gather x1, waiting for transfers between devices, on_device(): attn_rows = lax.all_gather(attn_input, 'tensor', axis=0, tiled=True)  90.9 us
    all_gather x1, waiting for transfers between devices, on_device(): mlp_rows = lax.all_gather(mlp_input, 'tensor', axis=0, tiled=True)  90.6 us
    all_gather x1, waiting for transfers between devices, on_device(): grad_rows = lax.all_gather(cotangent, 'tensor', axis=0, tiled=True)  90.1 us
    reduce_scatter x1, waiting for transfers between devices, on_device(): lax.psum_scatter(jnp.einsum('tf,df->td', grad_pre, expand_full, preferred...  88.9 us
    all_gather x1, waiting for transfers between devices, on_device(): lax.all_gather(up_weight, 'dp', axis=0, tiled=True)  73.8 us
  transfers between devices with their start and end apart: 16, of which 12 were waited for; matrix products, arithmetic and copies ran while one was open for 30% of the time, Pallas kernels for 0%

commit v1 on v0

v1 whole, which is shorter than its diff:
```python
import functools
import math

import jax
import jax.numpy as jnp
from jax import lax
from jax.experimental import pallas as pl
from jax.experimental.pallas import tpu as pltpu
from jax.sharding import PartitionSpec as P

VMEM_LIMIT = 62 << 20


def flip(index, bit):
    return index + (1 - 2 * ((index // 2**bit) % 2)) * 2**bit


def chip_bits(n):
    return n.bit_length() - 2


def column_parts(width, count):
    blocks = width // 128
    edges = [128 * (blocks * i // count) for i in range(count + 1)]
    return [(a, b - a) for a, b in zip(edges[:-1], edges[1:])]


def peer(index):
    return {"tensor": index}


def greet(me, bits):
    barrier = pltpu.get_barrier_semaphore()
    for bit in range(bits + 1):
        pl.semaphore_signal(
            barrier, inc=1, device_id=peer(flip(me, bit)), device_id_type=pl.DeviceIdType.MESH
        )
    pl.semaphore_wait(barrier, bits + 1)


def remote(src, dst, send_sem, recv_sem, target):
    return pltpu.make_async_remote_copy(
        src_ref=src,
        dst_ref=dst,
        send_sem=send_sem,
        recv_sem=recv_sem,
        device_id=peer(target),
        device_id_type=pl.DeviceIdType.MESH,
    )


def gather_body(n, own_ref, out_ref, own_sem, chip_send, chip_recv, core_send, core_recv):
    me = lax.axis_index("tensor")
    bits = chip_bits(n)
    rows, width = own_ref.shape
    parts = column_parts(width, bits)
    held = 2**bits
    other_core = flip(me, 0)
    greet(me, bits)

    def slot(part, index):
        at = me
        for step in range(bits):
            if (index >> step) & 1:
                at = flip(at, 1 + (part + step) % bits)
        return at

    def block(part, index):
        start, size = parts[part]
        return out_ref.at[pl.ds(slot(part, index) * rows, rows), pl.ds(start, size)]

    sends = []
    keep = pltpu.make_async_copy(own_ref, out_ref.at[pl.ds(me * rows, rows), :], own_sem)

    def send(part, index, step):
        start, size = parts[part]
        source = own_ref.at[:, pl.ds(start, size)] if index == 0 else block(part, index)
        arrives = index + 2**step
        copy = remote(
            source,
            block(part, index),
            chip_send.at[part, arrives],
            chip_recv.at[part, arrives],
            flip(me, 1 + (part + step) % bits),
        )
        copy.start()
        sends.append(copy)

    for step in range(bits):
        for part in range(bits):
            send(part, 0, step)
    for part in range(bits):
        start, size = parts[part]
        copy = remote(
            own_ref.at[:, pl.ds(start, size)],
            block(part, 0),
            core_send.at[part, 0],
            core_recv.at[part, 0],
            other_core,
        )
        copy.start()
        sends.append(copy)
    keep.start()
    for index in range(1, held):
        for part in range(bits):
            arrived = block(part, index)
            remote(arrived, arrived, chip_send.at[part, index], chip_recv.at[part, index], other_core).wait_recv()
            for step in range(index.bit_length(), bits):
                send(part, index, step)
            copy = remote(arrived, arrived, core_send.at[part, index], core_recv.at[part, index], other_core)
            copy.start()
            sends.append(copy)
    for copy in sends:
        copy.wait_send()
    for part in range(bits):
        for index in range(held):
            arrived = block(part, index)
            remote(arrived, arrived, core_send.at[part, index], core_recv.at[part, index], other_core).wait_recv()
    keep.wait()


def gather_kernel(n, x_ref, out_ref, *sems):
    gather_body(n, x_ref, out_ref, *sems)


def gather_sems(n):
    bits = chip_bits(n)
    dma = pltpu.SemaphoreType.DMA
    return [dma(())] + [dma((bits, 2**bits))] * 4


def gather_rows(x, n, collective_id):
    rows, width = x.shape
    return pl.pallas_call(
        functools.partial(gather_kernel, n),
        out_shape=jax.ShapeDtypeStruct((n * rows, width), x.dtype),
        in_specs=[pl.BlockSpec(memory_space=pltpu.VMEM)],
        out_specs=pl.BlockSpec(memory_space=pl.ANY),
        scratch_shapes=gather_sems(n),
        compiler_params=pltpu.CompilerParams(
            collective_id=collective_id, has_side_effects=True, vmem_limit_bytes=VMEM_LIMIT
        ),
        name="gather_rows",
    )(x)


def scatter_kernel(n, chunk, transposed, a_ref, w_ref, out_ref, csend, crecv, held, recv, *sems):
    me = lax.axis_index("tensor")
    bits = chip_bits(n)
    core_send, core_recv, chip_send, chip_recv = sems
    rows, width = out_ref.shape
    chunks = rows // chunk
    parts = column_parts(width, bits)
    total = 2**bits
    other_core = flip(me, 0)
    greet(me, bits)

    def slot(part, index):
        at = me
        for step in range(bits):
            if (index >> (bits - 1 - step)) & 1:
                at = flip(at, 1 + (part + step) % bits)
        return at

    def product(at, j, part):
        start, size = parts[part]
        lhs = a_ref[pl.ds(pl.multiple_of(at * rows + j * chunk, chunk), chunk), :]
        if transposed:
            return lax.dot_general(
                lhs, w_ref[start : start + size, :], (((1,), (1,)), ((), ())), preferred_element_type=jnp.float32
            )
        return jnp.dot(lhs, w_ref[:, start : start + size], preferred_element_type=jnp.float32)

    def strip(ref, first, count, j, part):
        start, size = parts[part]
        return ref.at[pl.ds(first, count), pl.ds(pl.multiple_of(j * chunk, chunk), chunk), pl.ds(start, size)]

    def core_copy(j, part):
        return remote(
            strip(csend, 0, total, j, part),
            strip(crecv, 0, total, j, part),
            core_send.at[part, j],
            core_recv.at[part, j],
            other_core,
        )

    def chip_copy(j, part, step):
        half = total >> (step + 1)
        first = sum(total >> (s + 1) for s in range(step))
        return remote(
            strip(held, half, half, j, part),
            strip(recv, first, half, j, part),
            chip_send.at[part, step, j],
            chip_recv.at[part, step, j],
            flip(me, 1 + (part + step) % bits),
        )

    def rows_of(j):
        return pl.ds(pl.multiple_of(j * chunk, chunk), chunk)

    def stage_core(j):
        for part in range(bits):
            start, size = parts[part]
            for index in range(total):
                csend[index, rows_of(j), start : start + size] = product(
                    flip(slot(part, index), 0), j, part
                ).astype(csend.dtype)
            core_copy(j, part).start()

    def stage_first(j):
        for part in range(bits):
            start, size = parts[part]
            core_copy(j, part).wait_recv()
            for index in reversed(range(total)):
                value = product(slot(part, index), j, part) + crecv[index, rows_of(j), start : start + size].astype(
                    jnp.float32
                )
                if index:
                    held[index, rows_of(j), start : start + size] = value.astype(held.dtype)
                else:
                    out_ref[rows_of(j), start : start + size] = value
            chip_copy(j, part, 0).start()

    def stage_next(j, step):
        half = total >> (step + 1)
        first = sum(total >> (s + 1) for s in range(step))
        for part in range(bits):
            start, size = parts[part]
            chip_copy(j, part, step).wait_recv()
            for index in reversed(range(half)):
                got = recv[first + index, rows_of(j), start : start + size].astype(jnp.float32)
                if index:
                    value = held[index, rows_of(j), start : start + size].astype(jnp.float32) + got
                    held[index, rows_of(j), start : start + size] = value.astype(held.dtype)
                else:
                    out_ref[rows_of(j), start : start + size] += got
            if step + 1 < bits:
                chip_copy(j, part, step + 1).start()

    def body(u, carry):
        for stage in range(bits + 2):
            j = u - stage

            @pl.when((j >= 0) & (j < chunks))
            def _():
                if stage == 0:
                    stage_core(j)
                elif stage == 1:
                    stage_first(j)
                else:
                    stage_next(j, stage - 2)

        return carry

    lax.fori_loop(0, chunks + bits + 1, body, 0)

    def drain(j, carry):
        for part in range(bits):
            core_copy(j, part).wait_send()
            for step in range(bits):
                chip_copy(j, part, step).wait_send()
        return carry

    lax.fori_loop(0, chunks, drain, 0)


def scatter_rows(a, w, n, collective_id, transposed=False, chunks=4):
    rows = a.shape[0] // n
    width = w.shape[0] if transposed else w.shape[1]
    bits = chip_bits(n)
    total = 2**bits
    chunk = rows // chunks
    dma = pltpu.SemaphoreType.DMA
    return pl.pallas_call(
        functools.partial(scatter_kernel, n, chunk, transposed),
        out_shape=jax.ShapeDtypeStruct((rows, width), jnp.float32),
        in_specs=[pl.BlockSpec(memory_space=pltpu.VMEM)] * 2,
        out_specs=pl.BlockSpec(memory_space=pltpu.VMEM),
        scratch_shapes=[
            pltpu.VMEM((total, rows, width), jnp.bfloat16),
            pltpu.VMEM((total, rows, width), jnp.bfloat16),
            pltpu.VMEM((total, rows, width), jnp.bfloat16),
            pltpu.VMEM((total - 1, rows, width), jnp.bfloat16),
            dma((bits, chunks)),
            dma((bits, chunks)),
            dma((bits, bits, chunks)),
            dma((bits, bits, chunks)),
        ],
        compiler_params=pltpu.CompilerParams(
            collective_id=collective_id, has_side_effects=True, vmem_limit_bytes=VMEM_LIMIT
        ),
        name="scatter_rows",
    )(a, w)


HEAD_DIM = 128
LOG2E = 1.4426950408889634
SCALE = 1.0 / math.sqrt(HEAD_DIM)
BLOCK = 256
NT = (((1,), (1,)), ((), ()))
TN = (((0,), (0,)), ((), ()))


def masked_scores(slope, q, keys, query_labels, key_labels, first):
    raw = lax.dot_general(q, keys, NT, preferred_element_type=jnp.float32)
    rows, width = raw.shape
    column = lax.broadcasted_iota(jnp.int32, (1, width), 1)
    bias = column.astype(jnp.float32) * slope
    same = query_labels == key_labels
    causal = lax.broadcasted_iota(jnp.int32, (rows, width), 1) <= first + lax.broadcasted_iota(
        jnp.int32, (rows, width), 0
    )
    return jnp.where(same & causal, raw * (SCALE * LOG2E) + bias, -1e30)


def attend_kernel(slope_ref, q_ref, k_ref, v_ref, column_ref, row_ref, out_ref):
    slope = slope_ref[pl.program_id(1)]
    length = q_ref.shape[0]
    for first in range(0, length, BLOCK):
        last = first + BLOCK
        scores = masked_scores(
            slope,
            q_ref[first:last, :],
            k_ref[:last, :],
            column_ref[0, first:last, :],
            row_ref[0, :, :last],
            first,
        )
        top = jnp.max(scores, axis=1, keepdims=True)
        expo = jnp.exp2(scores - top)
        total = jnp.sum(expo, axis=1, keepdims=True)
        mixed = jnp.dot(expo.astype(jnp.bfloat16), v_ref[:last, :], preferred_element_type=jnp.float32)
        out_ref[first:last, :] = (mixed / total).astype(out_ref.dtype)


def attend(proj, slopes, labels, length):
    rows, width = proj.shape
    heads = width // (3 * HEAD_DIM)
    sequences = rows // length
    part = lambda which: pl.BlockSpec((length, HEAD_DIM), lambda s, h: (s, h * 3 + which))
    return pl.pallas_call(
        attend_kernel,
        grid=(sequences, heads),
        in_specs=[
            pl.BlockSpec(memory_space=pltpu.SMEM),
            part(0),
            part(1),
            part(2),
            pl.BlockSpec((1, length, 1), lambda s, h: (s, 0, 0)),
            pl.BlockSpec((1, 1, length), lambda s, h: (s, 0, 0)),
        ],
        out_specs=pl.BlockSpec((length, HEAD_DIM), lambda s, h: (s, h)),
        out_shape=jax.ShapeDtypeStruct((rows, heads * HEAD_DIM), jnp.bfloat16),
        name="attend",
    )(slopes, proj, proj, proj, labels[:, :, None], labels[:, None, :])


def attend_back_kernel(slope_ref, q_ref, k_ref, v_ref, g_ref, column_ref, row_ref, out_ref, dk_ref, dv_ref):
    slope = slope_ref[pl.program_id(1)]
    length = q_ref.shape[0]
    for first in reversed(range(0, length, BLOCK)):
        last = first + BLOCK
        q, g = q_ref[first:last, :], g_ref[first:last, :]
        scores = masked_scores(
            slope, q, k_ref[:last, :], column_ref[0, first:last, :], row_ref[0, :, :last], first
        )
        top = jnp.max(scores, axis=1, keepdims=True)
        expo = jnp.exp2(scores - top)
        probs = expo * (1.0 / jnp.sum(expo, axis=1, keepdims=True))
        grad_probs = lax.dot_general(g, v_ref[:last, :], NT, preferred_element_type=jnp.float32)
        product = probs * grad_probs
        grad_scores = (product - probs * jnp.sum(product, axis=1, keepdims=True)).astype(jnp.bfloat16)
        rounded = probs.astype(jnp.bfloat16)
        out_ref[first:last, :HEAD_DIM] = (
            jnp.dot(grad_scores, k_ref[:last, :], preferred_element_type=jnp.float32) * SCALE
        ).astype(out_ref.dtype)
        grad_keys = lax.dot_general(grad_scores, q, TN, preferred_element_type=jnp.float32)
        grad_values = lax.dot_general(rounded, g, TN, preferred_element_type=jnp.float32)
        if last == length:
            dk_ref[...] = grad_keys
            dv_ref[...] = grad_values
        else:
            dk_ref[:last, :] += grad_keys
            dv_ref[:last, :] += grad_values
    out_ref[:, HEAD_DIM : 2 * HEAD_DIM] = (dk_ref[...] * SCALE).astype(out_ref.dtype)
    out_ref[:, 2 * HEAD_DIM :] = dv_ref[...].astype(out_ref.dtype)


def attend_back(proj, grad_mixed, slopes, labels, length):
    rows, width = proj.shape
    heads = width // (3 * HEAD_DIM)
    sequences = rows // length
    part = lambda which: pl.BlockSpec((length, HEAD_DIM), lambda s, h: (s, h * 3 + which))
    return pl.pallas_call(
        attend_back_kernel,
        grid=(sequences, heads),
        in_specs=[
            pl.BlockSpec(memory_space=pltpu.SMEM),
            part(0),
            part(1),
            part(2),
            pl.BlockSpec((length, HEAD_DIM), lambda s, h: (s, h)),
            pl.BlockSpec((1, length, 1), lambda s, h: (s, 0, 0)),
            pl.BlockSpec((1, 1, length), lambda s, h: (s, 0, 0)),
        ],
        out_specs=pl.BlockSpec((length, 3 * HEAD_DIM), lambda s, h: (s, h)),
        out_shape=jax.ShapeDtypeStruct((rows, width), jnp.bfloat16),
        scratch_shapes=[pltpu.VMEM((length, HEAD_DIM), jnp.float32)] * 2,
        name="attend_back",
    )(slopes, proj, proj, proj, grad_mixed, labels[:, :, None], labels[:, None, :])


HEADS = 16


def gelu_tanh(value):
    return (
        0.5
        * value
        * (1.0 + jnp.tanh(0.7978845608028654 * (value + 0.044715 * value * value * value)))
    )


def normalize(rows):
    center = rows - jnp.mean(rows, axis=1, keepdims=True)
    factor = lax.rsqrt(jnp.mean(center * center, axis=1, keepdims=True) + 1e-05)
    return (center * factor, factor)


def norm_back(grad_out, normed, factor, gain):
    scaled = grad_out * gain
    return factor * (
        scaled
        - jnp.mean(scaled, axis=1, keepdims=True)
        - normed * jnp.mean(scaled * normed, axis=1, keepdims=True)
    )


def on_device(
    hidden_input,
    first_gain,
    first_shift,
    qkv_weight,
    query_bias,
    value_bias,
    dense_weight,
    dense_bias,
    second_gain,
    second_shift,
    up_weight,
    up_bias,
    down_weight,
    down_bias,
    segments,
    document_lengths,
    cotangent,
    *,
    n,
):
    heads_local = query_bias.shape[0] // HEAD_DIM
    first_gain32 = first_gain.astype(jnp.float32)
    second_gain32 = second_gain.astype(jnp.float32)
    inputs = hidden_input.astype(jnp.float32)
    normed_first, factor_first = normalize(inputs)
    attn_input = (normed_first * first_gain32 + first_shift.astype(jnp.float32)).astype(
        jnp.bfloat16
    )
    attn_rows = gather_rows(attn_input, n, 1)
    project_full, dense_full, expand_full, shrink_full = (
        lax.all_gather(qkv_weight, "dp", axis=0, tiled=True),
        lax.all_gather(dense_weight, "dp", axis=1, tiled=True),
        lax.all_gather(up_weight, "dp", axis=0, tiled=True),
        lax.all_gather(down_weight, "dp", axis=1, tiled=True),
    )
    group_rows = attn_rows.shape[0]
    sequences = document_lengths.shape[0]
    length = group_rows // sequences
    heads_index = lax.axis_index("tensor") * heads_local + lax.broadcasted_iota(
        jnp.int32, (heads_local,), 0
    )
    slopes = jnp.exp2(-8.0 * (heads_index.astype(jnp.float32) + 1.0) / HEADS) * LOG2E
    position = lax.broadcasted_iota(jnp.int32, (sequences, length), 1)
    filled = jnp.sum(document_lengths, axis=1, keepdims=True)
    labels = jnp.where(position < filled, segments.reshape(sequences, length), length + position)
    query_bias32 = query_bias.astype(jnp.float32).reshape(heads_local, HEAD_DIM)
    value_bias32 = value_bias.astype(jnp.float32).reshape(heads_local, HEAD_DIM)
    proj_bias = jnp.stack((query_bias32, jnp.zeros_like(query_bias32), value_bias32), axis=1).reshape(
        heads_local * 3 * HEAD_DIM
    )
    proj = (jnp.dot(attn_rows, project_full, preferred_element_type=jnp.float32) + proj_bias).astype(
        jnp.bfloat16
    )
    mixed = attend(proj, slopes, labels, length)
    attn_out = scatter_rows(mixed, dense_full, n, 2)
    residual = inputs + attn_out + dense_bias.astype(jnp.float32)
    normed_second, factor_second = normalize(residual)
    mlp_input = (normed_second * second_gain32 + second_shift.astype(jnp.float32)).astype(
        jnp.bfloat16
    )
    mlp_rows = gather_rows(mlp_input, n, 1)
    pre_act = jnp.dot(mlp_rows, expand_full, preferred_element_type=jnp.float32) + up_bias.astype(
        jnp.float32
    )
    activated = gelu_tanh(pre_act).astype(jnp.bfloat16)
    mlp_out = scatter_rows(activated, shrink_full, n, 3)
    hidden_output = (residual + mlp_out + down_bias.astype(jnp.float32)).astype(jnp.bfloat16)
    grad_rows = gather_rows(cotangent, n, 1)
    grad_down = jnp.einsum("tf,td->fd", activated, grad_rows, preferred_element_type=jnp.float32)
    grad_act = jnp.einsum("td,fd->tf", grad_rows, shrink_full, preferred_element_type=jnp.float32)
    grad_pre = jax.vjp(gelu_tanh, pre_act)[1](grad_act)[0].astype(jnp.bfloat16)
    grad_up = jnp.einsum("td,tf->df", mlp_rows, grad_pre, preferred_element_type=jnp.float32)
    sum_up_bias = jnp.sum(grad_pre.astype(jnp.float32), axis=0)
    grad_mlp_in = scatter_rows(grad_pre, expand_full, n, 4, transposed=True, chunks=2)
    cotangent32 = cotangent.astype(jnp.float32)
    grad_residual = cotangent32 + norm_back(
        grad_mlp_in, normed_second, factor_second, second_gain32
    )
    sum_second_gain = jnp.sum(grad_mlp_in * normed_second, axis=0)
    sum_second_shift = jnp.sum(grad_mlp_in, axis=0)
    sum_down_bias = jnp.sum(cotangent32, axis=0)
    sum_dense_bias = jnp.sum(grad_residual, axis=0)
    grad_attn_rows = gather_rows(grad_residual.astype(jnp.bfloat16), n, 1)
    grad_dense = jnp.einsum("tc,td->cd", mixed, grad_attn_rows, preferred_element_type=jnp.float32)
    grad_mixed = jnp.einsum(
        "td,cd->tc", grad_attn_rows, dense_full, preferred_element_type=jnp.float32
    ).astype(jnp.bfloat16)
    grad_proj = attend_back(proj, grad_mixed, slopes, labels, length)
    proj_sums = jnp.sum(grad_proj.astype(jnp.float32), axis=0).reshape(heads_local, 3, HEAD_DIM)
    sum_query_bias = proj_sums[:, 0].reshape(heads_local * HEAD_DIM)
    sum_value_bias = proj_sums[:, 2].reshape(heads_local * HEAD_DIM)
    grad_project = jnp.einsum("td,tc->dc", attn_rows, grad_proj, preferred_element_type=jnp.float32)
    grad_attn_in = scatter_rows(grad_proj, project_full, n, 5, transposed=True, chunks=2)
    grad_input = grad_residual + norm_back(grad_attn_in, normed_first, factor_first, first_gain32)
    sum_first_gain = jnp.sum(grad_attn_in * normed_first, axis=0)
    sum_first_shift = jnp.sum(grad_attn_in, axis=0)
    grad_qkv_weight, grad_dense_weight, grad_up_weight, grad_down_weight = (
        lax.psum_scatter(
            grad_project.astype(jnp.bfloat16), "dp", scatter_dimension=0, tiled=True
        ).astype(jnp.float32),
        lax.psum_scatter(
            grad_dense.astype(jnp.bfloat16), "dp", scatter_dimension=1, tiled=True
        ).astype(jnp.float32),
        lax.psum_scatter(
            grad_up.astype(jnp.bfloat16), "dp", scatter_dimension=0, tiled=True
        ).astype(jnp.float32),
        lax.psum_scatter(
            grad_down.astype(jnp.bfloat16), "dp", scatter_dimension=1, tiled=True
        ).astype(jnp.float32),
    )
    grad_query_bias, grad_value_bias, grad_up_bias = lax.psum(
        (sum_query_bias, sum_value_bias, sum_up_bias), "dp"
    )
    (
        grad_first_gain,
        grad_first_shift,
        grad_second_gain,
        grad_second_shift,
        grad_dense_bias,
        grad_down_bias,
    ) = lax.psum(
        (
            sum_first_gain,
            sum_first_shift,
            sum_second_gain,
            sum_second_shift,
            sum_dense_bias,
            sum_down_bias,
        ),
        ("dp", "tensor"),
    )
    return (
        hidden_output,
        grad_input,
        grad_first_gain,
        grad_first_shift,
        grad_qkv_weight,
        grad_query_bias,
        grad_value_bias,
        grad_dense_weight,
        grad_dense_bias,
        grad_second_gain,
        grad_second_shift,
        grad_up_weight,
        grad_up_bias,
        grad_down_weight,
        grad_down_bias,
    )


def solution(mesh):
    return jax.shard_map(
        functools.partial(on_device, n=mesh.shape["tensor"]),
        mesh=mesh,
        in_specs=(
            P(("dp", "tensor"), None),
            P(),
            P(),
            P("dp", "tensor"),
            P("tensor"),
            P("tensor"),
            P("tensor", "dp"),
            P(),
            P(),
            P(),
            P("dp", "tensor"),
            P("tensor"),
            P("tensor", "dp"),
            P(),
            P("dp"),
            P("dp", None),
            P(("dp", "tensor"), None),
        ),
        out_specs=(
            P(("dp", "tensor"), None),
            P(("dp", "tensor"), None),
            P(),
            P(),
            P("dp", "tensor"),
            P("tensor"),
            P("tensor"),
            P("tensor", "dp"),
            P(),
            P(),
            P(),
            P("dp", "tensor"),
            P("tensor"),
            P("tensor", "dp"),
            P(),
        ),
        check_vma=False,
    )
```

time: 1640 us -> 1020 us (0.62)
  waiting for transfers between devices: 966 us -> 13.3 us
  Pallas kernels: 0 us -> 700 us
  matrix products: 373 us -> 173 us
  other arithmetic: 140 us -> 49.5 us
  local copies, waits for them, and re-layouts: 74.4 us -> 6.17 us
    pallas_call x0 -> x10, Pallas kernels: none -> 700 us  [the longest x4 344 us: scatter_rows(): pl.pallas_call(functools.partial(scatter_kernel, n, chunk, transposed), o...]
    reduce_scatter x4 -> x0, waiting for transfers between devices: 435 us -> none  [the longest x1 117 us: on_device(): lax.psum_scatter(jnp.einsum('tc,dc->td', grad_proj, project_full, preferr...]
    all_gather x4 -> x0, waiting for transfers between devices: 310 us -> none  [the longest x1 90.9 us: on_device(): attn_rows = lax.all_gather(attn_input, 'tensor', axis=0, tiled=True)]
    dot_general x32 -> x0, matrix products: 201 us -> none  [the longest x8 48.5 us: head_scores(): jnp.einsum('qhd,khd->hqk', queries, keys, preferred_element_type=jnp.floa...]
    all_gather x1, waiting for transfers between devices: 73.8 us -> 0.02 us  [on_device(): lax.all_gather(up_weight, 'dp', axis=0, tiled=True)]
    all_gather x1, waiting for transfers between devices: 60 us -> 0.01 us  [on_device(): lax.all_gather(qkv_weight, 'dp', axis=0, tiled=True)]
    all_gather x1, waiting for transfers between devices: 58.9 us -> 0.01 us  [on_device(): lax.all_gather(down_weight, 'dp', axis=1, tiled=True)]
    convert_element_type x15 -> x1, other arithmetic: 45.4 us -> 1.6 us  [on_device(): grad_attn_rows = gather_rows(grad_residual.astype(jnp.bfloat16), n, 1)]
  transfers between devices with their start and end apart: 16 -> 8, of which waited for: 12 -> 1; matrix products, arithmetic and copies ran while one was open for 30% -> 15% of each run, Pallas kernels for 0% -> 44%
where the time goes in v1:
time: 1020 us; the launch traced here: 1010 us
  Pallas kernels  700 us (69%)
  matrix products  173 us (17%)
  blocking collectives  54.4 us (5%)
  other arithmetic  49.5 us (5%)
  between operations  14.8 us (1%)
  waiting for transfers between devices  13.3 us (1%)
    pallas_call x4, Pallas kernels, scatter_rows(): pl.pallas_call(functools.partial(scatter_kernel, n, chunk, transposed), o...  344 us
    pallas_call x4, Pallas kernels, gather_rows(): pl.pallas_call(functools.partial(gather_kernel, n), out_shape=jax.ShapeDt...  307 us
    psum x1, blocking collectives, on_device(): lax.psum((sum_first_gain, sum_first_shift, sum_second_gain, sum_second_sh...  41.4 us
    dot_general x1, matrix products, on_device(): jnp.einsum('td,fd->tf', grad_rows, shrink_full, preferred_element_type=jn...  40.3 us
    pallas_call x1, Pallas kernels, attend_back(): pl.pallas_call(attend_back_kernel, grid=(sequences, heads), in_specs=[pl....  31 us
    dot_general x1, matrix products, on_device(): jnp.einsum('tf,td->fd', activated, grad_rows, preferred_element_type=jnp....  24 us
    dot_general x1, matrix products, on_device(): jnp.einsum('td,tf->df', mlp_rows, grad_pre, preferred_element_type=jnp.fl...  23.8 us
    dot_general x1, matrix products, on_device(): jnp.dot(mlp_rows, expand_full, preferred_element_type=jnp.float32)  23.4 us
  transfers between devices with their start and end apart: 8, of which 1 were waited for; matrix products, arithmetic and copies ran while one was open for 15% of the time, Pallas kernels for 44%

profile of v1, /device:TPU:0, one launch (start us, length us, event | category | flops | bytes accessed | tf_op | source)
XLA Modules:
  0.0 1011.9 jit_solution(4942233582719790903)
XLA Ops:
  14.0 78.5 %gather_rows.4 = bf16[4096,2048]{1,0:T(8,128)(2,1)} custom-call(bf16[512,2048]{1,0:T(8,128)(2,1)} %fusion.13.x_ref), custom_call_target="tpu_custom_call" | custom-call | tf_op jit(solution)/shard_map/gather_rows/pallas_call | solution.py:134
  97.6 76.5 %gather_rows.6 = bf16[4096,2048]{1,0:T(8,128)(2,1)} custom-call(bf16[512,2048]{1,0:T(8,128)(2,1)} %x_ref.1), custom_call_target="tpu_custom_call" | custom-call | tf_op jit(solution)/shard_map/gather_rows/pallas_call | solution.py:134
  174.8 19.7 %add_convert_fusion.q_ref.k_ref.v_ref = bf16[4096,768]{1,0:T(8,128)(2,1)} fusion(bf16[4096,2048]{1,0:T(8,128)(2,1)} %gather_rows.4, bf16[2048,768]{1,0:T(8,128)(2,1)} %all-gather.5.cloned.1.call-done.w_ref, f32[768]{0:T(1024)S(1)} %add.137), kind=kOutput, calls=%fused_computation.13 | convolution fusion | flops 12891193344 | bytes 26217472 | tf_op jit(solution)/shard_map/dot_general | solution.py:490
  194.4 18.1 %attend.1.a_ref = bf16[4096,256]{1,0:T(8,128)(2,1)} custom-call(f32[2]{0:T(128)} %exponential_multiply_fusion.slope_ref, bf16[4096,768]{1,0:T(8,128)(2,1)} %add_convert_fusion.q_ref.k_ref.v_ref, bf16[4096,768]{1,0:T(8,128)(2,1)} %add_convert_fusion.q_ref.k_ref.v_ref, bf16[4096,768]{1,0:T(8,128)(2,1)} %add_convert_fusion.q_ref.k_ref.v_ref, ...), custom_call_target="tpu_custom_call" | custom-call | tf_op jit(solution)/shard_map/attend/pallas_call | solution.py:341
  212.5 79.8 %scatter_rows.4 = f32[512,2048]{1,0:T(8,128)} custom-call(bf16[4096,256]{1,0:T(8,128)(2,1)} %attend.1.a_ref, bf16[256,2048]{1,0:T(8,128)(2,1)} %all-gather.7.cloned.1.call-done.w_ref), custom_call_target="tpu_custom_call" | custom-call | tf_op jit(solution)/shard_map/scatter_rows/pallas_call | solution.py:274
  300.0 76.0 %gather_rows.5 = bf16[4096,2048]{1,0:T(8,128)(2,1)} custom-call(bf16[512,2048]{1,0:T(8,128)(2,1)} %add_convert_fusion.2.x_ref), custom_call_target="tpu_custom_call" | custom-call | tf_op jit(solution)/shard_map/gather_rows/pallas_call | solution.py:134
  376.1 23.4 %fusion.27 = f32[4096,1024]{1,0:T(8,128)} fusion(bf16[4096,2048]{1,0:T(8,128)(2,1)} %gather_rows.5, bf16[2048,1024]{1,0:T(8,128)(2,1)} %all-gather.9.cloned.1.call-done.w_ref), kind=kOutput, calls=%fused_computation.64 | convolution fusion | flops 17179869184 | bytes 37748736 | tf_op jit(solution)/shard_map/dot_general | solution.py:501
  399.5 40.3 %convert_reduce_fusion = (f32[1024]{0:T(1024)S(1)}, bf16[4096,1024]{1,0:T(8,128)(2,1)}, bf16[4096,1024]{1,0:T(8,128)(2,1)}) fusion(f32[4096,1024]{1,0:T(8,128)} %fusion.27, f32[1024]{0:T(1024)S(1)} %convert_element_type.96, bf16[4096,2048]{1,0:T(8,128)(2,1)} %gather_rows.6, bf16[1024,2048]{1,0:T(8,128)(2,1)} %all-gather.11.cloned.1.call-done.w_ref), kind=kOutput, calls=%fused_computation.10 | convolution fusion | flops 17301504000 | bytes 54534144 | tf_op jit(solution)/shard_map/td,fd->tf/dot_general | solution.py:509
  439.8 92.0 %scatter_rows.6 = f32[512,2048]{1,0:T(8,128)} custom-call(bf16[4096,1024]{1,0:T(8,128)(2,1)} %get-tuple-element.33.a_ref, bf16[2048,1024]{1,0:T(8,128)(2,1)} %all-gather.9.cloned.1.call-done.w_ref), custom_call_target="tpu_custom_call" | custom-call | tf_op jit(solution)/shard_map/scatter_rows/pallas_call | solution.py:274
  531.8 4.4 multiply_reduce_fusion
  536.2 84.6 %scatter_rows.5 = f32[512,2048]{1,0:T(8,128)} custom-call(bf16[4096,1024]{1,0:T(8,128)(2,1)} %get-tuple-element.38.a_ref, bf16[1024,2048]{1,0:T(8,128)(2,1)} %all-gather.11.cloned.1.call-done.w_ref), custom_call_target="tpu_custom_call" | custom-call | tf_op jit(solution)/shard_map/scatter_rows/pallas_call | solution.py:274
  620.8 7.7 fusion.23
  632.1 76.0 %gather_rows.7 = bf16[4096,2048]{1,0:T(8,128)(2,1)} custom-call(bf16[512,2048]{1,0:T(8,128)(2,1)} %convert_element_type.102.x_ref), custom_call_target="tpu_custom_call" | custom-call | tf_op jit(solution)/shard_map/gather_rows/pallas_call | solution.py:134
  708.1 12.0 %convolution_convert_fusion.4 = bf16[256,2048]{1,0:T(8,128)(2,1)} fusion(bf16[4096,256]{1,0:T(8,128)(2,1)} %attend.1.a_ref, bf16[4096,2048]{1,0:T(8,128)(2,1)} %gather_rows.7), kind=kOutput, calls=%fused_computation.46 | convolution fusion | flops 4295491584 | bytes 19922944 | tf_op jit(solution)/shard_map/tc,td->cd/dot_general | solution.py:523
  720.2 10.1 convolution_convert_fusion.g_ref
  730.3 31.0 %attend_back.1.a_ref = bf16[4096,768]{1,0:T(8,128)(2,1)} custom-call(f32[2]{0:T(128)} %exponential_multiply_fusion.slope_ref, bf16[4096,768]{1,0:T(8,128)(2,1)} %add_convert_fusion.q_ref.k_ref.v_ref, bf16[4096,768]{1,0:T(8,128)(2,1)} %add_convert_fusion.q_ref.k_ref.v_ref, bf16[4096,768]{1,0:T(8,128)(2,1)} %add_convert_fusion.q_ref.k_ref.v_ref, ...), custom_call_target="tpu_custom_call" | custom-call | tf_op jit(solution)/shard_map/attend_back/pallas_call | solution.py:394
  761.3 20.2 %convolution_convert_fusion.3 = bf16[2048,768]{1,0:T(8,128)(2,1)} fusion(bf16[4096,2048]{1,0:T(8,128)(2,1)} %gather_rows.4, bf16[4096,768]{1,0:T(8,128)(2,1)} %attend_back.1.a_ref), kind=kOutput, calls=%fused_computation.45 | convolution fusion | flops 12886474752 | bytes 26214400 | tf_op jit(solution)/shard_map/td,tc->dc/dot_general | solution.py:531
  781.5 23.8 %convolution_convert_fusion.2 = bf16[2048,1024]{1,0:T(8,128)(2,1)} fusion(bf16[4096,2048]{1,0:T(8,128)(2,1)} %gather_rows.5, bf16[4096,1024]{1,0:T(8,128)(2,1)} %get-tuple-element.33.a_ref), kind=kOutput, calls=%fused_computation.42 | convolution fusion | flops 17181966336 | bytes 29360128 | tf_op jit(solution)/shard_map/td,tf->df/dot_general | solution.py:511
  805.3 24.0 %convolution_convert_fusion.1 = bf16[1024,2048]{1,0:T(8,128)(2,1)} fusion(bf16[4096,1024]{1,0:T(8,128)(2,1)} %get-tuple-element.38.a_ref, bf16[4096,2048]{1,0:T(8,128)(2,1)} %gather_rows.6), kind=kOutput, calls=%fused_computation.41 | convolution fusion | flops 17181966336 | bytes 29360128 | tf_op jit(solution)/shard_map/tf,td->fd/dot_general | solution.py:508
  833.1 87.5 %scatter_rows.7 = f32[512,2048]{1,0:T(8,128)} custom-call(bf16[4096,768]{1,0:T(8,128)(2,1)} %attend_back.1.a_ref, bf16[2048,768]{1,0:T(8,128)(2,1)} %all-gather.5.cloned.1.call-done.w_ref), custom_call_target="tpu_custom_call" | custom-call | tf_op jit(solution)/shard_map/scatter_rows/pallas_call | solution.py:274
  920.6 13.0 %all-reduce.1 = (f32[256]{0:T(256)}, f32[256]{0:T(256)}, f32[1024]{0:T(1024)}) all-reduce(f32[256]{0:T(256)S(1)} %bitcast.24, f32[256]{0:T(256)S(1)} %bitcast.23, f32[1024]{0:T(1024)S(1)} %get-tuple-element.32), channel_id=1, replica_groups=mesh['dp'=4,'tensor'=8] {'dp'}, use_global_device_ids=true, to_apply=%region_15.16 | all-reduce | flops 1536 | bytes 12288 | tf_op jit(solution)/shard_map/psum | solution.py:550
  937.4 41.4 %all-reduce = (f32[2048]{0:T(1024)}, f32[2048]{0:T(1024)}, f32[2048]{0:T(1024)}, f32[2048]{0:T(1024)}, f32[2048]{0:T(1024)}, /*index=5*/f32[2048]{0:T(1024)}) all-reduce(f32[2048]{0:T(1024)S(1)} %get-tuple-element.17, f32[2048]{0:T(1024)S(1)} %get-tuple-element.22, ...), channel_id=1, replica_groups=mesh['dp'=4,'tensor'=8] {'dp','tensor'}, use_global_device_ids=true, to_apply=%region_10.11 | all-reduce | flops 12288 | bytes 98304 | tf_op jit(solution)/shard_map/psum | solution.py:560
  978.9 5.6 fusion.17
  991.4 10.6 %reduce-scatter.11.cloned.1.call-done = bf16[1024,512]{1,0:T(8,128)(2,1)} async-done(((bf16[1024,2048]{1,0:T(8,128)(2,1)}), bf16[1024,512]{1,0:T(8,128)(2,1)}) %reduce-scatter.11.cloned.1.call-update) | async-done | bytes 1048592 | tf_op jit(solution)/shard_map/reduce_scatter | solution.py:546
  (109 shorter events, 41.1 us)
Async XLA Ops:
  7.2 4.0 copy-start.14
  7.2 167.6 %all-gather.5.cloned.1.call-start = ((), (), s32[]{:S(2)}) async-start(), calls=%async_computation.4 | async-start | bytes 3932160 | tf_op jit(solution)/shard_map/all_gather | solution.py:470
  7.9 204.6 %all-gather.7.cloned.1.call-start = ((), (), s32[]{:S(2)}) async-start(), calls=%async_computation.5 | async-start | bytes 1310720 | tf_op jit(solution)/shard_map/all_gather | solution.py:471
  8.7 367.4 %all-gather.9.cloned.1.call-start = ((), (), s32[]{:S(2)}) async-start(), calls=%async_computation.6 | async-start | bytes 5242880 | tf_op jit(solution)/shard_map/all_gather | solution.py:472
  9.4 390.1 %all-gather.11.cloned.1.call-start = ((), (), s32[]{:S(2)}) async-start(), calls=%async_computation.7 | async-start | bytes 5242880 | tf_op jit(solution)/shard_map/all_gather | solution.py:473
  10.0 974.4 %reduce-scatter.7.cloned.1.call-start = ((), (), s32[]{:S(2)}) async-start(), calls=%async_computation.9 | async-start | bytes 1310720 | tf_op jit(solution)/shard_map/reduce_scatter | solution.py:540
  13.9 78.5 %copy-start.21 = (bf16[256]{0:T(256)(128)(2,1)S(1)}, bf16[256]{0:T(256)(128)(2,1)}, u32[]{:S(2)}) copy-start(bf16[256]{0:T(256)(128)(2,1)} %param.21) | copy-start | bytes 1540
  13.9 78.6 %copy-start.22 = (bf16[256]{0:T(256)(128)(2,1)S(1)}, bf16[256]{0:T(256)(128)(2,1)}, u32[]{:S(2)}) copy-start(bf16[256]{0:T(256)(128)(2,1)} %param.22) | copy-start | bytes 1540
  13.9 78.7 %copy-start.7 = (s32[4096]{0:T(1024)S(1)}, s32[4096]{0:T(1024)}, u32[]{:S(2)}) copy-start(s32[4096]{0:T(1024)} %param.31) | copy-start | bytes 49156
  13.9 80.7 %copy-start.20 = (s32[4,18]{1,0:T(4,128)S(1)}, s32[4,18]{1,0:T(4,128)}, u32[]{:S(2)}) copy-start(s32[4,18]{1,0:T(4,128)} %param.32) | copy-start | bytes 868
  92.5 5.1 copy-start.15
  92.5 5.1 copy-start.16
  92.5 5.1 copy-start.17
  97.6 76.5 %copy-start.19 = (bf16[1024]{0:T(1024)(128)(2,1)S(1)}, bf16[1024]{0:T(1024)(128)(2,1)}, u32[]{:S(2)}) copy-start(bf16[1024]{0:T(1024)(128)(2,1)} %param.28) | copy-start | bytes 6148
  97.6 76.6 %copy-start.18 = (bf16[2048]{0:T(1024)(128)(2,1)S(1)}, bf16[2048]{0:T(1024)(128)(2,1)}, u32[]{:S(2)}) copy-start(bf16[2048]{0:T(1024)(128)(2,1)} %param.30) | copy-start | bytes 12292
  536.2 84.6 %copy-start.12 = (f32[2048]{0:T(1024)S(1)}, f32[2048]{0:T(1024)}, u32[]{:S(2)}) copy-start(f32[2048]{0:T(1024)} %convert_element_type.98) | copy-start | bytes 24580
  708.1 12.0 %copy-start.4 = (bf16[256,2048]{1,0:T(8,128)(2,1)S(1)}, bf16[256,2048]{1,0:T(8,128)(2,1)}, u32[]{:S(2)}) copy-start(bf16[256,2048]{1,0:T(8,128)(2,1)} %all-gather.7.cloned.1.call-done.w_ref) | copy-start | bytes 3145732
  720.1 266.1 %reduce-scatter.5.cloned.1.call-start = ((), (), s32[]{:S(2)}) async-start(), calls=%async_computation.8 | async-start | bytes 3932160 | tf_op jit(solution)/shard_map/reduce_scatter | solution.py:537
  781.4 207.2 %reduce-scatter.9.cloned.1.call-start = ((), (), s32[]{:S(2)}) async-start(), calls=%async_computation.10 | async-start | bytes 5242880 | tf_op jit(solution)/shard_map/reduce_scatter | solution.py:543
  805.3 196.7 %reduce-scatter.11.cloned.1.call-start = ((), (), s32[]{:S(2)}) async-start(), calls=%async_computation.11 | async-start | bytes 5242880 | tf_op jit(solution)/shard_map/reduce_scatter | solution.py:546
  833.1 100.5 %copy-start.6 = (f32[2048]{0:T(1024)S(1)}, f32[2048]{0:T(1024)}, u32[]{:S(2)}) copy-start(f32[2048]{0:T(1024)} %copy-done.5) | copy-start | bytes 24580
  833.1 100.5 %copy-start.9 = (f32[512]{0:T(512)S(1)}, f32[512]{0:T(512)}, u32[]{:S(2)}) copy-start(f32[512]{0:T(512)} %copy-done.8) | copy-start | bytes 6148
  833.1 100.5 %copy-start.11 = (f32[512]{0:T(512)S(1)}, f32[512]{0:T(512)}, u32[]{:S(2)}) copy-start(f32[512]{0:T(512)} %copy-done.10) | copy-start | bytes 6148
  920.6 58.2 %copy-start.2 = (bf16[512,2048]{1,0:T(8,128)(2,1)S(1)}, bf16[512,2048]{1,0:T(8,128)(2,1)}, u32[]{:S(2)}) copy-start(bf16[512,2048]{1,0:T(8,128)(2,1)} %param.17) | copy-start | bytes 6291460
  (7 other events, 12.8 us)
Sparse Core Ops, SparseCore 0:
  9.6 66.1 all-gather.4
  77.4 26.6 all-gather.6
  105.6 80.1 all-gather.8
  187.2 79.2 all-gather.10
  720.2 27.4 reduce-scatter.6
  781.6 60.5 reduce-scatter.4
  844.5 76.7 reduce-scatter.8
  923.5 78.4 reduce-scatter.10

commit v2 on v1

--- a/solution.py
+++ b/solution.py
@@ -49,78 +49,114 @@
     )
 
 
-def gather_body(n, own_ref, out_ref, own_sem, chip_send, chip_recv, core_send, core_recv):
-    me = lax.axis_index("tensor")
-    bits = chip_bits(n)
-    rows, width = own_ref.shape
-    parts = column_parts(width, bits)
-    held = 2**bits
-    other_core = flip(me, 0)
-    greet(me, bits)
-
-    def slot(part, index):
-        at = me
-        for step in range(bits):
+class Gather:
+    def __init__(self, n, own_ref, out_ref, sems):
+        self.me = lax.axis_index("tensor")
+        self.bits = chip_bits(n)
+        self.rows, width = own_ref.shape
+        self.parts = column_parts(width, self.bits)
+        self.own, self.out = own_ref, out_ref
+        self.own_sem, self.chip_send, self.chip_recv, self.core_send, self.core_recv = sems
+        self.sends = []
+
+    def slot(self, part, index):
+        at = self.me
+        for step in range(self.bits):
             if (index >> step) & 1:
-                at = flip(at, 1 + (part + step) % bits)
+                at = flip(at, 1 + (part + step) % self.bits)
         return at
 
-    def block(part, index):
-        start, size = parts[part]
-        return out_ref.at[pl.ds(slot(part, index) * rows, rows), pl.ds(start, size)]
-
-    sends = []
-    keep = pltpu.make_async_copy(own_ref, out_ref.at[pl.ds(me * rows, rows), :], own_sem)
-
-    def send(part, index, step):
-        start, size = parts[part]
-        source = own_ref.at[:, pl.ds(start, size)] if index == 0 else block(part, index)
+    def place(self, mask, core):
+        at = flip(self.me, 0) if core else self.me
+        for bit in range(self.bits):
+            if (mask >> bit) & 1:
+                at = flip(at, 1 + bit)
+        return at
+
+    def index_of(self, part, mask):
+        return sum(2 ** ((bit - part) % self.bits) for bit in range(self.bits) if (mask >> bit) & 1)
+
+    def level(self, count):
+        return [index for index in range(2**self.bits) if index.bit_count() == count]
+
+    def block(self, part, index, core=0):
+        start, size = self.parts[part]
+        at = flip(self.slot(part, index), 0) if core else self.slot(part, index)
+        return self.out.at[pl.ds(pl.multiple_of(at * self.rows, self.rows), self.rows), pl.ds(start, size)]
+
+    def source(self, part, index):
+        start, size = self.parts[part]
+        return self.own.at[:, pl.ds(start, size)] if index == 0 else self.block(part, index)
+
+    def send(self, part, index, step):
         arrives = index + 2**step
         copy = remote(
-            source,
-            block(part, index),
-            chip_send.at[part, arrives],
-            chip_recv.at[part, arrives],
-            flip(me, 1 + (part + step) % bits),
+            self.source(part, index),
+            self.block(part, index),
+            self.chip_send.at[part, arrives],
+            self.chip_recv.at[part, arrives],
+            flip(self.me, 1 + (part + step) % self.bits),
         )
         copy.start()
-        sends.append(copy)
-
-    for step in range(bits):
-        for part in range(bits):
-            send(part, 0, step)
-    for part in range(bits):
-        start, size = parts[part]
+        self.sends.append(copy)
+
+    def hand_over(self, part, index):
         copy = remote(
-            own_ref.at[:, pl.ds(start, size)],
-            block(part, 0),
-            core_send.at[part, 0],
-            core_recv.at[part, 0],
-            other_core,
+            self.source(part, index),
+            self.block(part, index),
+            self.core_send.at[part, index],
+            self.core_recv.at[part, index],
+            flip(self.me, 0),
         )
         copy.start()
-        sends.append(copy)
-    keep.start()
-    for index in range(1, held):
-        for part in range(bits):
-            arrived = block(part, index)
-            remote(arrived, arrived, chip_send.at[part, index], chip_recv.at[part, index], other_core).wait_recv()
-            for step in range(index.bit_length(), bits):
-                send(part, index, step)
-            copy = remote(arrived, arrived, core_send.at[part, index], core_recv.at[part, index], other_core)
-            copy.start()
-            sends.append(copy)
-    for copy in sends:
-        copy.wait_send()
-    for part in range(bits):
-        for index in range(held):
-            arrived = block(part, index)
-            remote(arrived, arrived, core_send.at[part, index], core_recv.at[part, index], other_core).wait_recv()
-    keep.wait()
+        self.sends.append(copy)
+
+    def keep(self):
+        rows = pl.ds(pl.multiple_of(self.me * self.rows, self.rows), self.rows)
+        return pltpu.make_async_copy(self.own, self.out.at[rows, :], self.own_sem)
+
+    def start(self):
+        greet(self.me, self.bits)
+        for step in range(self.bits):
+            for part in range(self.bits):
+                self.send(part, 0, step)
+        for part in range(self.bits):
+            self.hand_over(part, 0)
+        self.keep().start()
+
+    def forward(self, count):
+        for index in self.level(count):
+            for part in range(self.bits):
+                arrived = self.block(part, index)
+                remote(
+                    arrived, arrived, self.chip_send.at[part, index], self.chip_recv.at[part, index], flip(self.me, 0)
+                ).wait_recv()
+                for step in range(index.bit_length(), self.bits):
+                    self.send(part, index, step)
+                self.hand_over(part, index)
+
+    def wait_core(self, mask):
+        for part in range(self.bits):
+            index = self.index_of(part, mask)
+            arrived = self.block(part, index, 1)
+            remote(
+                arrived, arrived, self.core_send.at[part, index], self.core_recv.at[part, index], flip(self.me, 0)
+            ).wait_recv()
+
+    def finish_sends(self):
+        for copy in self.sends:
+            copy.wait_send()
 
 
 def gather_kernel(n, x_ref, out_ref, *sems):
-    gather_body(n, x_ref, out_ref, *sems)
+    gather = Gather(n, x_ref, out_ref, sems)
+    gather.start()
+    for count in range(1, gather.bits + 1):
+        gather.forward(count)
+    for mask in range(2**gather.bits):
+        gather.wait_core(mask)
+    gather.finish_sends()
+    gather.keep().wait()
 
 
 def gather_sems(n):
@@ -410,6 +446,322 @@
     )(slopes, proj, proj, proj, grad_mixed, labels[:, :, None], labels[:, None, :])
 
 
+def sum_kernel(n, d, flat_rows, x_ref, out_ref, pair, lines, send_sem, recv_sem, line_send, line_recv):
+    me, z = lax.axis_index("tensor"), lax.axis_index("dp")
+    levels = n.bit_length() - 1
+    barrier = pltpu.get_barrier_semaphore()
+    for level in range(levels):
+        pl.semaphore_signal(
+            barrier, inc=1, device_id=peer(flip(me, level)), device_id_type=pl.DeviceIdType.MESH
+        )
+    for ahead in range(1, d):
+        pl.semaphore_signal(
+            barrier, inc=1, device_id={"dp": lax.rem(z + ahead, d)}, device_id_type=pl.DeviceIdType.MESH
+        )
+    pl.semaphore_wait(barrier, levels + d - 1)
+    pair[0] = x_ref[:flat_rows, :]
+    sends = []
+    for level in range(levels):
+        copy = remote(
+            pair.at[2 * level], pair.at[2 * level + 1], send_sem.at[level], recv_sem.at[level], flip(me, level)
+        )
+        copy.start()
+        sends.append(copy)
+        copy.wait_recv()
+        pair[2 * level + 2] = pair[2 * level] + pair[2 * level + 1]
+    lines[0, :flat_rows, :] = pair[2 * levels]
+    lines[0, flat_rows:, :] = x_ref[flat_rows:, :]
+    for ahead in range(1, d):
+        copy = pltpu.make_async_remote_copy(
+            src_ref=lines.at[0],
+            dst_ref=lines.at[ahead],
+            send_sem=line_send.at[ahead],
+            recv_sem=line_recv.at[ahead],
+            device_id={"dp": lax.rem(z + ahead, d)},
+            device_id_type=pl.DeviceIdType.MESH,
+        )
+        copy.start()
+        sends.append(copy)
+    for copy in sends[levels:]:
+        copy.wait_recv()
+
+    total = None
+    for index in range(d):
+        value = lines[lax.rem(z - index + d, d)]
+        total = value if total is None else total + value
+    out_ref[...] = total
+    for copy in sends:
+        copy.wait_send()
+
+
+def sum_small(x, flat_rows, n, d, collective_id):
+    rows, width = x.shape
+    levels = n.bit_length() - 1
+    dma = pltpu.SemaphoreType.DMA
+    return pl.pallas_call(
+        functools.partial(sum_kernel, n, d, flat_rows),
+        out_shape=jax.ShapeDtypeStruct((rows, width), jnp.float32),
+        in_specs=[pl.BlockSpec(memory_space=pltpu.VMEM)],
+        out_specs=pl.BlockSpec(memory_space=pltpu.VMEM),
+        scratch_shapes=[
+            pltpu.VMEM((2 * levels + 1, flat_rows, width), jnp.float32),
+            pltpu.VMEM((d, rows, width), jnp.float32),
+            dma((levels,)),
+            dma((levels,)),
+            dma((d,)),
+            dma((d,)),
+        ],
+        compiler_params=pltpu.CompilerParams(collective_id=collective_id, has_side_effects=True),
+        name="sum_small",
+    )(x)
+
+
+def tile_of(width):
+    return 256 if width % 256 == 0 else width
+
+
+def attend_one(slope, proj_ref, start, head, column_ref, row_ref, out_ref, length):
+    at = pl.multiple_of(head * 3 * HEAD_DIM, HEAD_DIM)
+
+    def take(which, first, size):
+        return proj_ref[pl.ds(start + first, size), pl.ds(at + which * HEAD_DIM, HEAD_DIM)]
+
+    for first in range(0, length, BLOCK):
+        last = first + BLOCK
+        scores = masked_scores(
+            slope, take(0, first, BLOCK), take(1, 0, last), column_ref[first:last, :], row_ref[:, :last], first
+        )
+        top = jnp.max(scores, axis=1, keepdims=True)
+        expo = jnp.exp2(scores - top)
+        total = jnp.sum(expo, axis=1, keepdims=True)
+        mixed = jnp.dot(expo.astype(jnp.bfloat16), take(2, 0, last), preferred_element_type=jnp.float32)
+        out_ref[pl.ds(start + first, BLOCK), pl.ds(pl.multiple_of(head * HEAD_DIM, HEAD_DIM), HEAD_DIM)] = (
+            mixed / total
+        ).astype(out_ref.dtype)
+
+
+def project_kernel(
+    n, length, slope_ref, own_ref, rows_hbm, w_ref, bias_ref, column_ref, row_ref, gathered, proj_hbm, mixed_ref,
+    proj, buf, load_sem, store_sem, *sems
+):
+    gather = Gather(n, own_ref, gathered, sems)
+    rows = own_ref.shape[0]
+    width = w_ref.shape[1]
+    tile = tile_of(width)
+    heads = width // (3 * HEAD_DIM)
+    sequences = n * rows // length
+
+    def load(i):
+        at = pl.ds(pl.multiple_of(i * rows, rows), rows)
+        return pltpu.make_async_copy(rows_hbm.at[at, :], buf.at[lax.rem(i, 2)], load_sem.at[lax.rem(i, 2)])
+
+    load(0).start()
+    gather.start()
+
+    def store(i):
+        at = pl.ds(pl.multiple_of(i * rows, rows), rows)
+        return pltpu.make_async_copy(proj.at[at, :], proj_hbm.at[at, :], store_sem.at[i])
+
+    def project(i, carry):
+        load(i).wait()
+
+        @pl.when(i + 1 < n)
+        def _():
+            load(i + 1).start()
+
+        at = pl.ds(pl.multiple_of(i * rows, rows), rows)
+        for first in range(0, width, tile):
+            cols = slice(first, first + tile)
+            proj[at, cols] = (
+                jnp.dot(buf[lax.rem(i, 2)], w_ref[:, cols], preferred_element_type=jnp.float32) + bias_ref[:, cols]
+            ).astype(proj.dtype)
+        store(i).start()
+        return carry
+
+    lax.fori_loop(0, n, project, 0)
+    gather.forward(1)
+
+    def one(i, carry):
+        s, head = i // heads, lax.rem(i, heads)
+        attend_one(
+            slope_ref[head],
+            proj,
+            pl.multiple_of(s * length, length),
+            head,
+            column_ref.at[s],
+            row_ref.at[s],
+            mixed_ref,
+            length,
+        )
+        return carry
+
+    lax.fori_loop(0, sequences * heads, one, 0)
+    for count in range(2, gather.bits + 1):
+        gather.forward(count)
+    for i in range(n):
+        store(i).wait()
+    for mask in range(2**gather.bits):
+        gather.wait_core(mask)
+    gather.finish_sends()
+    gather.keep().wait()
+
+
+def project_attend(attn_rows, weight, bias, slopes, labels, own, n, collective_id):
+    total, depth = attn_rows.shape
+    rows, width = own.shape[0], weight.shape[1]
+    heads = width // (3 * HEAD_DIM)
+    vmem = pl.BlockSpec(memory_space=pltpu.VMEM)
+    hbm = pl.BlockSpec(memory_space=pl.ANY)
+    dma = pltpu.SemaphoreType.DMA
+    return pl.pallas_call(
+        functools.partial(project_kernel, n, labels.shape[1]),
+        out_shape=(
+            jax.ShapeDtypeStruct((total, own.shape[1]), own.dtype),
+            jax.ShapeDtypeStruct((total, width), jnp.bfloat16),
+            jax.ShapeDtypeStruct((total, heads * HEAD_DIM), jnp.bfloat16),
+        ),
+        in_specs=[pl.BlockSpec(memory_space=pltpu.SMEM), vmem, hbm, vmem, vmem, vmem, vmem],
+        out_specs=(hbm, hbm, vmem),
+        scratch_shapes=[
+            pltpu.VMEM((total, width), jnp.bfloat16),
+            pltpu.VMEM((2, rows, depth), jnp.bfloat16),
+            dma((2,)),
+            dma((n,)),
+        ]
+        + gather_sems(n),
+        compiler_params=pltpu.CompilerParams(
+            collective_id=collective_id, has_side_effects=True, vmem_limit_bytes=VMEM_LIMIT
+        ),
+        name="project_attend",
+    )(slopes, own, attn_rows, weight, bias, labels[:, :, None], labels[:, None, :])
+
+
+def gelu_both(value):
+    c, a = 0.7978845608028654, 0.044715
+    square = value * value
+    half = 0.5 + 0.5 * jnp.tanh(value * (c + (c * a) * square))
+    active = value * half
+    slope = half + (2.0 * active) * (1.0 - half) * (c + (3.0 * c * a) * square)
+    return active, slope
+
+
+def expand_kernel(
+    n, own_ref, grad_hbm, up_ref, down_ref, bias_ref, rows_hbm, act_hbm, pre_hbm, sum_ref,
+    gathered, grads, act, pre, load_sem, act_sem, pre_sem, rows_sem, *sems
+):
+    gather = Gather(n, own_ref, gathered, sems)
+    rows, depth = own_ref.shape
+    width = up_ref.shape[1]
+    tile = tile_of(width)
+    order = [gather.place(mask, core) for mask in (0,) for core in (0, 1)]
+    for count in range(1, gather.bits + 1):
+        for core in (0, 1):
+            order += [gather.place(mask, core) for mask in gather.level(count)]
+
+    def span(at):
+        return pl.ds(pl.multiple_of(at * rows, rows), rows)
+
+    def load(i):
+        return pltpu.make_async_copy(grad_hbm.at[span(order[i]), :], grads.at[i % 2], load_sem.at[i % 2])
+
+    def store(i):
+        return (
+            pltpu.make_async_copy(act.at[i % 2], act_hbm.at[span(order[i]), :], act_sem.at[i % 2]),
+            pltpu.make_async_copy(pre.at[i % 2], pre_hbm.at[span(order[i]), :], pre_sem.at[i % 2]),
+        )
+
+    def keep_rows(i):
+        return pltpu.make_async_copy(gathered.at[span(order[i]), :], rows_hbm.at[span(order[i]), :], rows_sem.at[i])
+
+    def work(i):
+        at = order[i]
+        keep_rows(i).start()
+        load(i).wait()
+        if i + 1 < n:
+            load(i + 1).start()
+        if i >= 2:
+            for copy in store(i - 2):
+                copy.wait()
+
+        def columns(j, carry):
+            cols = pl.ds(pl.multiple_of(j * tile, tile), tile)
+            before = (
+                jnp.dot(gathered[span(at), :], up_ref[:, cols], preferred_element_type=jnp.float32)
+                + bias_ref[:, cols]
+            )
+            back = lax.dot_general(grads[i % 2], down_ref[cols, :], NT, preferred_element_type=jnp.float32)
+            active, slope = gelu_both(before)
+            act[i % 2, :, cols] = active.astype(act.dtype)
+            rounded = (back * slope).astype(pre.dtype)
+            pre[i % 2, :, cols] = rounded
+            sum_ref[:, cols] += jnp.sum(rounded.astype(jnp.float32), axis=0, keepdims=True)
+            return carry
+
+        lax.fori_loop(0, width // tile, columns, 0)
+        for copy in store(i):
+            copy.start()
+
+    sum_ref[...] = jnp.zeros_like(sum_ref)
+    load(0).start()
+    gather.start()
+    gather.keep().wait()
+    work(0)
+    gather.wait_core(0)
+    work(1)
+    i = 2
+    for count in range(1, gather.bits + 1):
+        masks = gather.level(count)
+        gather.forward(count)
+        for _ in masks:
+            work(i)
+            i += 1
+        for mask in masks:
+            gather.wait_core(mask)
+            work(i)
+            i += 1
+    for last in (n - 2, n - 1):
+        for copy in store(last):
+            copy.wait()
+    for i in range(n):
+        keep_rows(i).wait()
+    gather.finish_sends()
+
+
+def expand(own, grad_rows, up, down, bias, n, collective_id):
+    rows, depth = own.shape
+    width = up.shape[1]
+    total = n * rows
+    vmem = pl.BlockSpec(memory_space=pltpu.VMEM)
+    hbm = pl.BlockSpec(memory_space=pl.ANY)
+    dma = pltpu.SemaphoreType.DMA
+    return pl.pallas_call(
+        functools.partial(expand_kernel, n),
+        out_shape=(
+            jax.ShapeDtypeStruct((total, depth), jnp.bfloat16),
+            jax.ShapeDtypeStruct((total, width), jnp.bfloat16),
+            jax.ShapeDtypeStruct((total, width), jnp.bfloat16),
+            jax.ShapeDtypeStruct((1, width), jnp.float32),
+        ),
+        in_specs=[vmem, hbm, vmem, vmem, vmem],
+        out_specs=(hbm, hbm, hbm, vmem),
+        scratch_shapes=[
+            pltpu.VMEM((total, depth), jnp.bfloat16),
+            pltpu.VMEM((2, rows, depth), jnp.bfloat16),
+            pltpu.VMEM((2, rows, width), jnp.bfloat16),
+            pltpu.VMEM((2, rows, width), jnp.bfloat16),
+            dma((2,)),
+            dma((2,)),
+            dma((2,)),
+            dma((n,)),
+        ]
+        + gather_sems(n),
+        compiler_params=pltpu.CompilerParams(
+            collective_id=collective_id, has_side_effects=True, vmem_limit_bytes=VMEM_LIMIT
+        ),
+        name="expand",
+    )(own, grad_rows, up, down, bias)
+
+
 HEADS = 16
 
 
@@ -456,6 +808,7 @@
     cotangent,
     *,
     n,
+    d,
 ):
     heads_local = query_bias.shape[0] // HEAD_DIM
     first_gain32 = first_gain.astype(jnp.float32)
@@ -487,29 +840,22 @@
     proj_bias = jnp.stack((query_bias32, jnp.zeros_like(query_bias32), value_bias32), axis=1).reshape(
         heads_local * 3 * HEAD_DIM
     )
-    proj = (jnp.dot(attn_rows, project_full, preferred_element_type=jnp.float32) + proj_bias).astype(
-        jnp.bfloat16
-    )
-    mixed = attend(proj, slopes, labels, length)
+    grad_rows, proj, mixed = project_attend(
+        attn_rows, project_full, proj_bias[None], slopes, labels, cotangent, n, 6
+    )
     attn_out = scatter_rows(mixed, dense_full, n, 2)
     residual = inputs + attn_out + dense_bias.astype(jnp.float32)
     normed_second, factor_second = normalize(residual)
     mlp_input = (normed_second * second_gain32 + second_shift.astype(jnp.float32)).astype(
         jnp.bfloat16
     )
-    mlp_rows = gather_rows(mlp_input, n, 1)
-    pre_act = jnp.dot(mlp_rows, expand_full, preferred_element_type=jnp.float32) + up_bias.astype(
-        jnp.float32
-    )
-    activated = gelu_tanh(pre_act).astype(jnp.bfloat16)
+    mlp_rows, activated, grad_pre, sum_up_bias = expand(
+        mlp_input, grad_rows, expand_full, shrink_full, up_bias.astype(jnp.float32)[None], n, 7
+    )
     mlp_out = scatter_rows(activated, shrink_full, n, 3)
     hidden_output = (residual + mlp_out + down_bias.astype(jnp.float32)).astype(jnp.bfloat16)
-    grad_rows = gather_rows(cotangent, n, 1)
     grad_down = jnp.einsum("tf,td->fd", activated, grad_rows, preferred_element_type=jnp.float32)
-    grad_act = jnp.einsum("td,fd->tf", grad_rows, shrink_full, preferred_element_type=jnp.float32)
-    grad_pre = jax.vjp(gelu_tanh, pre_act)[1](grad_act)[0].astype(jnp.bfloat16)
     grad_up = jnp.einsum("td,tf->df", mlp_rows, grad_pre, preferred_element_type=jnp.float32)
-    sum_up_bias = jnp.sum(grad_pre.astype(jnp.float32), axis=0)
     grad_mlp_in = scatter_rows(grad_pre, expand_full, n, 4, transposed=True, chunks=2)
     cotangent32 = cotangent.astype(jnp.float32)
     grad_residual = cotangent32 + norm_back(
@@ -547,17 +893,11 @@
             grad_down.astype(jnp.bfloat16), "dp", scatter_dimension=1, tiled=True
         ).astype(jnp.float32),
     )
-    grad_query_bias, grad_value_bias, grad_up_bias = lax.psum(
-        (sum_query_bias, sum_value_bias, sum_up_bias), "dp"
-    )
-    (
-        grad_first_gain,
-        grad_first_shift,
-        grad_second_gain,
-        grad_second_shift,
-        grad_dense_bias,
-        grad_down_bias,
-    ) = lax.psum(
+    model = sum_first_gain.shape[0]
+    heads_width = heads_local * HEAD_DIM
+    biases = jnp.concatenate((sum_query_bias, sum_value_bias, sum_up_bias[0]))
+    lines = -(-biases.shape[0] // model)
+    sums = jnp.concatenate(
         (
             sum_first_gain,
             sum_first_shift,
@@ -565,9 +905,18 @@
             sum_second_shift,
             sum_dense_bias,
             sum_down_bias,
-        ),
-        ("dp", "tensor"),
-    )
+            jnp.zeros((2 * model,), jnp.float32),
+            jnp.pad(biases, (0, -(-lines // 8) * 8 * model - biases.shape[0])),
+        )
+    ).reshape(-1, model)
+    sums = sum_small(sums, 8, n, d, 8)
+    grad_first_gain, grad_first_shift, grad_second_gain, grad_second_shift, grad_dense_bias, grad_down_bias = (
+        sums[i] for i in range(6)
+    )
+    biases = sums[8:].reshape(-1)
+    grad_query_bias = biases[:heads_width]
+    grad_value_bias = biases[heads_width : 2 * heads_width]
+    grad_up_bias = biases[2 * heads_width : 2 * heads_width + up_bias.shape[0]]
     return (
         hidden_output,
         grad_input,
@@ -589,7 +938,7 @@
 
 def solution(mesh):
     return jax.shard_map(
-        functools.partial(on_device, n=mesh.shape["tensor"]),
+        functools.partial(on_device, n=mesh.shape["tensor"], d=mesh.shape["dp"]),
         mesh=mesh,
         in_specs=(
             P(("dp", "tensor"), None),

time: 1020 us -> 943 us (0.925)
  matrix products: 173 us -> 90.3 us
  blocking collectives: 54.4 us -> 0 us
  Pallas kernels: 700 us -> 731 us
  waiting for transfers between devices: 13.3 us -> 38.3 us
    pallas_call x1 -> x3, Pallas kernels: 18.1 us -> 203 us  [the longest x1 92.7 us: expand(): pl.pallas_call(functools.partial(expand_kernel, n), out_shape=(jax.ShapeD...]
    pallas_call x4 -> x2, Pallas kernels: 307 us -> 154 us  [gather_rows(): pl.pallas_call(functools.partial(gather_kernel, n), out_shape=jax.ShapeDt...]
    dot_general x3 -> x0, matrix products: 83.4 us -> none  [the longest x1 40.3 us: on_device(): jnp.einsum('td,fd->tf', grad_rows, shrink_full, preferred_element_type=jn...]
    psum x2 -> x0, blocking collectives: 54.4 us -> none  [the longest x1 41.4 us: on_device(): lax.psum((sum_first_gain, sum_first_shift, sum_second_gain, sum_second_sh...]
    reduce_scatter x1, waiting for transfers between devices: 10.6 us -> 35.7 us  [on_device(): lax.psum_scatter(grad_down.astype(jnp.bfloat16), 'dp', scatter_dimension=...]
  transfers between devices with their start and end apart: 8 -> 8, of which waited for: 1 -> 1; matrix products, arithmetic and copies ran while one was open for 15% -> 13% of each run, Pallas kernels for 44% -> 41%
where the time goes in v2:
time: 943 us; the launch traced here: 937 us
  Pallas kernels  731 us (78%)
  matrix products  90.3 us (10%)
  other arithmetic  51.6 us (5%)
  waiting for transfers between devices  38.3 us (4%)
  between operations  14.7 us (2%)
  local copies, waits for them, and re-layouts  10.6 us (1%)
    pallas_call x4, Pallas kernels, scatter_rows(): pl.pallas_call(functools.partial(scatter_kernel, n, chunk, transposed), o...  343 us
    pallas_call x2, Pallas kernels, gather_rows(): pl.pallas_call(functools.partial(gather_kernel, n), out_shape=jax.ShapeDt...  154 us
    pallas_call x1, Pallas kernels, expand(): pl.pallas_call(functools.partial(expand_kernel, n), out_shape=(jax.ShapeD...  92.7 us
    pallas_call x1, Pallas kernels, project_attend(): pl.pallas_call(functools.partial(project_kernel, n, labels.shape[1]), out...  79.5 us
    reduce_scatter x1, waiting for transfers between devices, on_device(): lax.psum_scatter(grad_down.astype(jnp.bfloat16), 'dp', scatter_dimension=...  35.7 us
    pallas_call x1, Pallas kernels, attend_back(): pl.pallas_call(attend_back_kernel, grid=(sequences, heads), in_specs=[pl....  31 us
    pallas_call x1, Pallas kernels, sum_small(): pl.pallas_call(functools.partial(sum_kernel, n, d, flat_rows), out_shape=...  30.8 us
    dot_general x1, matrix products, on_device(): jnp.einsum('tf,td->fd', activated, grad_rows, preferred_element_type=jnp....  24.1 us
  transfers between devices with their start and end apart: 8, of which 1 were waited for; matrix products, arithmetic and copies ran while one was open for 13% of the time, Pallas kernels for 41%

profile of v2, /device:TPU:0, one launch (start us, length us, event | category | flops | bytes accessed | tf_op | source)
XLA Modules:
  0.0 937.0 jit_solution(10576593892872755103)
XLA Ops:
  14.7 78.5 %gather_rows.2.rows_hbm = bf16[4096,2048]{1,0:T(8,128)(2,1)} custom-call(bf16[512,2048]{1,0:T(8,128)(2,1)} %fusion.7.x_ref), custom_call_target="tpu_custom_call" | custom-call | tf_op jit(solution)/shard_map/gather_rows/pallas_call | solution.py:170
  99.5 79.5 %project_attend.1 = (bf16[4096,2048]{1,0:T(8,128)(2,1)}, bf16[4096,768]{1,0:T(8,128)(2,1)}, bf16[4096,256]{1,0:T(8,128)(2,1)}) custom-call(f32[2]{0:T(128)} %exponential_multiply_fusion.slope_ref, bf16[512,2048]{1,0:T(8,128)(2,1)} %own_ref.1, bf16[4096,2048]{1,0:T(8,128)(2,1)} %gather_rows.2.rows_hbm, bf16[2048,768]{1,0:T(8,128)(2,1)} %all-gather.5.cloned.1.call-done.w_ref, ...), custom_call_target="tpu_custom_call" | custom-call | tf_op jit(solution)/shard_map/project_attend/pallas_call | solution.py:616
  179.1 79.8 %scatter_rows.4 = f32[512,2048]{1,0:T(8,128)} custom-call(bf16[4096,256]{1,0:T(8,128)(2,1)} %get-tuple-element.22.a_ref, bf16[256,2048]{1,0:T(8,128)(2,1)} %all-gather.7.cloned.1.call-done.w_ref), custom_call_target="tpu_custom_call" | custom-call | tf_op jit(solution)/shard_map/scatter_rows/pallas_call | solution.py:310
  258.9 3.5 fusion.18
  266.5 92.7 %expand.1 = (bf16[4096,2048]{1,0:T(8,128)(2,1)}, bf16[4096,1024]{1,0:T(8,128)(2,1)}, bf16[4096,1024]{1,0:T(8,128)(2,1)}, f32[1,1024]{1,0:T(1,128)}) custom-call(bf16[512,2048]{1,0:T(8,128)(2,1)} %add_convert_fusion.1.own_ref, bf16[4096,2048]{1,0:T(8,128)(2,1)} %get-tuple-element.23.grad_hbm, bf16[2048,1024]{1,0:T(8,128)(2,1)} %all-gather.9.cloned.1.call-done.up_ref.w_ref, ...), custom_call_target="tpu_custom_call" | custom-call | tf_op jit(solution)/shard_map/expand/pallas_call | solution.py:737
  359.2 90.6 %scatter_rows.6 = f32[512,2048]{1,0:T(8,128)} custom-call(bf16[4096,1024]{1,0:T(8,128)(2,1)} %get-tuple-element.25.a_ref, bf16[2048,1024]{1,0:T(8,128)(2,1)} %all-gather.9.cloned.1.call-done.up_ref.w_ref), custom_call_target="tpu_custom_call" | custom-call | tf_op jit(solution)/shard_map/scatter_rows/pallas_call | solution.py:310
  449.9 4.4 multiply_reduce_fusion
  454.3 85.2 %scatter_rows.5 = f32[512,2048]{1,0:T(8,128)} custom-call(bf16[4096,1024]{1,0:T(8,128)(2,1)} %get-tuple-element.24.a_ref, bf16[1024,2048]{1,0:T(8,128)(2,1)} %all-gather.11.cloned.1.call-done.down_ref.w_ref), custom_call_target="tpu_custom_call" | custom-call | tf_op jit(solution)/shard_map/scatter_rows/pallas_call | solution.py:310
  539.5 7.7 fusion.17
  550.8 75.5 %gather_rows.3 = bf16[4096,2048]{1,0:T(8,128)(2,1)} custom-call(bf16[512,2048]{1,0:T(8,128)(2,1)} %convert_element_type.86.x_ref), custom_call_target="tpu_custom_call" | custom-call | tf_op jit(solution)/shard_map/gather_rows/pallas_call | solution.py:170
  626.3 12.0 %convolution_convert_fusion.4 = bf16[256,2048]{1,0:T(8,128)(2,1)} fusion(bf16[4096,256]{1,0:T(8,128)(2,1)} %get-tuple-element.22.a_ref, bf16[4096,2048]{1,0:T(8,128)(2,1)} %gather_rows.3), kind=kOutput, calls=%fused_computation.33 | convolution fusion | flops 4295491584 | bytes 19922944 | tf_op jit(solution)/shard_map/tc,td->cd/dot_general | solution.py:869
  638.3 10.3 %convolution_convert_fusion.g_ref = bf16[4096,256]{1,0:T(8,128)(2,1)} fusion(bf16[4096,2048]{1,0:T(8,128)(2,1)} %gather_rows.3, bf16[256,2048]{1,0:T(8,128)(2,1)S(1)} %copy-done.4), kind=kOutput, calls=%fused_computation.6 | convolution fusion | flops 4296015872 | bytes 19922944 | tf_op jit(solution)/shard_map/td,cd->tc/dot_general | solution.py:870
  648.6 31.0 %attend_back.1.a_ref = bf16[4096,768]{1,0:T(8,128)(2,1)} custom-call(f32[2]{0:T(128)} %exponential_multiply_fusion.slope_ref, bf16[4096,768]{1,0:T(8,128)(2,1)} %get-tuple-element.26.q_ref.k_ref.v_ref, bf16[4096,768]{1,0:T(8,128)(2,1)} %get-tuple-element.26.q_ref.k_ref.v_ref, bf16[4096,768]{1,0:T(8,128)(2,1)} %get-tuple-element.26.q_ref.k_ref.v_ref, ...), custom_call_target="tpu_custom_call" | custom-call | tf_op jit(solution)/shard_map/attend_back/pallas_call | solution.py:430
  679.6 20.2 %convolution_convert_fusion.3 = bf16[2048,768]{1,0:T(8,128)(2,1)} fusion(bf16[4096,2048]{1,0:T(8,128)(2,1)} %gather_rows.2.rows_hbm, bf16[4096,768]{1,0:T(8,128)(2,1)} %attend_back.1.a_ref), kind=kOutput, calls=%fused_computation.32 | convolution fusion | flops 12886474752 | bytes 26214400 | tf_op jit(solution)/shard_map/td,tc->dc/dot_general | solution.py:877
  699.8 23.8 %convolution_convert_fusion.2 = bf16[2048,1024]{1,0:T(8,128)(2,1)} fusion(bf16[4096,2048]{1,0:T(8,128)(2,1)} %get-tuple-element.28, bf16[4096,1024]{1,0:T(8,128)(2,1)} %get-tuple-element.25.a_ref), kind=kOutput, calls=%fused_computation.29 | convolution fusion | flops 17181966336 | bytes 29360128 | tf_op jit(solution)/shard_map/td,tf->df/dot_general | solution.py:858
  723.7 24.1 %convolution_convert_fusion.1 = bf16[1024,2048]{1,0:T(8,128)(2,1)} fusion(bf16[4096,1024]{1,0:T(8,128)(2,1)} %get-tuple-element.24.a_ref, bf16[4096,2048]{1,0:T(8,128)(2,1)} %get-tuple-element.23.grad_hbm), kind=kOutput, calls=%fused_computation.28 | convolution fusion | flops 17181966336 | bytes 29360128 | tf_op jit(solution)/shard_map/tf,td->fd/dot_general | solution.py:857
  747.8 3.7 convert_reduce_fusion
  751.5 87.5 %scatter_rows.7 = f32[512,2048]{1,0:T(8,128)} custom-call(bf16[4096,768]{1,0:T(8,128)(2,1)} %attend_back.1.a_ref, bf16[2048,768]{1,0:T(8,128)(2,1)} %all-gather.5.cloned.1.call-done.w_ref), custom_call_target="tpu_custom_call" | custom-call | tf_op jit(solution)/shard_map/scatter_rows/pallas_call | solution.py:310
  839.1 4.5 fusion.12
  844.3 30.8 %sum_small.1 = f32[16,2048]{1,0:T(8,128)} custom-call(f32[16,2048]{1,0:T(8,128)} %reshape.201.x_ref), custom_call_target="tpu_custom_call" | custom-call | tf_op jit(solution)/shard_map/sum_small/pallas_call | solution.py:501
  878.9 5.6 fusion.11
  888.7 2.8 convert_element_type.94
  891.5 35.7 %reduce-scatter.11.cloned.1.call-done = bf16[1024,512]{1,0:T(8,128)(2,1)} async-done(((bf16[1024,2048]{1,0:T(8,128)(2,1)}), bf16[1024,512]{1,0:T(8,128)(2,1)}) %reduce-scatter.11.cloned.1.call-update) | async-done | bytes 1048592 | tf_op jit(solution)/shard_map/reduce_scatter | solution.py:892
  927.2 2.8 convert_element_type.96
  (102 shorter events, 30.3 us)
Async XLA Ops:
  7.2 4.2 copy-start.1
  7.2 92.3 %all-gather.5.cloned.1.call-start = ((), (), s32[]{:S(2)}) async-start(), calls=%async_computation.4 | async-start | bytes 3932160 | tf_op jit(solution)/shard_map/all_gather | solution.py:823
  7.9 171.2 %all-gather.7.cloned.1.call-start = ((), (), s32[]{:S(2)}) async-start(), calls=%async_computation.5 | async-start | bytes 1310720 | tf_op jit(solution)/shard_map/all_gather | solution.py:824
  8.7 257.9 %all-gather.11.cloned.1.call-start = ((), (), s32[]{:S(2)}) async-start(), calls=%async_computation.7 | async-start | bytes 5242880 | tf_op jit(solution)/shard_map/all_gather | solution.py:826
  9.4 257.1 %all-gather.9.cloned.1.call-start = ((), (), s32[]{:S(2)}) async-start(), calls=%async_computation.6 | async-start | bytes 5242880 | tf_op jit(solution)/shard_map/all_gather | solution.py:825
  10.0 874.5 %reduce-scatter.7.cloned.1.call-start = ((), (), s32[]{:S(2)}) async-start(), calls=%async_computation.9 | async-start | bytes 1310720 | tf_op jit(solution)/shard_map/reduce_scatter | solution.py:886
  14.6 78.6 %copy-start.5 = (s32[4096]{0:T(1024)S(1)}, s32[4096]{0:T(1024)}, u32[]{:S(2)}) copy-start(s32[4096]{0:T(1024)} %param.31) | copy-start | bytes 49156
  14.6 80.5 %copy-start.13 = (bf16[256]{0:T(256)(128)(2,1)S(1)}, bf16[256]{0:T(256)(128)(2,1)}, u32[]{:S(2)}) copy-start(bf16[256]{0:T(256)(128)(2,1)} %param.21) | copy-start | bytes 1540
  14.6 80.6 %copy-start.14 = (bf16[256]{0:T(256)(128)(2,1)S(1)}, bf16[256]{0:T(256)(128)(2,1)}, u32[]{:S(2)}) copy-start(bf16[256]{0:T(256)(128)(2,1)} %param.22) | copy-start | bytes 1540
  14.6 81.3 %copy-start.6 = (bf16[2048]{0:T(1024)(128)(2,1)S(1)}, bf16[2048]{0:T(1024)(128)(2,1)}, u32[]{:S(2)}) copy-start(bf16[2048]{0:T(1024)(128)(2,1)} %param.24) | copy-start | bytes 12292
  14.6 81.3 %copy-start.7 = (bf16[2048]{0:T(1024)(128)(2,1)S(1)}, bf16[2048]{0:T(1024)(128)(2,1)}, u32[]{:S(2)}) copy-start(bf16[2048]{0:T(1024)(128)(2,1)} %param.25) | copy-start | bytes 12292
  14.7 81.3 %copy-start.8 = (bf16[2048]{0:T(1024)(128)(2,1)S(1)}, bf16[2048]{0:T(1024)(128)(2,1)}, u32[]{:S(2)}) copy-start(bf16[2048]{0:T(1024)(128)(2,1)} %param.26) | copy-start | bytes 12292
  14.7 81.3 %copy-start.11 = (bf16[1024]{0:T(1024)(128)(2,1)S(1)}, bf16[1024]{0:T(1024)(128)(2,1)}, u32[]{:S(2)}) copy-start(bf16[1024]{0:T(1024)(128)(2,1)} %param.28) | copy-start | bytes 6148
  14.7 81.9 %copy-start.9 = (bf16[2048]{0:T(1024)(128)(2,1)S(1)}, bf16[2048]{0:T(1024)(128)(2,1)}, u32[]{:S(2)}) copy-start(bf16[2048]{0:T(1024)(128)(2,1)} %param.30) | copy-start | bytes 12292
  14.7 81.9 %copy-start.12 = (s32[4,18]{1,0:T(4,128)S(1)}, s32[4,18]{1,0:T(4,128)}, u32[]{:S(2)}) copy-start(s32[4,18]{1,0:T(4,128)} %param.32) | copy-start | bytes 868
  262.4 2.0 copy-start
  547.1 2.0 copy-start.3
  626.3 12.0 %copy-start.4 = (bf16[256,2048]{1,0:T(8,128)(2,1)S(1)}, bf16[256,2048]{1,0:T(8,128)(2,1)}, u32[]{:S(2)}) copy-start(bf16[256,2048]{1,0:T(8,128)(2,1)} %all-gather.7.cloned.1.call-done.w_ref) | copy-start | bytes 3145732
  638.3 248.0 %reduce-scatter.5.cloned.1.call-start = ((), (), s32[]{:S(2)}) async-start(), calls=%async_computation.8 | async-start | bytes 3932160 | tf_op jit(solution)/shard_map/reduce_scatter | solution.py:883
  699.8 188.9 %reduce-scatter.9.cloned.1.call-start = ((), (), s32[]{:S(2)}) async-start(), calls=%async_computation.10 | async-start | bytes 5242880 | tf_op jit(solution)/shard_map/reduce_scatter | solution.py:889
  723.6 203.5 %reduce-scatter.11.cloned.1.call-start = ((), (), s32[]{:S(2)}) async-start(), calls=%async_computation.11 | async-start | bytes 5242880 | tf_op jit(solution)/shard_map/reduce_scatter | solution.py:892
  839.1 4.6 copy-start.10
  839.1 39.8 %copy-start.2 = (bf16[512,2048]{1,0:T(8,128)(2,1)S(1)}, bf16[512,2048]{1,0:T(8,128)(2,1)}, u32[]{:S(2)}) copy-start(bf16[512,2048]{1,0:T(8,128)(2,1)} %param.17) | copy-start | bytes 6291460
Sparse Core Ops, SparseCore 0:
  9.6 66.1 all-gather.4
  77.3 26.6 all-gather.6
  105.6 80.1 all-gather.10
  187.2 79.2 all-gather.8
  638.4 27.1 reduce-scatter.6
  699.9 60.1 reduce-scatter.4
  762.4 76.7 reduce-scatter.8
  841.4 85.7 reduce-scatter.10

commit v3 on v2

--- a/solution.py
+++ b/solution.py
@@ -180,153 +180,206 @@
     )(x)
 
 
-def scatter_kernel(n, chunk, transposed, a_ref, w_ref, out_ref, csend, crecv, held, recv, *sems):
-    me = lax.axis_index("tensor")
-    bits = chip_bits(n)
-    core_send, core_recv, chip_send, chip_recv = sems
-    rows, width = out_ref.shape
-    chunks = rows // chunk
-    parts = column_parts(width, bits)
-    total = 2**bits
-    other_core = flip(me, 0)
-    greet(me, bits)
-
-    def slot(part, index):
-        at = me
-        for step in range(bits):
-            if (index >> (bits - 1 - step)) & 1:
-                at = flip(at, 1 + (part + step) % bits)
+class Scatter:
+    def __init__(self, n, transposed, a_hbm, w_ref, out_ref, scratch):
+        (self.csend, self.crecv, self.recv, self.other, self.mine, self.load_sem) = scratch[:6]
+        self.core_send, self.core_recv, self.chip_send, self.chip_recv = scratch[6:]
+        self.me = lax.axis_index("tensor")
+        self.bits = chip_bits(n)
+        self.total = 2**self.bits
+        self.transposed = transposed
+        self.a, self.w, self.out = a_hbm, w_ref, out_ref
+        self.rows, width = out_ref.shape
+        self.chunk = self.csend.shape[2]
+        self.chunks = self.rows // self.chunk
+        self.parts = column_parts(width, self.bits)
+
+    def index_of(self, part, mask):
+        top = self.bits - 1
+        return sum(2 ** (top - (bit - part) % self.bits) for bit in range(self.bits) if (mask >> bit) & 1)
+
+    def place(self, mask, core):
+        at = flip(self.me, 0) if core else self.me
+        for bit in range(self.bits):
+            if (mask >> bit) & 1:
+                at = flip(at, 1 + bit)
         return at
 
-    def product(at, j, part):
-        start, size = parts[part]
-        lhs = a_ref[pl.ds(pl.multiple_of(at * rows + j * chunk, chunk), chunk), :]
-        if transposed:
-            return lax.dot_general(
-                lhs, w_ref[start : start + size, :], (((1,), (1,)), ((), ())), preferred_element_type=jnp.float32
+    def rows_of(self, j):
+        return pl.ds(pl.multiple_of(j * self.chunk, self.chunk), self.chunk)
+
+    def loads(self, j, core):
+        into = self.other if core else self.mine
+        copies = []
+        for mask in range(self.total):
+            start = pl.multiple_of(self.place(mask, core) * self.rows + j * self.chunk, self.chunk)
+            copies.append(
+                pltpu.make_async_copy(
+                    self.a.at[pl.ds(start, self.chunk), :],
+                    into.at[lax.rem(j, 2), pl.ds(mask * self.chunk, self.chunk), :],
+                    self.load_sem.at[core, lax.rem(j, 2), mask],
+                )
             )
-        return jnp.dot(lhs, w_ref[:, start : start + size], preferred_element_type=jnp.float32)
-
-    def strip(ref, first, count, j, part):
-        start, size = parts[part]
-        return ref.at[pl.ds(first, count), pl.ds(pl.multiple_of(j * chunk, chunk), chunk), pl.ds(start, size)]
-
-    def core_copy(j, part):
+        return copies
+
+    def core_copy(self, j, part):
+        start, size = self.parts[part]
         return remote(
-            strip(csend, 0, total, j, part),
-            strip(crecv, 0, total, j, part),
-            core_send.at[part, j],
-            core_recv.at[part, j],
-            other_core,
-        )
-
-    def chip_copy(j, part, step):
-        half = total >> (step + 1)
-        first = sum(total >> (s + 1) for s in range(step))
+            self.csend.at[lax.rem(j, 2), :, :, pl.ds(start, size)],
+            self.crecv.at[:, self.rows_of(j), pl.ds(start, size)],
+            self.core_send.at[part, j],
+            self.core_recv.at[part, j],
+            flip(self.me, 0),
+        )
+
+    def chip_copy(self, j, part, step):
+        half = self.total >> (step + 1)
+        first = sum(self.total >> (s + 1) for s in range(step))
+        start, size = self.parts[part]
         return remote(
-            strip(held, half, half, j, part),
-            strip(recv, first, half, j, part),
-            chip_send.at[part, step, j],
-            chip_recv.at[part, step, j],
-            flip(me, 1 + (part + step) % bits),
-        )
-
-    def rows_of(j):
-        return pl.ds(pl.multiple_of(j * chunk, chunk), chunk)
-
-    def stage_core(j):
-        for part in range(bits):
-            start, size = parts[part]
-            for index in range(total):
-                csend[index, rows_of(j), start : start + size] = product(
-                    flip(slot(part, index), 0), j, part
-                ).astype(csend.dtype)
-            core_copy(j, part).start()
-
-    def stage_first(j):
-        for part in range(bits):
-            start, size = parts[part]
-            core_copy(j, part).wait_recv()
-            for index in reversed(range(total)):
-                value = product(slot(part, index), j, part) + crecv[index, rows_of(j), start : start + size].astype(
-                    jnp.float32
+            self.crecv.at[pl.ds(half, half), self.rows_of(j), pl.ds(start, size)],
+            self.recv.at[pl.ds(first, half), self.rows_of(j), pl.ds(start, size)],
+            self.chip_send.at[part, step, j],
+            self.chip_recv.at[part, step, j],
+            flip(self.me, 1 + (part + step) % self.bits),
+        )
+
+    def tiles(self, part, lhs, put):
+        start, size = self.parts[part]
+        tile = 256 if size % 256 == 0 and start % 256 == 0 else 128
+
+        def one(i, carry):
+            cols = pl.ds(pl.multiple_of(start + i * tile, tile), tile)
+            if self.transposed:
+                value = lax.dot_general(
+                    lhs[...], self.w[cols, :], (((1,), (1,)), ((), ())), preferred_element_type=jnp.float32
                 )
+            else:
+                value = jnp.dot(lhs[...], self.w[:, cols], preferred_element_type=jnp.float32)
+            put(cols, value)
+            return carry
+
+        lax.fori_loop(0, size // tile, one, 0)
+
+    def piece(self, value, mask):
+        return value[mask * self.chunk : (mask + 1) * self.chunk, :]
+
+    def stage_core(self, j):
+        for copy in self.loads(j, 1):
+            copy.wait()
+
+        @pl.when(j >= 2)
+        def _():
+            for part in range(self.bits):
+                self.core_copy(j - 2, part).wait_send()
+
+        for part in range(self.bits):
+
+            def put(cols, value):
+                for mask in range(self.total):
+                    self.csend[lax.rem(j, 2), self.index_of(part, mask), :, cols] = self.piece(value, mask).astype(
+                        self.csend.dtype
+                    )
+
+            self.tiles(part, self.other.at[lax.rem(j, 2)], put)
+            self.core_copy(j, part).start()
+
+    def stage_first(self, j):
+        for copy in self.loads(j, 0):
+            copy.wait()
+        for part in range(self.bits):
+            self.core_copy(j, part).wait_recv()
+
+            def put(cols, value):
+                for mask in range(self.total):
+                    index = self.index_of(part, mask)
+                    got = self.piece(value, mask) + self.crecv[index, self.rows_of(j), cols].astype(jnp.float32)
+                    if index:
+                        self.crecv[index, self.rows_of(j), cols] = got.astype(self.crecv.dtype)
+                    else:
+                        self.out[self.rows_of(j), cols] = got
+
+            self.tiles(part, self.mine.at[lax.rem(j, 2)], put)
+            self.chip_copy(j, part, 0).start()
+
+    def stage_next(self, j, step):
+        half = self.total >> (step + 1)
+        first = sum(self.total >> (s + 1) for s in range(step))
+        for part in range(self.bits):
+            start, size = self.parts[part]
+            cols = slice(start, start + size)
+            self.chip_copy(j, part, step).wait_recv()
+            for index in reversed(range(half)):
+                got = self.recv[first + index, self.rows_of(j), cols].astype(jnp.float32)
                 if index:
-                    held[index, rows_of(j), start : start + size] = value.astype(held.dtype)
+                    value = self.crecv[index, self.rows_of(j), cols].astype(jnp.float32) + got
+                    self.crecv[index, self.rows_of(j), cols] = value.astype(self.crecv.dtype)
                 else:
-                    out_ref[rows_of(j), start : start + size] = value
-            chip_copy(j, part, 0).start()
-
-    def stage_next(j, step):
-        half = total >> (step + 1)
-        first = sum(total >> (s + 1) for s in range(step))
-        for part in range(bits):
-            start, size = parts[part]
-            chip_copy(j, part, step).wait_recv()
-            for index in reversed(range(half)):
-                got = recv[first + index, rows_of(j), start : start + size].astype(jnp.float32)
-                if index:
-                    value = held[index, rows_of(j), start : start + size].astype(jnp.float32) + got
-                    held[index, rows_of(j), start : start + size] = value.astype(held.dtype)
-                else:
-                    out_ref[rows_of(j), start : start + size] += got
-            if step + 1 < bits:
-                chip_copy(j, part, step + 1).start()
-
-    def body(u, carry):
-        for stage in range(bits + 2):
-            j = u - stage
-
-            @pl.when((j >= 0) & (j < chunks))
+                    self.out[self.rows_of(j), cols] += got
+            if step + 1 < self.bits:
+                self.chip_copy(j, part, step + 1).start()
+
+    def run(self, filler=None):
+        for copy in self.loads(0, 1):
+            copy.start()
+        greet(self.me, self.bits)
+
+        def body(u, carry):
+            @pl.when(u + 1 < self.chunks)
             def _():
-                if stage == 0:
-                    stage_core(j)
-                elif stage == 1:
-                    stage_first(j)
-                else:
-                    stage_next(j, stage - 2)
-
-        return carry
-
-    lax.fori_loop(0, chunks + bits + 1, body, 0)
-
-    def drain(j, carry):
-        for part in range(bits):
-            core_copy(j, part).wait_send()
-            for step in range(bits):
-                chip_copy(j, part, step).wait_send()
-        return carry
-
-    lax.fori_loop(0, chunks, drain, 0)
-
-
-def scatter_rows(a, w, n, collective_id, transposed=False, chunks=4):
-    rows = a.shape[0] // n
-    width = w.shape[0] if transposed else w.shape[1]
+                for copy in self.loads(u + 1, 1):
+                    copy.start()
+
+            @pl.when(u < self.chunks)
+            def _():
+                for copy in self.loads(u, 0):
+                    copy.start()
+                self.stage_core(u)
+
+            @pl.when((u >= 1) & (u <= self.chunks))
+            def _():
+                self.stage_first(u - 1)
+
+            for step in range(self.bits):
+
+                @pl.when((u >= 2 + step) & (u < self.chunks + 2 + step))
+                def _():
+                    self.stage_next(u - 2 - step, step)
+
+            if filler is not None:
+
+                @pl.when((u >= 1) & (u <= self.chunks))
+                def _():
+                    filler(u - 1)
+
+            return carry
+
+        lax.fori_loop(0, self.chunks + self.bits + 1, body, 0)
+        for part in range(self.bits):
+            for j in range(self.chunks):
+                if j >= self.chunks - 2:
+                    self.core_copy(j, part).wait_send()
+                for step in range(self.bits):
+                    self.chip_copy(j, part, step).wait_send()
+
+
+def scatter_scratch(n, rows, depth, width, chunks):
     bits = chip_bits(n)
     total = 2**bits
     chunk = rows // chunks
     dma = pltpu.SemaphoreType.DMA
-    return pl.pallas_call(
-        functools.partial(scatter_kernel, n, chunk, transposed),
-        out_shape=jax.ShapeDtypeStruct((rows, width), jnp.float32),
-        in_specs=[pl.BlockSpec(memory_space=pltpu.VMEM)] * 2,
-        out_specs=pl.BlockSpec(memory_space=pltpu.VMEM),
-        scratch_shapes=[
-            pltpu.VMEM((total, rows, width), jnp.bfloat16),
-            pltpu.VMEM((total, rows, width), jnp.bfloat16),
-            pltpu.VMEM((total, rows, width), jnp.bfloat16),
-            pltpu.VMEM((total - 1, rows, width), jnp.bfloat16),
-            dma((bits, chunks)),
-            dma((bits, chunks)),
-            dma((bits, bits, chunks)),
-            dma((bits, bits, chunks)),
-        ],
-        compiler_params=pltpu.CompilerParams(
-            collective_id=collective_id, has_side_effects=True, vmem_limit_bytes=VMEM_LIMIT
-        ),
-        name="scatter_rows",
-    )(a, w)
+    return [
+        pltpu.VMEM((2, total, chunk, width), jnp.bfloat16),
+        pltpu.VMEM((total, rows, width), jnp.bfloat16),
+        pltpu.VMEM((total - 1, rows, width), jnp.bfloat16),
+        pltpu.VMEM((2, total * chunk, depth), jnp.bfloat16),
+        pltpu.VMEM((2, total * chunk, depth), jnp.bfloat16),
+        dma((2, 2, total)),
+        dma((bits, chunks)),
+        dma((bits, chunks)),
+        dma((bits, bits, chunks)),
+        dma((bits, bits, chunks)),
+    ]
 
 
 HEAD_DIM = 128
@@ -349,104 +402,8 @@
     return jnp.where(same & causal, raw * (SCALE * LOG2E) + bias, -1e30)
 
 
-def attend_kernel(slope_ref, q_ref, k_ref, v_ref, column_ref, row_ref, out_ref):
-    slope = slope_ref[pl.program_id(1)]
-    length = q_ref.shape[0]
-    for first in range(0, length, BLOCK):
-        last = first + BLOCK
-        scores = masked_scores(
-            slope,
-            q_ref[first:last, :],
-            k_ref[:last, :],
-            column_ref[0, first:last, :],
-            row_ref[0, :, :last],
-            first,
-        )
-        top = jnp.max(scores, axis=1, keepdims=True)
-        expo = jnp.exp2(scores - top)
-        total = jnp.sum(expo, axis=1, keepdims=True)
-        mixed = jnp.dot(expo.astype(jnp.bfloat16), v_ref[:last, :], preferred_element_type=jnp.float32)
-        out_ref[first:last, :] = (mixed / total).astype(out_ref.dtype)
-
-
-def attend(proj, slopes, labels, length):
-    rows, width = proj.shape
-    heads = width // (3 * HEAD_DIM)
-    sequences = rows // length
-    part = lambda which: pl.BlockSpec((length, HEAD_DIM), lambda s, h: (s, h * 3 + which))
-    return pl.pallas_call(
-        attend_kernel,
-        grid=(sequences, heads),
-        in_specs=[
-            pl.BlockSpec(memory_space=pltpu.SMEM),
-            part(0),
-            part(1),
-            part(2),
-            pl.BlockSpec((1, length, 1), lambda s, h: (s, 0, 0)),
-            pl.BlockSpec((1, 1, length), lambda s, h: (s, 0, 0)),
-        ],
-        out_specs=pl.BlockSpec((length, HEAD_DIM), lambda s, h: (s, h)),
-        out_shape=jax.ShapeDtypeStruct((rows, heads * HEAD_DIM), jnp.bfloat16),
-        name="attend",
-    )(slopes, proj, proj, proj, labels[:, :, None], labels[:, None, :])
-
-
-def attend_back_kernel(slope_ref, q_ref, k_ref, v_ref, g_ref, column_ref, row_ref, out_ref, dk_ref, dv_ref):
-    slope = slope_ref[pl.program_id(1)]
-    length = q_ref.shape[0]
-    for first in reversed(range(0, length, BLOCK)):
-        last = first + BLOCK
-        q, g = q_ref[first:last, :], g_ref[first:last, :]
-        scores = masked_scores(
-            slope, q, k_ref[:last, :], column_ref[0, first:last, :], row_ref[0, :, :last], first
-        )
-        top = jnp.max(scores, axis=1, keepdims=True)
-        expo = jnp.exp2(scores - top)
-        probs = expo * (1.0 / jnp.sum(expo, axis=1, keepdims=True))
-        grad_probs = lax.dot_general(g, v_ref[:last, :], NT, preferred_element_type=jnp.float32)
-        product = probs * grad_probs
-        grad_scores = (product - probs * jnp.sum(product, axis=1, keepdims=True)).astype(jnp.bfloat16)
-        rounded = probs.astype(jnp.bfloat16)
-        out_ref[first:last, :HEAD_DIM] = (
-            jnp.dot(grad_scores, k_ref[:last, :], preferred_element_type=jnp.float32) * SCALE
-        ).astype(out_ref.dtype)
-        grad_keys = lax.dot_general(grad_scores, q, TN, preferred_element_type=jnp.float32)
-        grad_values = lax.dot_general(rounded, g, TN, preferred_element_type=jnp.float32)
-        if last == length:
-            dk_ref[...] = grad_keys
-            dv_ref[...] = grad_values
-        else:
-            dk_ref[:last, :] += grad_keys
-            dv_ref[:last, :] += grad_values
-    out_ref[:, HEAD_DIM : 2 * HEAD_DIM] = (dk_ref[...] * SCALE).astype(out_ref.dtype)
-    out_ref[:, 2 * HEAD_DIM :] = dv_ref[...].astype(out_ref.dtype)
-
-
-def attend_back(proj, grad_mixed, slopes, labels, length):
-    rows, width = proj.shape
-    heads = width // (3 * HEAD_DIM)
-    sequences = rows // length
-    part = lambda which: pl.BlockSpec((length, HEAD_DIM), lambda s, h: (s, h * 3 + which))
-    return pl.pallas_call(
-        attend_back_kernel,
-        grid=(sequences, heads),
-        in_specs=[
-            pl.BlockSpec(memory_space=pltpu.SMEM),
-            part(0),
-            part(1),
-            part(2),
-            pl.BlockSpec((length, HEAD_DIM), lambda s, h: (s, h)),
-            pl.BlockSpec((1, length, 1), lambda s, h: (s, 0, 0)),
-            pl.BlockSpec((1, 1, length), lambda s, h: (s, 0, 0)),
-        ],
-        out_specs=pl.BlockSpec((length, 3 * HEAD_DIM), lambda s, h: (s, h)),
-        out_shape=jax.ShapeDtypeStruct((rows, width), jnp.bfloat16),
-        scratch_shapes=[pltpu.VMEM((length, HEAD_DIM), jnp.float32)] * 2,
-        name="attend_back",
-    )(slopes, proj, proj, proj, grad_mixed, labels[:, :, None], labels[:, None, :])
-
-
-def sum_kernel(n, d, flat_rows, x_ref, out_ref, pair, lines, send_sem, recv_sem, line_send, line_recv):
+def sum_kernel(n, d, x_ref, y_ref, out_ref, pair, lines, send_sem, recv_sem, line_send, line_recv):
+    flat_rows = x_ref.shape[0]
     me, z = lax.axis_index("tensor"), lax.axis_index("dp")
     levels = n.bit_length() - 1
     barrier = pltpu.get_barrier_semaphore()
@@ -459,7 +416,7 @@
             barrier, inc=1, device_id={"dp": lax.rem(z + ahead, d)}, device_id_type=pl.DeviceIdType.MESH
         )
     pl.semaphore_wait(barrier, levels + d - 1)
-    pair[0] = x_ref[:flat_rows, :]
+    pair[0] = x_ref[...]
     sends = []
     for level in range(levels):
         copy = remote(
@@ -470,7 +427,7 @@
         copy.wait_recv()
         pair[2 * level + 2] = pair[2 * level] + pair[2 * level + 1]
     lines[0, :flat_rows, :] = pair[2 * levels]
-    lines[0, flat_rows:, :] = x_ref[flat_rows:, :]
+    lines[0, flat_rows:, :] = y_ref[...]
     for ahead in range(1, d):
         copy = pltpu.make_async_remote_copy(
             src_ref=lines.at[0],
@@ -494,14 +451,15 @@
         copy.wait_send()
 
 
-def sum_small(x, flat_rows, n, d, collective_id):
-    rows, width = x.shape
+def sum_small(x, y, n, d, collective_id):
+    flat_rows, width = x.shape
+    rows = flat_rows + y.shape[0]
     levels = n.bit_length() - 1
     dma = pltpu.SemaphoreType.DMA
     return pl.pallas_call(
-        functools.partial(sum_kernel, n, d, flat_rows),
+        functools.partial(sum_kernel, n, d),
         out_shape=jax.ShapeDtypeStruct((rows, width), jnp.float32),
-        in_specs=[pl.BlockSpec(memory_space=pltpu.VMEM)],
+        in_specs=[pl.BlockSpec(memory_space=pltpu.VMEM)] * 2,
         out_specs=pl.BlockSpec(memory_space=pltpu.VMEM),
         scratch_shapes=[
             pltpu.VMEM((2 * levels + 1, flat_rows, width), jnp.float32),
@@ -513,7 +471,7 @@
         ],
         compiler_params=pltpu.CompilerParams(collective_id=collective_id, has_side_effects=True),
         name="sum_small",
-    )(x)
+    )(x, y)
 
 
 def tile_of(width):
@@ -762,30 +720,475 @@
     )(own, grad_rows, up, down, bias)
 
 
+class Product:
+    def __init__(self, left, right, out, scratch):
+        self.left, self.right, self.out = left, right, out
+        self.lbuf, self.rbuf, self.acc, self.obuf, self.left_sem, self.right_sem, self.out_sem = scratch
+        self.depth, self.tall = self.lbuf.shape[1:]
+        self.wide = self.rbuf.shape[2]
+        self.inner = left.shape[0] // self.depth
+        self.across = right.shape[1] // self.wide
+        self.steps = (left.shape[1] // self.tall) * self.across * self.inner
+
+    def load(self, i):
+        k = lax.rem(i, self.inner)
+        col = lax.rem(i // self.inner, self.across)
+        row = i // (self.inner * self.across)
+        rows = pl.ds(pl.multiple_of(k * self.depth, self.depth), self.depth)
+        slot = lax.rem(i, 2)
+        return (
+            pltpu.make_async_copy(
+                self.left.at[rows, pl.ds(pl.multiple_of(row * self.tall, self.tall), self.tall)],
+                self.lbuf.at[slot],
+                self.left_sem.at[slot],
+            ),
+            pltpu.make_async_copy(
+                self.right.at[rows, pl.ds(pl.multiple_of(col * self.wide, self.wide), self.wide)],
+                self.rbuf.at[slot],
+                self.right_sem.at[slot],
+            ),
+        )
+
+    def store(self, tile):
+        col = lax.rem(tile, self.across)
+        row = tile // self.across
+        return pltpu.make_async_copy(
+            self.obuf,
+            self.out.at[
+                pl.ds(pl.multiple_of(row * self.tall, self.tall), self.tall),
+                pl.ds(pl.multiple_of(col * self.wide, self.wide), self.wide),
+            ],
+            self.out_sem,
+        )
+
+    def start(self):
+        for copy in self.load(0):
+            copy.start()
+
+    def step(self, i, carry=0):
+        for copy in self.load(i):
+            copy.wait()
+
+        @pl.when(i + 1 < self.steps)
+        def _():
+            for copy in self.load(i + 1):
+                copy.start()
+
+        k = lax.rem(i, self.inner)
+        slot = lax.rem(i, 2)
+        part = min(self.wide, 512)
+
+        @pl.when(k == 0)
+        def _():
+            self.acc[...] = jnp.zeros_like(self.acc)
+
+        for first in range(0, self.wide, part):
+            cols = slice(first, first + part)
+            self.acc[:, cols] += lax.dot_general(
+                self.lbuf[slot], self.rbuf[slot, :, cols], TN, preferred_element_type=jnp.float32
+            )
+
+        @pl.when(k == self.inner - 1)
+        def _():
+            tile = i // self.inner
+
+            @pl.when(tile > 0)
+            def _():
+                self.store(tile - 1).wait()
+
+            self.obuf[...] = self.acc[...].astype(self.obuf.dtype)
+            self.store(tile).start()
+
+        return carry
+
+    def batch(self, j, batches):
+        per = -(-self.steps // batches)
+        first = j * per
+        lax.fori_loop(first, jnp.minimum(first + per, self.steps), self.step, 0)
+
+    def finish(self):
+        self.store(self.steps // self.inner - 1).wait()
+
+
+def product_scratch(rows, tall, wide):
+    dma = pltpu.SemaphoreType.DMA
+    depth = min(1024, rows)
+    tall, wide = min(512, tall), min(1024, wide)
+    return [
+        pltpu.VMEM((2, depth, tall), jnp.bfloat16),
+        pltpu.VMEM((2, depth, wide), jnp.bfloat16),
+        pltpu.VMEM((tall, wide), jnp.float32),
+        pltpu.VMEM((tall, wide), jnp.bfloat16),
+        dma((2,)),
+        dma((2,)),
+        dma(()),
+    ]
+
+
+def row_blocks(rows, each, work):
+    def one(i, carry):
+        work(pl.ds(pl.multiple_of(i * each, each), each))
+        return carry
+
+    lax.fori_loop(0, rows // each, one, 0)
+
+
+def normal_rows(value):
+    center = value - jnp.mean(value, axis=1, keepdims=True)
+    factor = lax.rsqrt(jnp.mean(center * center, axis=1, keepdims=True) + 1e-05)
+    return center * factor, factor
+
+
+def dense_kernel(
+    n, a_hbm, w_ref, input_hbm, bias_ref, gain_ref, shift_ref, out_ref, next_ref, inputs, input_sem, *scratch
+):
+    fetch = pltpu.make_async_copy(input_hbm, inputs, input_sem)
+    fetch.start()
+    Scatter(n, False, a_hbm, w_ref, out_ref, scratch).run()
+    fetch.wait()
+
+    def work(at):
+        residual = inputs[at, :].astype(jnp.float32) + out_ref[at, :] + bias_ref[...]
+        out_ref[at, :] = residual
+        normed, _ = normal_rows(residual)
+        next_ref[at, :] = (normed * gain_ref[...] + shift_ref[...]).astype(next_ref.dtype)
+
+    row_blocks(out_ref.shape[0], 32, work)
+
+
+def back_rows(grad, source, gain):
+    normed, factor = normal_rows(source)
+    scaled = grad * gain
+    product = grad * normed
+    back = factor * (
+        scaled
+        - jnp.mean(scaled, axis=1, keepdims=True)
+        - normed * jnp.mean(scaled * normed, axis=1, keepdims=True)
+    )
+    return back, product
+
+
+def column_sum(value):
+    return jnp.sum(value, axis=0, keepdims=True)
+
+
+def expand_back_kernel(
+    n, a_hbm, w_ref, act_hbm, rows_hbm, residual_hbm, cotangent_hbm, gain_ref,
+    out_ref, next_ref, sums_ref, grad_hbm, residual, cotangent, fetch_sem, *scratch
+):
+    fetches = (
+        pltpu.make_async_copy(residual_hbm, residual, fetch_sem.at[0]),
+        pltpu.make_async_copy(cotangent_hbm, cotangent, fetch_sem.at[1]),
+    )
+    for fetch in fetches:
+        fetch.start()
+    product = Product(act_hbm, rows_hbm, grad_hbm, scratch[:7])
+    scatter = Scatter(n, True, a_hbm, w_ref, out_ref, scratch[7:])
+    product.start()
+    scatter.run(lambda j: product.batch(j, scatter.chunks))
+    product.finish()
+    for fetch in fetches:
+        fetch.wait()
+    sums_ref[...] = jnp.zeros_like(sums_ref)
+
+    def work(at):
+        grad = out_ref[at, :]
+        other = cotangent[at, :].astype(jnp.float32)
+        back, terms = back_rows(grad, residual[at, :], gain_ref[...])
+        result = other + back
+        out_ref[at, :] = result
+        next_ref[at, :] = result.astype(next_ref.dtype)
+        sums_ref[0:1, :] += column_sum(terms)
+        sums_ref[1:2, :] += column_sum(grad)
+        sums_ref[2:3, :] += column_sum(result)
+        sums_ref[3:4, :] += column_sum(other)
+
+    row_blocks(out_ref.shape[0], 32, work)
+
+
+def comm_params(collective_id):
+    return pltpu.CompilerParams(collective_id=collective_id, has_side_effects=True, vmem_limit_bytes=VMEM_LIMIT)
+
+
+VMEM_SPEC = pl.BlockSpec(memory_space=pltpu.VMEM)
+HBM_SPEC = pl.BlockSpec(memory_space=pl.ANY)
+CHUNKS = 4
+
+
+def dense(mixed, weight, inputs, bias, gain, shift, n, collective_id):
+    rows, width = inputs.shape
+    return pl.pallas_call(
+        functools.partial(dense_kernel, n),
+        out_shape=(
+            jax.ShapeDtypeStruct((rows, width), jnp.float32),
+            jax.ShapeDtypeStruct((rows, width), jnp.bfloat16),
+        ),
+        in_specs=[HBM_SPEC, VMEM_SPEC, HBM_SPEC, VMEM_SPEC, VMEM_SPEC, VMEM_SPEC],
+        out_specs=(VMEM_SPEC, VMEM_SPEC),
+        scratch_shapes=[pltpu.VMEM((rows, width), inputs.dtype), pltpu.SemaphoreType.DMA(())]
+        + scatter_scratch(n, rows, mixed.shape[1], width, CHUNKS),
+        compiler_params=comm_params(collective_id),
+        name="dense",
+    )(mixed, weight, inputs, bias, gain, shift)
+
+
+def expand_back(grad_pre, up, activated, grad_rows, residual, cotangent, gain, n, collective_id):
+    rows, width = residual.shape
+    units = activated.shape[1]
+    return pl.pallas_call(
+        functools.partial(expand_back_kernel, n),
+        out_shape=(
+            jax.ShapeDtypeStruct((rows, width), jnp.float32),
+            jax.ShapeDtypeStruct((rows, width), jnp.bfloat16),
+            jax.ShapeDtypeStruct((8, width), jnp.float32),
+            jax.ShapeDtypeStruct((units, width), jnp.bfloat16),
+        ),
+        in_specs=[HBM_SPEC, VMEM_SPEC, HBM_SPEC, HBM_SPEC, HBM_SPEC, HBM_SPEC, VMEM_SPEC],
+        out_specs=(VMEM_SPEC, VMEM_SPEC, VMEM_SPEC, HBM_SPEC),
+        scratch_shapes=[
+            pltpu.VMEM((rows, width), jnp.float32),
+            pltpu.VMEM((rows, width), cotangent.dtype),
+            pltpu.SemaphoreType.DMA((2,)),
+        ]
+        + product_scratch(n * rows, units, width)
+        + scatter_scratch(n, rows, units, width, CHUNKS),
+        compiler_params=comm_params(collective_id),
+        name="expand_back",
+    )(grad_pre, up, activated, grad_rows, residual, cotangent, gain)
+
+
+def dense_back_kernel(
+    n, own_ref, mixed_ref, w_ref, left_hbm, right_hbm, grad_mixed_ref, grad_dense_ref, grad_up_hbm, gathered, acc, *scratch
+):
+    product = Product(left_hbm, right_hbm, grad_up_hbm, scratch[:7])
+    gather = Gather(n, own_ref, gathered, scratch[7:])
+    rows = own_ref.shape[0]
+
+    def work(at):
+        span = pl.ds(pl.multiple_of(at * rows, rows), rows)
+        grad_mixed_ref[span, :] = lax.dot_general(
+            gathered[span, :], w_ref[...], NT, preferred_element_type=jnp.float32
+        ).astype(grad_mixed_ref.dtype)
+        width = acc.shape[1]
+        part = min(width, 512)
+        for first in range(0, width, part):
+            cols = slice(first, first + part)
+            acc[:, cols] += lax.dot_general(
+                mixed_ref[span, :], gathered[span, cols], TN, preferred_element_type=jnp.float32
+            )
+
+    product.start()
+    gather.start()
+    acc[...] = jnp.zeros_like(acc)
+    product.batch(0, 1)
+    for count in range(1, gather.bits + 1):
+        gather.forward(count)
+        if count == 1:
+            gather.keep().wait()
+            work(gather.place(0, 0))
+            gather.wait_core(0)
+            work(gather.place(0, 1))
+        for core in (0, 1):
+            for mask in gather.level(count):
+                if core:
+                    gather.wait_core(mask)
+                work(gather.place(mask, core))
+    grad_dense_ref[...] = acc[...].astype(grad_dense_ref.dtype)
+    product.finish()
+    gather.finish_sends()
+
+
+def dense_back(own, mixed, weight, mlp_rows, grad_pre, n, collective_id):
+    rows, width = own.shape
+    total, depth = mixed.shape
+    return pl.pallas_call(
+        functools.partial(dense_back_kernel, n),
+        out_shape=(
+            jax.ShapeDtypeStruct((total, depth), jnp.bfloat16),
+            jax.ShapeDtypeStruct((depth, width), jnp.bfloat16),
+            jax.ShapeDtypeStruct((mlp_rows.shape[1], grad_pre.shape[1]), jnp.bfloat16),
+        ),
+        in_specs=[VMEM_SPEC, VMEM_SPEC, VMEM_SPEC, HBM_SPEC, HBM_SPEC],
+        out_specs=(VMEM_SPEC, VMEM_SPEC, HBM_SPEC),
+        scratch_shapes=[pltpu.VMEM((total, width), jnp.bfloat16), pltpu.VMEM((depth, width), jnp.float32)]
+        + product_scratch(total, mlp_rows.shape[1], grad_pre.shape[1])
+        + gather_sems(n),
+        compiler_params=comm_params(collective_id),
+        name="dense_back",
+    )(own, mixed, weight, mlp_rows, grad_pre)
+
+
+def attend_back_one(slope, proj_ref, grad_ref, start, head, column_ref, row_ref, out_ref, dk_ref, dv_ref, sums_ref, length):
+    at = pl.multiple_of(head * 3 * HEAD_DIM, HEAD_DIM)
+    own = pl.ds(pl.multiple_of(head * HEAD_DIM, HEAD_DIM), HEAD_DIM)
+
+    def cols(which):
+        return pl.ds(at + which * HEAD_DIM, HEAD_DIM)
+
+    def take(which, first, size):
+        return proj_ref[pl.ds(start + first, size), cols(which)]
+
+    sums = None
+    for first in reversed(range(0, length, BLOCK)):
+        last = first + BLOCK
+        q, g = take(0, first, BLOCK), grad_ref[pl.ds(start + first, BLOCK), own]
+        scores = masked_scores(slope, q, take(1, 0, last), column_ref[first:last, :], row_ref[:, :last], first)
+        top = jnp.max(scores, axis=1, keepdims=True)
+        expo = jnp.exp2(scores - top)
+        probs = expo * (1.0 / jnp.sum(expo, axis=1, keepdims=True))
+        grad_probs = lax.dot_general(g, take(2, 0, last), NT, preferred_element_type=jnp.float32)
+        product = probs * grad_probs
+        grad_scores = (product - probs * jnp.sum(product, axis=1, keepdims=True)).astype(jnp.bfloat16)
+        rounded = probs.astype(jnp.bfloat16)
+        grad_queries = (jnp.dot(grad_scores, take(1, 0, last), preferred_element_type=jnp.float32) * SCALE).astype(
+            out_ref.dtype
+        )
+        out_ref[pl.ds(start + first, BLOCK), cols(0)] = grad_queries
+        here = column_sum(grad_queries.astype(jnp.float32))
+        sums = here if sums is None else sums + here
+        grad_keys = lax.dot_general(grad_scores, q, TN, preferred_element_type=jnp.float32)
+        grad_values = lax.dot_general(rounded, g, TN, preferred_element_type=jnp.float32)
+        if last == length:
+            dk_ref[...] = grad_keys
+            dv_ref[...] = grad_values
+        else:
+            dk_ref[:last, :] += grad_keys
+            dv_ref[:last, :] += grad_values
+    span = pl.ds(start, length)
+    out_ref[span, cols(1)] = (dk_ref[...] * SCALE).astype(out_ref.dtype)
+    grad_values = dv_ref[...].astype(out_ref.dtype)
+    out_ref[span, cols(2)] = grad_values
+    sums_ref[0:1, own] += sums
+    sums_ref[1:2, own] += column_sum(grad_values.astype(jnp.float32))
+
+
+def shrink_kernel(
+    n, length, slope_ref, a_hbm, w_ref, residual_hbm, bias_ref, proj_hbm, grad_mixed_ref, column_ref, row_ref,
+    hidden_ref, grad_proj_ref, sums_ref, out, residual, proj, dk, dv, fetch_sem, *scratch
+):
+    fetches = (
+        pltpu.make_async_copy(proj_hbm, proj, fetch_sem.at[0]),
+        pltpu.make_async_copy(residual_hbm, residual, fetch_sem.at[1]),
+    )
+    for fetch in fetches:
+        fetch.start()
+    scatter = Scatter(n, False, a_hbm, w_ref, out, scratch)
+    heads = grad_proj_ref.shape[1] // (3 * HEAD_DIM)
+    units = grad_proj_ref.shape[0] // length * heads
+    per = -(-units // scatter.chunks)
+    sums_ref[...] = jnp.zeros_like(sums_ref)
+
+    def one(i, carry):
+        s, head = i // heads, lax.rem(i, heads)
+        attend_back_one(
+            slope_ref[head], proj, grad_mixed_ref, pl.multiple_of(s * length, length), head, column_ref.at[s],
+            row_ref.at[s], grad_proj_ref, dk, dv, sums_ref, length,
+        )
+        return carry
+
+    def filler(j):
+        @pl.when(j == 0)
+        def _():
+            fetches[0].wait()
+
+        lax.fori_loop(j * per, jnp.minimum(j * per + per, units), one, 0)
+
+    scatter.run(filler)
+    fetches[1].wait()
+
+    def work(at):
+        hidden_ref[at, :] = (residual[at, :] + out[at, :] + bias_ref[...]).astype(hidden_ref.dtype)
+
+    row_blocks(out.shape[0], 64, work)
+
+
+def shrink(activated, down, residual, bias, slopes, proj, grad_mixed, labels, n, collective_id):
+    rows, width = residual.shape
+    heads_width = grad_mixed.shape[1]
+    length = labels.shape[1]
+    return pl.pallas_call(
+        functools.partial(shrink_kernel, n, length),
+        out_shape=(
+            jax.ShapeDtypeStruct((rows, width), jnp.bfloat16),
+            jax.ShapeDtypeStruct(proj.shape, jnp.bfloat16),
+            jax.ShapeDtypeStruct((8, heads_width), jnp.float32),
+        ),
+        in_specs=[
+            pl.BlockSpec(memory_space=pltpu.SMEM), HBM_SPEC, VMEM_SPEC, HBM_SPEC, VMEM_SPEC, HBM_SPEC, VMEM_SPEC, VMEM_SPEC,
+            VMEM_SPEC,
+        ],
+        out_specs=(VMEM_SPEC, VMEM_SPEC, VMEM_SPEC),
+        scratch_shapes=[
+            pltpu.VMEM((rows, width), jnp.float32),
+            pltpu.VMEM((rows, width), jnp.float32),
+            pltpu.VMEM(proj.shape, jnp.bfloat16),
+            pltpu.VMEM((length, HEAD_DIM), jnp.float32),
+            pltpu.VMEM((length, HEAD_DIM), jnp.float32),
+            pltpu.SemaphoreType.DMA((2,)),
+        ]
+        + scatter_scratch(n, rows, activated.shape[1], width, CHUNKS),
+        compiler_params=comm_params(collective_id),
+        name="shrink",
+    )(slopes, activated, down, residual, bias, proj, grad_mixed, labels[:, :, None], labels[:, None, :])
+
+
+def project_back_kernel(
+    n, a_hbm, w_ref, input_hbm, grad_hbm, gain_ref, earlier_ref, out_ref, sums_ref, inputs, grads, fetch_sem, *scratch
+):
+    fetches = (
+        pltpu.make_async_copy(input_hbm, inputs, fetch_sem.at[0]),
+        pltpu.make_async_copy(grad_hbm, grads, fetch_sem.at[1]),
+    )
+    for fetch in fetches:
+        fetch.start()
+    Scatter(n, True, a_hbm, w_ref, out_ref, scratch).run()
+    for fetch in fetches:
+        fetch.wait()
+    sums_ref[...] = earlier_ref[...]
+
+    def work(at):
+        grad = out_ref[at, :]
+        back, terms = back_rows(grad, inputs[at, :].astype(jnp.float32), gain_ref[...])
+        out_ref[at, :] = grads[at, :] + back
+        sums_ref[4:5, :] += column_sum(terms)
+        sums_ref[5:6, :] += column_sum(grad)
+
+    row_blocks(out_ref.shape[0], 32, work)
+
+
+def project_back(grad_proj, weight, inputs, grad_residual, gain, earlier, n, collective_id):
+    rows, width = inputs.shape
+    return pl.pallas_call(
+        functools.partial(project_back_kernel, n),
+        out_shape=(jax.ShapeDtypeStruct((rows, width), jnp.float32), jax.ShapeDtypeStruct((8, width), jnp.float32)),
+        in_specs=[HBM_SPEC, VMEM_SPEC, HBM_SPEC, HBM_SPEC, VMEM_SPEC, VMEM_SPEC],
+        out_specs=(VMEM_SPEC, VMEM_SPEC),
+        scratch_shapes=[
+            pltpu.VMEM((rows, width), inputs.dtype),
+            pltpu.VMEM((rows, width), jnp.float32),
+            pltpu.SemaphoreType.DMA((2,)),
+        ]
+        + scatter_scratch(n, rows, grad_proj.shape[1], width, CHUNKS),
+        compiler_params=comm_params(collective_id),
+        name="project_back",
+    )(grad_proj, weight, inputs, grad_residual, gain, earlier)
+
+
 HEADS = 16
-
-
-def gelu_tanh(value):
-    return (
-        0.5
-        * value
-        * (1.0 + jnp.tanh(0.7978845608028654 * (value + 0.044715 * value * value * value)))
-    )
 
 
 def normalize(rows):
     center = rows - jnp.mean(rows, axis=1, keepdims=True)
     factor = lax.rsqrt(jnp.mean(center * center, axis=1, keepdims=True) + 1e-05)
-    return (center * factor, factor)
-
-
-def norm_back(grad_out, normed, factor, gain):
-    scaled = grad_out * gain
-    return factor * (
-        scaled
-        - jnp.mean(scaled, axis=1, keepdims=True)
-        - normed * jnp.mean(scaled * normed, axis=1, keepdims=True)
-    )
+    return center * factor
+
+
+def wide(vector):
+    return vector.astype(jnp.float32)[None]
+
+
+def share(grad, dimension):
+    return lax.psum_scatter(grad, "dp", scatter_dimension=dimension, tiled=True).astype(jnp.float32)
 
 
 def on_device(
@@ -811,13 +1214,8 @@
     d,
 ):
     heads_local = query_bias.shape[0] // HEAD_DIM
-    first_gain32 = first_gain.astype(jnp.float32)
-    second_gain32 = second_gain.astype(jnp.float32)
-    inputs = hidden_input.astype(jnp.float32)
-    normed_first, factor_first = normalize(inputs)
-    attn_input = (normed_first * first_gain32 + first_shift.astype(jnp.float32)).astype(
-        jnp.bfloat16
-    )
+    normed_first = normalize(hidden_input.astype(jnp.float32))
+    attn_input = (normed_first * wide(first_gain) + wide(first_shift)).astype(jnp.bfloat16)
     attn_rows = gather_rows(attn_input, n, 1)
     project_full, dense_full, expand_full, shrink_full = (
         lax.all_gather(qkv_weight, "dp", axis=0, tiled=True),
@@ -843,74 +1241,38 @@
     grad_rows, proj, mixed = project_attend(
         attn_rows, project_full, proj_bias[None], slopes, labels, cotangent, n, 6
     )
-    attn_out = scatter_rows(mixed, dense_full, n, 2)
-    residual = inputs + attn_out + dense_bias.astype(jnp.float32)
-    normed_second, factor_second = normalize(residual)
-    mlp_input = (normed_second * second_gain32 + second_shift.astype(jnp.float32)).astype(
+    residual, mlp_input = dense(
+        mixed, dense_full, hidden_input, wide(dense_bias), wide(second_gain), wide(second_shift), n, 2
+    )
+    mlp_rows, activated, grad_pre, sum_up_bias = expand(
+        mlp_input, grad_rows, expand_full, shrink_full, wide(up_bias), n, 7
+    )
+    grad_residual, grad_attn_out, early_sums, grad_down = expand_back(
+        grad_pre, expand_full, activated, grad_rows, residual, cotangent, wide(second_gain), n, 4
+    )
+    grad_down_weight = share(grad_down, 1)
+    grad_mixed, grad_dense, grad_up = dense_back(grad_attn_out, mixed, dense_full, mlp_rows, grad_pre, n, 9)
+    grad_down_weight, activated, grad_mixed = lax.optimization_barrier((grad_down_weight, activated, grad_mixed))
+    grad_up_weight = share(grad_up, 0)
+    hidden_output, grad_proj, head_sums = shrink(
+        activated, shrink_full, residual, wide(down_bias), slopes, proj, grad_mixed, labels, n, 3
+    )
+    grad_up_weight, grad_proj = lax.optimization_barrier((grad_up_weight, grad_proj))
+    grad_project = jnp.einsum("td,tc->dc", attn_rows, grad_proj, preferred_element_type=jnp.float32).astype(
         jnp.bfloat16
     )
-    mlp_rows, activated, grad_pre, sum_up_bias = expand(
-        mlp_input, grad_rows, expand_full, shrink_full, up_bias.astype(jnp.float32)[None], n, 7
-    )
-    mlp_out = scatter_rows(activated, shrink_full, n, 3)
-    hidden_output = (residual + mlp_out + down_bias.astype(jnp.float32)).astype(jnp.bfloat16)
-    grad_down = jnp.einsum("tf,td->fd", activated, grad_rows, preferred_element_type=jnp.float32)
-    grad_up = jnp.einsum("td,tf->df", mlp_rows, grad_pre, preferred_element_type=jnp.float32)
-    grad_mlp_in = scatter_rows(grad_pre, expand_full, n, 4, transposed=True, chunks=2)
-    cotangent32 = cotangent.astype(jnp.float32)
-    grad_residual = cotangent32 + norm_back(
-        grad_mlp_in, normed_second, factor_second, second_gain32
-    )
-    sum_second_gain = jnp.sum(grad_mlp_in * normed_second, axis=0)
-    sum_second_shift = jnp.sum(grad_mlp_in, axis=0)
-    sum_down_bias = jnp.sum(cotangent32, axis=0)
-    sum_dense_bias = jnp.sum(grad_residual, axis=0)
-    grad_attn_rows = gather_rows(grad_residual.astype(jnp.bfloat16), n, 1)
-    grad_dense = jnp.einsum("tc,td->cd", mixed, grad_attn_rows, preferred_element_type=jnp.float32)
-    grad_mixed = jnp.einsum(
-        "td,cd->tc", grad_attn_rows, dense_full, preferred_element_type=jnp.float32
-    ).astype(jnp.bfloat16)
-    grad_proj = attend_back(proj, grad_mixed, slopes, labels, length)
-    proj_sums = jnp.sum(grad_proj.astype(jnp.float32), axis=0).reshape(heads_local, 3, HEAD_DIM)
-    sum_query_bias = proj_sums[:, 0].reshape(heads_local * HEAD_DIM)
-    sum_value_bias = proj_sums[:, 2].reshape(heads_local * HEAD_DIM)
-    grad_project = jnp.einsum("td,tc->dc", attn_rows, grad_proj, preferred_element_type=jnp.float32)
-    grad_attn_in = scatter_rows(grad_proj, project_full, n, 5, transposed=True, chunks=2)
-    grad_input = grad_residual + norm_back(grad_attn_in, normed_first, factor_first, first_gain32)
-    sum_first_gain = jnp.sum(grad_attn_in * normed_first, axis=0)
-    sum_first_shift = jnp.sum(grad_attn_in, axis=0)
-    grad_qkv_weight, grad_dense_weight, grad_up_weight, grad_down_weight = (
-        lax.psum_scatter(
-            grad_project.astype(jnp.bfloat16), "dp", scatter_dimension=0, tiled=True
-        ).astype(jnp.float32),
-        lax.psum_scatter(
-            grad_dense.astype(jnp.bfloat16), "dp", scatter_dimension=1, tiled=True
-        ).astype(jnp.float32),
-        lax.psum_scatter(
-            grad_up.astype(jnp.bfloat16), "dp", scatter_dimension=0, tiled=True
-        ).astype(jnp.float32),
-        lax.psum_scatter(
-            grad_down.astype(jnp.bfloat16), "dp", scatter_dimension=1, tiled=True
-        ).astype(jnp.float32),
-    )
-    model = sum_first_gain.shape[0]
+    grad_qkv_weight = share(grad_project, 0)
+    grad_dense_weight = share(grad_dense, 1)
+    grad_input, flat_sums = project_back(
+        grad_proj, project_full, hidden_input, grad_residual, wide(first_gain), early_sums, n, 5
+    )
+    model = hidden_input.shape[1]
     heads_width = heads_local * HEAD_DIM
-    biases = jnp.concatenate((sum_query_bias, sum_value_bias, sum_up_bias[0]))
-    lines = -(-biases.shape[0] // model)
-    sums = jnp.concatenate(
-        (
-            sum_first_gain,
-            sum_first_shift,
-            sum_second_gain,
-            sum_second_shift,
-            sum_dense_bias,
-            sum_down_bias,
-            jnp.zeros((2 * model,), jnp.float32),
-            jnp.pad(biases, (0, -(-lines // 8) * 8 * model - biases.shape[0])),
-        )
-    ).reshape(-1, model)
-    sums = sum_small(sums, 8, n, d, 8)
-    grad_first_gain, grad_first_shift, grad_second_gain, grad_second_shift, grad_dense_bias, grad_down_bias = (
+    biases = jnp.concatenate((head_sums[0], head_sums[1], sum_up_bias[0]))
+    lines = -(-biases.shape[0] // (8 * model)) * 8
+    biases = jnp.pad(biases, (0, lines * model - biases.shape[0])).reshape(lines, model)
+    sums = sum_small(flat_sums, biases, n, d, 8)
+    grad_second_gain, grad_second_shift, grad_dense_bias, grad_down_bias, grad_first_gain, grad_first_shift = (
         sums[i] for i in range(6)
     )
     biases = sums[8:].reshape(-1)

time: 943 us -> 873 us (0.926)
  matrix products: 90.3 us -> 20.3 us
  waiting for transfers between devices: 38.3 us -> 76.4 us
  other arithmetic: 51.6 us -> 20.6 us
    pallas_call x2 -> x1, Pallas kernels: 154 us -> 78.5 us  [gather_rows(): pl.pallas_call(functools.partial(gather_kernel, n), out_shape=jax.ShapeDt...]
    dot_general x4 -> x0, matrix products: 70.1 us -> none  [the longest x1 24.1 us: on_device(): jnp.einsum('tf,td->fd', activated, grad_rows, preferred_element_type=jnp....]
    pallas_call x6, Pallas kernels: 405 us -> 474 us  [the longest x1 99.1 us: expand_back(): pl.pallas_call(functools.partial(expand_back_kernel, n), out_shape=(jax.S...]
    reduce_scatter x4, waiting for transfers between devices: 35.7 us -> 73.5 us  [share(): lax.psum_scatter(grad, 'dp', scatter_dimension=dimension, tiled=True)]
    reduce_sum x4 -> x0, other arithmetic: 20.2 us -> none  [the longest x1 7.66 us: on_device(): sum_dense_bias = jnp.sum(grad_residual, axis=0)]
  transfers between devices with their start and end apart: 8 -> 8, of which waited for: 1 -> 2; matrix products, arithmetic and copies ran while one was open for 13% -> 5% of each run, Pallas kernels for 41% -> 61%
where the time goes in v3:
time: 873 us; the launch traced here: 868 us
  Pallas kernels  724 us (83%)
  waiting for transfers between devices  76.4 us (9%)
  other arithmetic  20.6 us (2%)
  matrix products  20.3 us (2%)
  between operations  14.7 us (2%)
  local copies, waits for them, and re-layouts  11.8 us (1%)
    pallas_call x1, Pallas kernels, expand_back(): pl.pallas_call(functools.partial(expand_back_kernel, n), out_shape=(jax.S...  99.1 us
    pallas_call x1, Pallas kernels, shrink(): pl.pallas_call(functools.partial(shrink_kernel, n, length), out_shape=(ja...  96 us
    pallas_call x1, Pallas kernels, expand(): pl.pallas_call(functools.partial(expand_kernel, n), out_shape=(jax.ShapeD...  92.5 us
    pallas_call x1, Pallas kernels, project_back(): pl.pallas_call(functools.partial(project_back_kernel, n), out_shape=(jax....  90.7 us
    pallas_call x1, Pallas kernels, dense(): pl.pallas_call(functools.partial(dense_kernel, n), out_shape=(jax.ShapeDt...  85.4 us
    pallas_call x1, Pallas kernels, project_attend(): pl.pallas_call(functools.partial(project_kernel, n, labels.shape[1]), out...  79.5 us
    pallas_call x1, Pallas kernels, gather_rows(): pl.pallas_call(functools.partial(gather_kernel, n), out_shape=jax.ShapeDt...  78.5 us
    pallas_call x1, Pallas kernels, dense_back(): pl.pallas_call(functools.partial(dense_back_kernel, n), out_shape=(jax.Sh...  77.9 us
  transfers between devices with their start and end apart: 8, of which 2 were waited for; matrix products, arithmetic and copies ran while one was open for 5% of the time, Pallas kernels for 61%

profile of v3, /device:TPU:0, one launch (start us, length us, event | category | flops | bytes accessed | tf_op | source)
XLA Modules:
  0.0 868.3 jit_solution(5095091824869815471)
XLA Ops:
  8.0 0.7 all-gather.7.cloned.1.call-update
  12.5 2.2 fusion.5.x_ref
  14.7 78.5 %gather_rows.1.rows_hbm = bf16[4096,2048]{1,0:T(8,128)(2,1)} custom-call(bf16[512,2048]{1,0:T(8,128)(2,1)} %fusion.5.x_ref), custom_call_target="tpu_custom_call" | custom-call | tf_op jit(solution)/shard_map/gather_rows/pallas_call | solution.py:170
  93.2 1.9 reshape.174
  99.7 1.6 fusion.6.column_ref
  101.3 79.5 %project_attend.1 = (bf16[4096,2048]{1,0:T(8,128)(2,1)}, bf16[4096,768]{1,0:T(8,128)(2,1)}, bf16[4096,256]{1,0:T(8,128)(2,1)}) custom-call(f32[2]{0:T(128)} %exponential_multiply_fusion.slope_ref, bf16[512,2048]{1,0:T(8,128)(2,1)} %cotangent_hbm.1, bf16[4096,2048]{1,0:T(8,128)(2,1)} %gather_rows.1.rows_hbm, ...), custom_call_target="tpu_custom_call" | custom-call | tf_op jit(solution)/shard_map/project_attend/pallas_call | solution.py:574
  180.9 85.4 %dense.1 = (f32[512,2048]{1,0:T(8,128)}, bf16[512,2048]{1,0:T(8,128)(2,1)}) custom-call(bf16[4096,256]{1,0:T(8,128)(2,1)} %get-tuple-element.41.a_hbm.mixed_ref, bf16[256,2048]{1,0:T(8,128)(2,1)} %all-gather.7.cloned.1.call-done.w_ref, bf16[512,2048]{1,0:T(8,128)(2,1)} %input_hbm.3, f32[1,2048]{1,0:T(1,128)} %bitcast.31, f32[1,2048]{1,0:T(1,128)} %bitcast.27, ...), custom_call_target="tpu_custom_call" | custom-call | tf_op jit(solution)/shard_map/dense/pallas_call | solution.py:920
  266.4 92.5 %expand.1 = (bf16[4096,2048]{1,0:T(8,128)(2,1)}, bf16[4096,1024]{1,0:T(8,128)(2,1)}, bf16[4096,1024]{1,0:T(8,128)(2,1)}, f32[1,1024]{1,0:T(1,128)}) custom-call(bf16[512,2048]{1,0:T(8,128)(2,1)} %get-tuple-element.42.own_ref, bf16[4096,2048]{1,0:T(8,128)(2,1)} %get-tuple-element.43.grad_hbm.rows_hbm, ...), custom_call_target="tpu_custom_call" | custom-call | tf_op jit(solution)/shard_map/expand/pallas_call | solution.py:695
  359.0 99.1 %expand_back.1 = (f32[512,2048]{1,0:T(8,128)}, bf16[512,2048]{1,0:T(8,128)(2,1)}, f32[8,2048]{1,0:T(8,128)}, bf16[1024,2048]{1,0:T(8,128)(2,1)}) custom-call(bf16[4096,1024]{1,0:T(8,128)(2,1)} %get-tuple-element.44.a_hbm.right_hbm, bf16[2048,1024]{1,0:T(8,128)(2,1)} %all-gather.9.cloned.1.call-done.up_ref.w_ref, ...), custom_call_target="tpu_custom_call" | custom-call | tf_op jit(solution)/shard_map/expand_back/pallas_call | solution.py:938
  458.2 77.9 %dense_back.1 = (bf16[4096,256]{1,0:T(8,128)(2,1)}, bf16[256,2048]{1,0:T(8,128)(2,1)}, bf16[2048,1024]{1,0:T(8,128)(2,1)}) custom-call(bf16[512,2048]{1,0:T(8,128)(2,1)} %get-tuple-element.48.own_ref, bf16[4096,256]{1,0:T(8,128)(2,1)} %get-tuple-element.41.a_hbm.mixed_ref, bf16[256,2048]{1,0:T(8,128)(2,1)} %all-gather.7.cloned.1.call-done.w_ref, ...), custom_call_target="tpu_custom_call" | custom-call | tf_op jit(solution)/shard_map/dense_back/pallas_call | solution.py:1004
  537.5 2.8 convert_element_type.46
  540.4 73.5 %reduce-scatter.7.cloned.1.call-done = bf16[512,1024]{1,0:T(8,128)(2,1)} async-done(((bf16[2048,1024]{1,0:T(8,128)(2,1)}), bf16[512,1024]{1,0:T(8,128)(2,1)}) %reduce-scatter.7.cloned.1.call-update) | async-done | bytes 1048592 | tf_op jit(solution)/shard_map/reduce_scatter | solution.py:1191
  613.8 2.8 convert_element_type.47
  616.6 96.0 %shrink.1 = (bf16[512,2048]{1,0:T(8,128)(2,1)}, bf16[4096,768]{1,0:T(8,128)(2,1)}, f32[8,256]{1,0:T(8,128)}) custom-call(f32[2]{0:T(128)} %exponential_multiply_fusion.slope_ref, bf16[4096,1024]{1,0:T(8,128)(2,1)} %get-tuple-element.51.act_hbm.a_hbm, bf16[1024,2048]{1,0:T(8,128)(2,1)} %all-gather.11.cloned.1.call-done.down_ref.w_ref, ...), custom_call_target="tpu_custom_call" | custom-call | tf_op jit(solution)/shard_map/shrink/pallas_call | solution.py:1109
  712.6 20.3 %convolution_convert_fusion = bf16[2048,768]{1,0:T(8,128)(2,1)} fusion(bf16[4096,2048]{1,0:T(8,128)(2,1)} %gather_rows.1.rows_hbm, bf16[4096,768]{1,0:T(8,128)(2,1)} %get-tuple-element.57.a_hbm), kind=kOutput, calls=%fused_computation.8 | convolution fusion | flops 12886474752 | bytes 26214400 | tf_op jit(solution)/shard_map/td,tc->dc/dot_general | solution.py:1261
  733.0 1.8 convert_element_type.50
  734.8 0.8 fusion.9
  736.2 90.7 %project_back.1 = (f32[512,2048]{1,0:T(8,128)}, f32[8,2048]{1,0:T(8,128)}) custom-call(bf16[4096,768]{1,0:T(8,128)(2,1)} %get-tuple-element.57.a_hbm, bf16[2048,768]{1,0:T(8,128)(2,1)} %all-gather.5.cloned.1.call-done.w_ref, bf16[512,2048]{1,0:T(8,128)(2,1)} %input_hbm.3, f32[512,2048]{1,0:T(8,128)} %get-tuple-element.58.grad_hbm, f32[1,2048]{1,0:T(1,128)} %bitcast.26, ...), custom_call_target="tpu_custom_call" | custom-call | tf_op jit(solution)/shard_map/project_back/pallas_call | solution.py:1161
  827.0 24.5 %sum_small.1 = f32[16,2048]{1,0:T(8,128)} custom-call(f32[8,2048]{1,0:T(8,128)} %get-tuple-element.61.x_ref, f32[8,2048]{1,0:T(8,128)} %reshape.165.y_ref), custom_call_target="tpu_custom_call" | custom-call | tf_op jit(solution)/shard_map/sum_small/pallas_call | solution.py:459
  851.5 0.8 slice_bitcast_fusion
  853.6 1.7 fusion.7
  855.3 2.5 convert_element_type.49
  857.8 1.3 copy.36
  859.2 2.0 copy.37
  (75 shorter events, 12.5 us)
Async XLA Ops:
  7.2 4.2 copy-start
  7.2 94.1 %all-gather.5.cloned.1.call-start = ((), (), s32[]{:S(2)}) async-start(), calls=%async_computation.4 | async-start | bytes 3932160 | tf_op jit(solution)/shard_map/all_gather | solution.py:1221
  7.9 172.9 %all-gather.7.cloned.1.call-start = ((), (), s32[]{:S(2)}) async-start(), calls=%async_computation.5 | async-start | bytes 1310720 | tf_op jit(solution)/shard_map/all_gather | solution.py:1222
  8.7 257.6 %all-gather.11.cloned.1.call-start = ((), (), s32[]{:S(2)}) async-start(), calls=%async_computation.7 | async-start | bytes 5242880 | tf_op jit(solution)/shard_map/all_gather | solution.py:1224
  9.4 257.0 %all-gather.9.cloned.1.call-start = ((), (), s32[]{:S(2)}) async-start(), calls=%async_computation.6 | async-start | bytes 5242880 | tf_op jit(solution)/shard_map/all_gather | solution.py:1223
  10.0 527.5 %reduce-scatter.5.cloned.1.call-start = ((), (), s32[]{:S(2)}) async-start(), calls=%async_computation.8 | async-start | bytes 5242880 | tf_op jit(solution)/shard_map/reduce_scatter | solution.py:1191
  10.7 3.9 copy-start.3
  14.6 78.6 %copy-start.4 = (s32[4096]{0:T(1024)S(1)}, s32[4096]{0:T(1024)}, u32[]{:S(2)}) copy-start(s32[4096]{0:T(1024)} %param.31) | copy-start | bytes 49156
  14.6 80.5 %copy-start.12 = (bf16[256]{0:T(256)(128)(2,1)S(1)}, bf16[256]{0:T(256)(128)(2,1)}, u32[]{:S(2)}) copy-start(bf16[256]{0:T(256)(128)(2,1)} %param.21) | copy-start | bytes 1540
  14.7 80.5 %copy-start.13 = (bf16[256]{0:T(256)(128)(2,1)S(1)}, bf16[256]{0:T(256)(128)(2,1)}, u32[]{:S(2)}) copy-start(bf16[256]{0:T(256)(128)(2,1)} %param.22) | copy-start | bytes 1540
  14.7 81.3 %copy-start.5 = (bf16[2048]{0:T(1024)(128)(2,1)S(1)}, bf16[2048]{0:T(1024)(128)(2,1)}, u32[]{:S(2)}) copy-start(bf16[2048]{0:T(1024)(128)(2,1)} %param.25) | copy-start | bytes 12292
  14.7 81.9 %copy-start.6 = (bf16[2048]{0:T(1024)(128)(2,1)S(1)}, bf16[2048]{0:T(1024)(128)(2,1)}, u32[]{:S(2)}) copy-start(bf16[2048]{0:T(1024)(128)(2,1)} %param.24) | copy-start | bytes 12292
  14.7 82.5 %copy-start.7 = (bf16[2048]{0:T(1024)(128)(2,1)S(1)}, bf16[2048]{0:T(1024)(128)(2,1)}, u32[]{:S(2)}) copy-start(bf16[2048]{0:T(1024)(128)(2,1)} %param.26) | copy-start | bytes 12292
  14.7 83.1 %copy-start.10 = (bf16[1024]{0:T(1024)(128)(2,1)S(1)}, bf16[1024]{0:T(1024)(128)(2,1)}, u32[]{:S(2)}) copy-start(bf16[1024]{0:T(1024)(128)(2,1)} %param.28) | copy-start | bytes 6148
  14.7 83.7 %copy-start.11 = (s32[4,18]{1,0:T(4,128)S(1)}, s32[4,18]{1,0:T(4,128)}, u32[]{:S(2)}) copy-start(s32[4,18]{1,0:T(4,128)} %param.32) | copy-start | bytes 868
  458.1 155.7 %reduce-scatter.7.cloned.1.call-start = ((), (), s32[]{:S(2)}) async-start(), calls=%async_computation.9 | async-start | bytes 5242880 | tf_op jit(solution)/shard_map/reduce_scatter | solution.py:1191
  536.1 0.7 copy-start.8
  536.2 196.8 %reduce-scatter.11.cloned.1.call-start = ((), (), s32[]{:S(2)}) async-start(), calls=%async_computation.11 | async-start | bytes 1310720 | tf_op jit(solution)/shard_map/reduce_scatter | solution.py:1191
  537.4 317.9 %reduce-scatter.9.cloned.1.call-start = ((), (), s32[]{:S(2)}) async-start(), calls=%async_computation.10 | async-start | bytes 3932160 | tf_op jit(solution)/shard_map/reduce_scatter | solution.py:1191
  712.6 22.9 %copy-start.9 = (f32[1,1024]{1,0:T(1,128)S(1)}, f32[1,1024]{1,0:T(1,128)}, u32[]{:S(2)}) copy-start(f32[1,1024]{1,0:T(1,128)} %get-tuple-element.63) | copy-start | bytes 12292
  827.0 30.9 %copy-start.2 = (bf16[512,2048]{1,0:T(8,128)(2,1)S(1)}, bf16[512,2048]{1,0:T(8,128)(2,1)}, u32[]{:S(2)}) copy-start(bf16[512,2048]{1,0:T(8,128)(2,1)} %get-tuple-element.92) | copy-start | bytes 6291460
  855.3 3.9 copy-start.1
Sparse Core Ops, SparseCore 0:
  9.6 66.1 all-gather.4
  77.3 26.6 all-gather.6
  105.6 80.1 all-gather.10
  187.1 79.2 all-gather.8
  458.2 76.0 reduce-scatter.4
  536.5 77.2 reduce-scatter.6
  616.1 27.7 reduce-scatter.10
  733.1 60.2 reduce-scatter.8

commit v4 on v3

--- a/solution.py
+++ b/solution.py
@@ -9,6 +9,7 @@
 from jax.sharding import PartitionSpec as P
 
 VMEM_LIMIT = 62 << 20
+LINK_COST = pl.CostEstimate(flops=0, bytes_accessed=280_000_000, transcendentals=0)
 
 
 def flip(index, bit):
@@ -29,13 +30,21 @@
     return {"tensor": index}
 
 
-def greet(me, bits):
+def greet(me, bits, d=1):
     barrier = pltpu.get_barrier_semaphore()
     for bit in range(bits + 1):
         pl.semaphore_signal(
             barrier, inc=1, device_id=peer(flip(me, bit)), device_id_type=pl.DeviceIdType.MESH
         )
-    pl.semaphore_wait(barrier, bits + 1)
+    for ahead in range(1, d):
+        pl.semaphore_signal(
+            barrier, inc=1, device_id=ahead_on_dp(ahead, d), device_id_type=pl.DeviceIdType.MESH
+        )
+    pl.semaphore_wait(barrier, bits + d)
+
+
+def ahead_on_dp(ahead, d):
+    return {"dp": lax.rem(lax.axis_index("dp") + ahead, d)}
 
 
 def remote(src, dst, send_sem, recv_sem, target):
@@ -176,6 +185,7 @@
         compiler_params=pltpu.CompilerParams(
             collective_id=collective_id, has_side_effects=True, vmem_limit_bytes=VMEM_LIMIT
         ),
+        cost_estimate=LINK_COST,
         name="gather_rows",
     )(x)
 
@@ -319,10 +329,10 @@
             if step + 1 < self.bits:
                 self.chip_copy(j, part, step + 1).start()
 
-    def run(self, filler=None):
+    def run(self, filler=None, d=1):
         for copy in self.loads(0, 1):
             copy.start()
-        greet(self.me, self.bits)
+        greet(self.me, self.bits, d)
 
         def body(u, carry):
             @pl.when(u + 1 < self.chunks)
@@ -402,76 +412,72 @@
     return jnp.where(same & causal, raw * (SCALE * LOG2E) + bias, -1e30)
 
 
-def sum_kernel(n, d, x_ref, y_ref, out_ref, pair, lines, send_sem, recv_sem, line_send, line_recv):
-    flat_rows = x_ref.shape[0]
-    me, z = lax.axis_index("tensor"), lax.axis_index("dp")
-    levels = n.bit_length() - 1
-    barrier = pltpu.get_barrier_semaphore()
-    for level in range(levels):
-        pl.semaphore_signal(
-            barrier, inc=1, device_id=peer(flip(me, level)), device_id_type=pl.DeviceIdType.MESH
-        )
-    for ahead in range(1, d):
-        pl.semaphore_signal(
-            barrier, inc=1, device_id={"dp": lax.rem(z + ahead, d)}, device_id_type=pl.DeviceIdType.MESH
-        )
-    pl.semaphore_wait(barrier, levels + d - 1)
-    pair[0] = x_ref[...]
-    sends = []
-    for level in range(levels):
-        copy = remote(
-            pair.at[2 * level], pair.at[2 * level + 1], send_sem.at[level], recv_sem.at[level], flip(me, level)
-        )
-        copy.start()
-        sends.append(copy)
-        copy.wait_recv()
-        pair[2 * level + 2] = pair[2 * level] + pair[2 * level + 1]
-    lines[0, :flat_rows, :] = pair[2 * levels]
-    lines[0, flat_rows:, :] = y_ref[...]
-    for ahead in range(1, d):
-        copy = pltpu.make_async_remote_copy(
-            src_ref=lines.at[0],
-            dst_ref=lines.at[ahead],
-            send_sem=line_send.at[ahead],
-            recv_sem=line_recv.at[ahead],
-            device_id={"dp": lax.rem(z + ahead, d)},
+class Total:
+    def __init__(self, n, d, scratch):
+        self.pair, self.lines, self.send, self.recv, self.line_send, self.line_recv = scratch
+        self.me, self.d = lax.axis_index("tensor"), d
+        self.levels = n.bit_length() - 1
+
+    def level_copy(self, level):
+        return remote(
+            self.pair.at[2 * level],
+            self.pair.at[2 * level + 1],
+            self.send.at[level],
+            self.recv.at[level],
+            flip(self.me, level),
+        )
+
+    def line_copy(self, ahead):
+        return pltpu.make_async_remote_copy(
+            src_ref=self.lines.at[0],
+            dst_ref=self.lines.at[ahead],
+            send_sem=self.line_send.at[ahead],
+            recv_sem=self.line_recv.at[ahead],
+            device_id=ahead_on_dp(ahead, self.d),
             device_id_type=pl.DeviceIdType.MESH,
         )
-        copy.start()
-        sends.append(copy)
-    for copy in sends[levels:]:
-        copy.wait_recv()
-
-    total = None
-    for index in range(d):
-        value = lines[lax.rem(z - index + d, d)]
-        total = value if total is None else total + value
-    out_ref[...] = total
-    for copy in sends:
-        copy.wait_send()
-
-
-def sum_small(x, y, n, d, collective_id):
-    flat_rows, width = x.shape
-    rows = flat_rows + y.shape[0]
+
+    def spread(self):
+        for ahead in range(1, self.d):
+            self.line_copy(ahead).start()
+
+    def step(self, level):
+        if level:
+            self.level_copy(level - 1).wait_recv()
+            self.pair[2 * level] = self.pair[2 * level - 2] + self.pair[2 * level - 1]
+        if level < self.levels:
+            self.level_copy(level).start()
+        else:
+            self.lines[0] = self.pair[2 * level]
+            self.spread()
+
+    def finish(self, levels=True):
+        for ahead in range(1, self.d):
+            self.line_copy(ahead).wait_recv()
+        z = lax.axis_index("dp")
+        total = None
+        for index in range(self.d):
+            value = self.lines[lax.rem(z - index + self.d, self.d)]
+            total = value if total is None else total + value
+        for ahead in range(1, self.d):
+            self.line_copy(ahead).wait_send()
+        if levels:
+            for level in range(self.levels):
+                self.level_copy(level).wait_send()
+        return total
+
+
+def total_scratch(n, d, rows, width):
     levels = n.bit_length() - 1
     dma = pltpu.SemaphoreType.DMA
-    return pl.pallas_call(
-        functools.partial(sum_kernel, n, d),
-        out_shape=jax.ShapeDtypeStruct((rows, width), jnp.float32),
-        in_specs=[pl.BlockSpec(memory_space=pltpu.VMEM)] * 2,
-        out_specs=pl.BlockSpec(memory_space=pltpu.VMEM),
-        scratch_shapes=[
-            pltpu.VMEM((2 * levels + 1, flat_rows, width), jnp.float32),
-            pltpu.VMEM((d, rows, width), jnp.float32),
-            dma((levels,)),
-            dma((levels,)),
-            dma((d,)),
-            dma((d,)),
-        ],
-        compiler_params=pltpu.CompilerParams(collective_id=collective_id, has_side_effects=True),
-        name="sum_small",
-    )(x, y)
+    return [
+        pltpu.VMEM((2 * levels + 1, rows, width), jnp.float32),
+        pltpu.VMEM((d, rows, width), jnp.float32),
+        dma((levels,)),
+        dma((levels,)),
+        dma((d,)),
+        dma((d,)),
+    ]
 
 
 def tile_of(width):
@@ -590,6 +596,7 @@
         compiler_params=pltpu.CompilerParams(
             collective_id=collective_id, has_side_effects=True, vmem_limit_bytes=VMEM_LIMIT
         ),
+        cost_estimate=LINK_COST,
         name="project_attend",
     )(slopes, own, attn_rows, weight, bias, labels[:, :, None], labels[:, None, :])
 
@@ -716,6 +723,7 @@
         compiler_params=pltpu.CompilerParams(
             collective_id=collective_id, has_side_effects=True, vmem_limit_bytes=VMEM_LIMIT
         ),
+        cost_estimate=LINK_COST,
         name="expand",
     )(own, grad_rows, up, down, bias)
 
@@ -928,6 +936,7 @@
         scratch_shapes=[pltpu.VMEM((rows, width), inputs.dtype), pltpu.SemaphoreType.DMA(())]
         + scatter_scratch(n, rows, mixed.shape[1], width, CHUNKS),
         compiler_params=comm_params(collective_id),
+        cost_estimate=LINK_COST,
         name="dense",
     )(mixed, weight, inputs, bias, gain, shift)
 
@@ -953,6 +962,7 @@
         + product_scratch(n * rows, units, width)
         + scatter_scratch(n, rows, units, width, CHUNKS),
         compiler_params=comm_params(collective_id),
+        cost_estimate=LINK_COST,
         name="expand_back",
     )(grad_pre, up, activated, grad_rows, residual, cotangent, gain)
 
@@ -1014,6 +1024,7 @@
         + product_scratch(total, mlp_rows.shape[1], grad_pre.shape[1])
         + gather_sems(n),
         compiler_params=comm_params(collective_id),
+        cost_estimate=LINK_COST,
         name="dense_back",
     )(own, mixed, weight, mlp_rows, grad_pre)
 
@@ -1128,12 +1139,14 @@
         ]
         + scatter_scratch(n, rows, activated.shape[1], width, CHUNKS),
         compiler_params=comm_params(collective_id),
+        cost_estimate=LINK_COST,
         name="shrink",
     )(slopes, activated, down, residual, bias, proj, grad_mixed, labels[:, :, None], labels[:, None, :])
 
 
 def project_back_kernel(
-    n, a_hbm, w_ref, input_hbm, grad_hbm, gain_ref, earlier_ref, out_ref, sums_ref, inputs, grads, fetch_sem, *scratch
+    n, d, a_hbm, w_ref, input_hbm, grad_hbm, gain_ref, early_ref, up_sum_ref, head_sums_ref,
+    out_ref, sums_ref, biases_ref, inputs, grads, fetch_sem, *scratch
 ):
     fetches = (
         pltpu.make_async_copy(input_hbm, inputs, fetch_sem.at[0]),
@@ -1141,37 +1154,86 @@
     )
     for fetch in fetches:
         fetch.start()
-    Scatter(n, True, a_hbm, w_ref, out_ref, scratch).run()
+    early, biases, late = (Total(n, d, scratch[6 * i : 6 * i + 6]) for i in range(3))
+    scatter = Scatter(n, True, a_hbm, w_ref, out_ref, scratch[18:])
+    model = out_ref.shape[1]
+    half, quarter = model // 2, model // 4
+    heads_width = head_sums_ref.shape[1]
+
+    def pack(i, width):
+        return [(i * (model // width) + k, slice(k * width, (k + 1) * width)) for k in range(model // width)]
+
+    def filler(j):
+        for level in range(min(early.levels + 1, scatter.chunks)):
+
+            @pl.when(j == level)
+            def _():
+                if level == 0:
+                    biases.lines[0] = jnp.zeros(biases.lines.shape[1:], jnp.float32)
+                    biases.lines[0, 0:1, :] = up_sum_ref[...]
+                    biases.lines[0, 1:3, :heads_width] = head_sums_ref[0:2, :]
+                    biases.spread()
+                    for i in range(4):
+                        for row, cols in pack(i, half):
+                            early.pair[0, row : row + 1, :] = early_ref[i : i + 1, cols]
+                early.step(level)
+
+    scatter.run(filler, d)
+    for level in range(scatter.chunks, early.levels + 1):
+        early.step(level)
     for fetch in fetches:
         fetch.wait()
-    sums_ref[...] = earlier_ref[...]
+    late.pair[0] = jnp.zeros(late.pair.shape[1:], jnp.float32)
 
     def work(at):
         grad = out_ref[at, :]
         back, terms = back_rows(grad, inputs[at, :].astype(jnp.float32), gain_ref[...])
         out_ref[at, :] = grads[at, :] + back
-        sums_ref[4:5, :] += column_sum(terms)
-        sums_ref[5:6, :] += column_sum(grad)
+        for i, value in enumerate((column_sum(terms), column_sum(grad))):
+            for row, cols in pack(i, quarter):
+                late.pair[0, row : row + 1, :] += value[:, cols]
 
     row_blocks(out_ref.shape[0], 32, work)
-
-
-def project_back(grad_proj, weight, inputs, grad_residual, gain, earlier, n, collective_id):
+    late.step(0)
+    biases_ref[...] = biases.finish(False)
+    total = early.finish()
+    for i in range(4):
+        for row, cols in pack(i, half):
+            sums_ref[i : i + 1, cols] = total[row : row + 1, :]
+    for level in range(1, late.levels + 1):
+        late.step(level)
+    total = late.finish()
+    for i in range(2):
+        for row, cols in pack(i, quarter):
+            sums_ref[4 + i : 5 + i, cols] = total[row : row + 1, :]
+    sums_ref[6:8, :] = jnp.zeros((2, model), jnp.float32)
+
+
+def project_back(grad_proj, weight, inputs, grad_residual, gain, early, up_sum, head_sums, n, d, collective_id):
     rows, width = inputs.shape
+    units = up_sum.shape[1]
     return pl.pallas_call(
-        functools.partial(project_back_kernel, n),
-        out_shape=(jax.ShapeDtypeStruct((rows, width), jnp.float32), jax.ShapeDtypeStruct((8, width), jnp.float32)),
-        in_specs=[HBM_SPEC, VMEM_SPEC, HBM_SPEC, HBM_SPEC, VMEM_SPEC, VMEM_SPEC],
-        out_specs=(VMEM_SPEC, VMEM_SPEC),
+        functools.partial(project_back_kernel, n, d),
+        out_shape=(
+            jax.ShapeDtypeStruct((rows, width), jnp.float32),
+            jax.ShapeDtypeStruct((8, width), jnp.float32),
+            jax.ShapeDtypeStruct((8, units), jnp.float32),
+        ),
+        in_specs=[HBM_SPEC, VMEM_SPEC, HBM_SPEC, HBM_SPEC] + [VMEM_SPEC] * 4,
+        out_specs=(VMEM_SPEC, VMEM_SPEC, VMEM_SPEC),
         scratch_shapes=[
             pltpu.VMEM((rows, width), inputs.dtype),
             pltpu.VMEM((rows, width), jnp.float32),
             pltpu.SemaphoreType.DMA((2,)),
         ]
+        + total_scratch(n, d, 8, width // 2)
+        + total_scratch(n, d, 8, units)
+        + total_scratch(n, d, 8, width // 4)
         + scatter_scratch(n, rows, grad_proj.shape[1], width, CHUNKS),
         compiler_params=comm_params(collective_id),
+        cost_estimate=LINK_COST,
         name="project_back",
-    )(grad_proj, weight, inputs, grad_residual, gain, earlier)
+    )(grad_proj, weight, inputs, grad_residual, gain, early, up_sum, head_sums)
 
 
 HEADS = 16
@@ -1257,28 +1319,19 @@
     hidden_output, grad_proj, head_sums = shrink(
         activated, shrink_full, residual, wide(down_bias), slopes, proj, grad_mixed, labels, n, 3
     )
-    grad_up_weight, grad_proj = lax.optimization_barrier((grad_up_weight, grad_proj))
     grad_project = jnp.einsum("td,tc->dc", attn_rows, grad_proj, preferred_element_type=jnp.float32).astype(
         jnp.bfloat16
     )
     grad_qkv_weight = share(grad_project, 0)
     grad_dense_weight = share(grad_dense, 1)
-    grad_input, flat_sums = project_back(
-        grad_proj, project_full, hidden_input, grad_residual, wide(first_gain), early_sums, n, 5
-    )
-    model = hidden_input.shape[1]
+    grad_input, sums, biases = project_back(
+        grad_proj, project_full, hidden_input, grad_residual, wide(first_gain), early_sums, sum_up_bias, head_sums, n, d, 5
+    )
     heads_width = heads_local * HEAD_DIM
-    biases = jnp.concatenate((head_sums[0], head_sums[1], sum_up_bias[0]))
-    lines = -(-biases.shape[0] // (8 * model)) * 8
-    biases = jnp.pad(biases, (0, lines * model - biases.shape[0])).reshape(lines, model)
-    sums = sum_small(flat_sums, biases, n, d, 8)
     grad_second_gain, grad_second_shift, grad_dense_bias, grad_down_bias, grad_first_gain, grad_first_shift = (
         sums[i] for i in range(6)
     )
-    biases = sums[8:].reshape(-1)
-    grad_query_bias = biases[:heads_width]
-    grad_value_bias = biases[heads_width : 2 * heads_width]
-    grad_up_bias = biases[2 * heads_width : 2 * heads_width + up_bias.shape[0]]
+    grad_up_bias, grad_query_bias, grad_value_bias = biases[0], biases[1, :heads_width], biases[2, :heads_width]
     return (
         hidden_output,
         grad_input,

time: 873 us -> 788 us (0.903)
  waiting for transfers between devices: 76.4 us -> 3.47 us
  Pallas kernels: 724 us -> 714 us
    reduce_scatter x4, waiting for transfers between devices: 73.5 us -> 0.03 us  [share(): lax.psum_scatter(grad, 'dp', scatter_dimension=dimension, tiled=True)]
    pallas_call x2 -> x1, Pallas kernels: 115 us -> 104 us  [project_back(): pl.pallas_call(functools.partial(project_back_kernel, n, d), out_shape=(j...]
  transfers between devices with their start and end apart: 8 -> 8, of which waited for: 2 -> 1; matrix products, arithmetic and copies ran while one was open for 5% -> 6% of each run, Pallas kernels for 61% -> 67%
where the time goes in v4:
time: 788 us; the launch traced here: 783 us
  Pallas kernels  714 us (91%)
  other arithmetic  20.5 us (3%)
  matrix products  20.3 us (3%)
  between operations  14.6 us (2%)
  local copies, waits for them, and re-layouts  10.6 us (1%)
    pallas_call x1, Pallas kernels, project_back(): pl.pallas_call(functools.partial(project_back_kernel, n, d), out_shape=(j...  104 us
    pallas_call x1, Pallas kernels, expand_back(): pl.pallas_call(functools.partial(expand_back_kernel, n), out_shape=(jax.S...  99.2 us
    pallas_call x1, Pallas kernels, shrink(): pl.pallas_call(functools.partial(shrink_kernel, n, length), out_shape=(ja...  96.2 us
    pallas_call x1, Pallas kernels, expand(): pl.pallas_call(functools.partial(expand_kernel, n), out_shape=(jax.ShapeD...  92.6 us
    pallas_call x1, Pallas kernels, dense(): pl.pallas_call(functools.partial(dense_kernel, n), out_shape=(jax.ShapeDt...  85.4 us
    pallas_call x1, Pallas kernels, project_attend(): pl.pallas_call(functools.partial(project_kernel, n, labels.shape[1]), out...  79.6 us
    pallas_call x1, Pallas kernels, gather_rows(): pl.pallas_call(functools.partial(gather_kernel, n), out_shape=jax.ShapeDt...  78.5 us
    pallas_call x1, Pallas kernels, dense_back(): pl.pallas_call(functools.partial(dense_back_kernel, n), out_shape=(jax.Sh...  78.1 us
  transfers between devices with their start and end apart: 8, of which 1 were waited for; matrix products, arithmetic and copies ran while one was open for 6% of the time, Pallas kernels for 67%

profile of v4, /device:TPU:0, one launch (start us, length us, event | category | flops | bytes accessed | tf_op | source)
XLA Modules:
  0.0 783.5 jit_solution(6313343435746993081)
XLA Ops:
  8.0 0.7 all-gather.7.cloned.1.call-update
  10.7 0.7 convert_element_type.42
  12.5 2.2 fusion.5.x_ref
  14.7 78.5 %gather_rows.1.rows_hbm = bf16[4096,2048]{1,0:T(8,128)(2,1)} custom-call(bf16[512,2048]{1,0:T(8,128)(2,1)} %fusion.5.x_ref), custom_call_target="tpu_custom_call" | custom-call | bytes 280000000 | tf_op jit(solution)/shard_map/gather_rows/pallas_call | solution.py:179
  93.2 1.9 reshape.166
  99.7 1.6 fusion.6.column_ref
  101.3 79.6 %project_attend.1 = (bf16[4096,2048]{1,0:T(8,128)(2,1)}, bf16[4096,768]{1,0:T(8,128)(2,1)}, bf16[4096,256]{1,0:T(8,128)(2,1)}) custom-call(f32[2]{0:T(128)} %exponential_multiply_fusion.slope_ref, bf16[512,2048]{1,0:T(8,128)(2,1)} %cotangent_hbm.1, bf16[4096,2048]{1,0:T(8,128)(2,1)} %gather_rows.1.rows_hbm, ...), custom_call_target="tpu_custom_call" | custom-call | bytes 280000000 | tf_op jit(solution)/shard_map/project_attend/pallas_call | solution.py:580
  180.9 85.4 %dense.1 = (f32[512,2048]{1,0:T(8,128)}, bf16[512,2048]{1,0:T(8,128)(2,1)}) custom-call(bf16[4096,256]{1,0:T(8,128)(2,1)} %get-tuple-element.40.a_hbm.mixed_ref, bf16[256,2048]{1,0:T(8,128)(2,1)} %all-gather.7.cloned.1.call-done.w_ref, bf16[512,2048]{1,0:T(8,128)(2,1)} %input_hbm.3, f32[1,2048]{1,0:T(1,128)} %bitcast.26, f32[1,2048]{1,0:T(1,128)} %bitcast.22, ...), custom_call_target="tpu_custom_call" | custom-call | bytes 280000000 | tf_op jit(solution)/shard_map/dense/pallas_call | solution.py:928
  266.4 92.6 %expand.1 = (bf16[4096,2048]{1,0:T(8,128)(2,1)}, bf16[4096,1024]{1,0:T(8,128)(2,1)}, bf16[4096,1024]{1,0:T(8,128)(2,1)}, f32[1,1024]{1,0:T(1,128)}) custom-call(bf16[512,2048]{1,0:T(8,128)(2,1)} %get-tuple-element.41.own_ref, bf16[4096,2048]{1,0:T(8,128)(2,1)} %get-tuple-element.42.grad_hbm.rows_hbm, ...), custom_call_target="tpu_custom_call" | custom-call | bytes 280000000 | tf_op jit(solution)/shard_map/expand/pallas_call | solution.py:702
  359.0 99.2 %expand_back.1 = (f32[512,2048]{1,0:T(8,128)}, bf16[512,2048]{1,0:T(8,128)(2,1)}, f32[8,2048]{1,0:T(8,128)}, bf16[1024,2048]{1,0:T(8,128)(2,1)}) custom-call(bf16[4096,1024]{1,0:T(8,128)(2,1)} %get-tuple-element.43.a_hbm.right_hbm, bf16[2048,1024]{1,0:T(8,128)(2,1)} %all-gather.9.cloned.1.call-done.up_ref.w_ref, ...), custom_call_target="tpu_custom_call" | custom-call | bytes 280000000 | tf_op jit(solution)/shard_map/expand_back/pallas_call | solution.py:947
  458.2 78.1 %dense_back.1 = (bf16[4096,256]{1,0:T(8,128)(2,1)}, bf16[256,2048]{1,0:T(8,128)(2,1)}, bf16[2048,1024]{1,0:T(8,128)(2,1)}) custom-call(bf16[512,2048]{1,0:T(8,128)(2,1)} %get-tuple-element.47.own_ref, bf16[4096,256]{1,0:T(8,128)(2,1)} %get-tuple-element.40.a_hbm.mixed_ref, bf16[256,2048]{1,0:T(8,128)(2,1)} %all-gather.7.cloned.1.call-done.w_ref, ...), custom_call_target="tpu_custom_call" | custom-call | bytes 280000000 | tf_op jit(solution)/shard_map/dense_back/pallas_call | solution.py:1014
  536.4 0.7 reduce-scatter.11.cloned.1.call-update
  537.8 2.8 convert_element_type.44
  540.6 96.2 %shrink.1 = (bf16[512,2048]{1,0:T(8,128)(2,1)}, bf16[4096,768]{1,0:T(8,128)(2,1)}, f32[8,256]{1,0:T(8,128)}) custom-call(f32[2]{0:T(128)} %exponential_multiply_fusion.slope_ref, bf16[4096,1024]{1,0:T(8,128)(2,1)} %get-tuple-element.50.act_hbm.a_hbm, bf16[1024,2048]{1,0:T(8,128)(2,1)} %all-gather.11.cloned.1.call-done.down_ref.w_ref, ...), custom_call_target="tpu_custom_call" | custom-call | bytes 280000000 | tf_op jit(solution)/shard_map/shrink/pallas_call | solution.py:1120
  636.8 20.3 %convolution_convert_fusion = bf16[2048,768]{1,0:T(8,128)(2,1)} fusion(bf16[4096,2048]{1,0:T(8,128)(2,1)} %gather_rows.1.rows_hbm, bf16[4096,768]{1,0:T(8,128)(2,1)} %get-tuple-element.54.a_hbm), kind=kOutput, calls=%fused_computation.8 | convolution fusion | flops 12886474752 | bytes 26214400 | tf_op jit(solution)/shard_map/td,tc->dc/dot_general | solution.py:1322
  657.2 1.8 convert_element_type.47
  659.0 104.1 %project_back.1 = (f32[512,2048]{1,0:T(8,128)}, f32[8,2048]{1,0:T(8,128)}, f32[8,1024]{1,0:T(8,128)}) custom-call(bf16[4096,768]{1,0:T(8,128)(2,1)} %get-tuple-element.54.a_hbm, bf16[2048,768]{1,0:T(8,128)(2,1)} %all-gather.5.cloned.1.call-done.w_ref, bf16[512,2048]{1,0:T(8,128)(2,1)} %input_hbm.3, f32[512,2048]{1,0:T(8,128)} %get-tuple-element.55.grad_hbm, ...), custom_call_target="tpu_custom_call" | custom-call | bytes 280000000 | tf_op jit(solution)/shard_map/project_back/pallas_call | solution.py:1215
  763.2 1.5 slice.34
  764.7 2.8 convert_element_type.48
  767.5 1.3 fusion.8
  768.8 1.7 fusion.7
  770.5 2.5 convert_element_type.46
  773.1 1.3 copy.35
  774.4 2.0 copy.36
  (67 shorter events, 9.3 us)
Async XLA Ops:
  7.2 4.2 copy-start
  7.2 94.1 %all-gather.5.cloned.1.call-start = ((), (), s32[]{:S(2)}) async-start(), calls=%async_computation.4 | async-start | bytes 3932160 | tf_op jit(solution)/shard_map/all_gather | solution.py:1283
  7.9 172.9 %all-gather.7.cloned.1.call-start = ((), (), s32[]{:S(2)}) async-start(), calls=%async_computation.5 | async-start | bytes 1310720 | tf_op jit(solution)/shard_map/all_gather | solution.py:1284
  8.7 257.7 %all-gather.11.cloned.1.call-start = ((), (), s32[]{:S(2)}) async-start(), calls=%async_computation.7 | async-start | bytes 5242880 | tf_op jit(solution)/shard_map/all_gather | solution.py:1286
  9.4 257.0 %all-gather.9.cloned.1.call-start = ((), (), s32[]{:S(2)}) async-start(), calls=%async_computation.6 | async-start | bytes 5242880 | tf_op jit(solution)/shard_map/all_gather | solution.py:1285
  10.0 527.8 %reduce-scatter.5.cloned.1.call-start = ((), (), s32[]{:S(2)}) async-start(), calls=%async_computation.8 | async-start | bytes 5242880 | tf_op jit(solution)/shard_map/reduce_scatter | solution.py:1253
  10.7 3.9 copy-start.3
  14.6 78.6 %copy-start.4 = (s32[4096]{0:T(1024)S(1)}, s32[4096]{0:T(1024)}, u32[]{:S(2)}) copy-start(s32[4096]{0:T(1024)} %param.31) | copy-start | bytes 49156
  14.6 80.5 %copy-start.11 = (bf16[256]{0:T(256)(128)(2,1)S(1)}, bf16[256]{0:T(256)(128)(2,1)}, u32[]{:S(2)}) copy-start(bf16[256]{0:T(256)(128)(2,1)} %param.21) | copy-start | bytes 1540
  14.7 80.5 %copy-start.12 = (bf16[256]{0:T(256)(128)(2,1)S(1)}, bf16[256]{0:T(256)(128)(2,1)}, u32[]{:S(2)}) copy-start(bf16[256]{0:T(256)(128)(2,1)} %param.22) | copy-start | bytes 1540
  14.7 81.3 %copy-start.5 = (bf16[2048]{0:T(1024)(128)(2,1)S(1)}, bf16[2048]{0:T(1024)(128)(2,1)}, u32[]{:S(2)}) copy-start(bf16[2048]{0:T(1024)(128)(2,1)} %param.25) | copy-start | bytes 12292
  14.7 81.9 %copy-start.6 = (bf16[2048]{0:T(1024)(128)(2,1)S(1)}, bf16[2048]{0:T(1024)(128)(2,1)}, u32[]{:S(2)}) copy-start(bf16[2048]{0:T(1024)(128)(2,1)} %param.24) | copy-start | bytes 12292
  14.7 82.5 %copy-start.7 = (bf16[2048]{0:T(1024)(128)(2,1)S(1)}, bf16[2048]{0:T(1024)(128)(2,1)}, u32[]{:S(2)}) copy-start(bf16[2048]{0:T(1024)(128)(2,1)} %param.26) | copy-start | bytes 12292
  14.7 83.1 %copy-start.9 = (bf16[1024]{0:T(1024)(128)(2,1)S(1)}, bf16[1024]{0:T(1024)(128)(2,1)}, u32[]{:S(2)}) copy-start(bf16[1024]{0:T(1024)(128)(2,1)} %param.28) | copy-start | bytes 6148
  14.7 83.7 %copy-start.10 = (s32[4,18]{1,0:T(4,128)S(1)}, s32[4,18]{1,0:T(4,128)}, u32[]{:S(2)}) copy-start(s32[4,18]{1,0:T(4,128)} %param.32) | copy-start | bytes 868
  458.2 199.0 %reduce-scatter.9.cloned.1.call-start = ((), (), s32[]{:S(2)}) async-start(), calls=%async_computation.10 | async-start | bytes 1310720 | tf_op jit(solution)/shard_map/reduce_scatter | solution.py:1253
  536.3 0.8 copy-start.8
  536.4 228.3 %reduce-scatter.11.cloned.1.call-start = ((), (), s32[]{:S(2)}) async-start(), calls=%async_computation.11 | async-start | bytes 5242880 | tf_op jit(solution)/shard_map/reduce_scatter | solution.py:1253
  537.1 233.4 %reduce-scatter.7.cloned.1.call-start = ((), (), s32[]{:S(2)}) async-start(), calls=%async_computation.9 | async-start | bytes 3932160 | tf_op jit(solution)/shard_map/reduce_scatter | solution.py:1253
  763.2 9.9 %copy-start.2 = (bf16[512,2048]{1,0:T(8,128)(2,1)S(1)}, bf16[512,2048]{1,0:T(8,128)(2,1)}, u32[]{:S(2)}) copy-start(bf16[512,2048]{1,0:T(8,128)(2,1)} %get-tuple-element.88) | copy-start | bytes 6291460
  770.5 3.9 copy-start.1
Sparse Core Ops, SparseCore 0:
  9.6 66.1 all-gather.4
  77.3 26.6 all-gather.6
  105.6 80.1 all-gather.10
  187.1 79.2 all-gather.8
  458.3 76.0 reduce-scatter.4
  536.5 27.8 reduce-scatter.8
  566.7 75.2 reduce-scatter.10
  657.3 62.1 reduce-scatter.6

commit v5 on v4

--- a/solution.py
+++ b/solution.py
@@ -329,7 +329,7 @@
             if step + 1 < self.bits:
                 self.chip_copy(j, part, step + 1).start()
 
-    def run(self, filler=None, d=1):
+    def run(self, filler=None, after=None, d=1):
         for copy in self.loads(0, 1):
             copy.start()
         greet(self.me, self.bits, d)
@@ -361,6 +361,13 @@
                 @pl.when((u >= 1) & (u <= self.chunks))
                 def _():
                     filler(u - 1)
+
+            if after is not None:
+                done = u - self.bits - 1
+
+                @pl.when(done >= 0)
+                def _():
+                    after(done)
 
             return carry
 
@@ -784,7 +791,7 @@
 
         k = lax.rem(i, self.inner)
         slot = lax.rem(i, 2)
-        part = min(self.wide, 512)
+        part = next(size for size in (512, 384, self.wide) if self.wide % size == 0)
 
         @pl.when(k == 0)
         def _():
@@ -833,12 +840,24 @@
     ]
 
 
-def row_blocks(rows, each, work):
+def row_blocks(first, rows, each, work):
     def one(i, carry):
-        work(pl.ds(pl.multiple_of(i * each, each), each))
+        work(pl.ds(pl.multiple_of(first + i * each, each), each))
         return carry
 
     lax.fori_loop(0, rows // each, one, 0)
+
+
+def after_chunk(scatter, fetches, work):
+    def after(j):
+        @pl.when(j == 0)
+        def _():
+            for fetch in fetches:
+                fetch.wait()
+
+        row_blocks(j * scatter.chunk, scatter.chunk, 32, work)
+
+    return after
 
 
 def normal_rows(value):
@@ -852,8 +871,7 @@
 ):
     fetch = pltpu.make_async_copy(input_hbm, inputs, input_sem)
     fetch.start()
-    Scatter(n, False, a_hbm, w_ref, out_ref, scratch).run()
-    fetch.wait()
+    scatter = Scatter(n, False, a_hbm, w_ref, out_ref, scratch)
 
     def work(at):
         residual = inputs[at, :].astype(jnp.float32) + out_ref[at, :] + bias_ref[...]
@@ -861,7 +879,7 @@
         normed, _ = normal_rows(residual)
         next_ref[at, :] = (normed * gain_ref[...] + shift_ref[...]).astype(next_ref.dtype)
 
-    row_blocks(out_ref.shape[0], 32, work)
+    scatter.run(after=after_chunk(scatter, (fetch,), work))
 
 
 def back_rows(grad, source, gain):
@@ -893,10 +911,6 @@
     product = Product(act_hbm, rows_hbm, grad_hbm, scratch[:7])
     scatter = Scatter(n, True, a_hbm, w_ref, out_ref, scratch[7:])
     product.start()
-    scatter.run(lambda j: product.batch(j, scatter.chunks))
-    product.finish()
-    for fetch in fetches:
-        fetch.wait()
     sums_ref[...] = jnp.zeros_like(sums_ref)
 
     def work(at):
@@ -911,7 +925,8 @@
         sums_ref[2:3, :] += column_sum(result)
         sums_ref[3:4, :] += column_sum(other)
 
-    row_blocks(out_ref.shape[0], 32, work)
+    scatter.run(lambda j: product.batch(j, scatter.chunks), after_chunk(scatter, fetches, work))
+    product.finish()
 
 
 def comm_params(collective_id):
@@ -965,68 +980,6 @@
         cost_estimate=LINK_COST,
         name="expand_back",
     )(grad_pre, up, activated, grad_rows, residual, cotangent, gain)
-
-
-def dense_back_kernel(
-    n, own_ref, mixed_ref, w_ref, left_hbm, right_hbm, grad_mixed_ref, grad_dense_ref, grad_up_hbm, gathered, acc, *scratch
-):
-    product = Product(left_hbm, right_hbm, grad_up_hbm, scratch[:7])
-    gather = Gather(n, own_ref, gathered, scratch[7:])
-    rows = own_ref.shape[0]
-
-    def work(at):
-        span = pl.ds(pl.multiple_of(at * rows, rows), rows)
-        grad_mixed_ref[span, :] = lax.dot_general(
-            gathered[span, :], w_ref[...], NT, preferred_element_type=jnp.float32
-        ).astype(grad_mixed_ref.dtype)
-        width = acc.shape[1]
-        part = min(width, 512)
-        for first in range(0, width, part):
-            cols = slice(first, first + part)
-            acc[:, cols] += lax.dot_general(
-                mixed_ref[span, :], gathered[span, cols], TN, preferred_element_type=jnp.float32
-            )
-
-    product.start()
-    gather.start()
-    acc[...] = jnp.zeros_like(acc)
-    product.batch(0, 1)
-    for count in range(1, gather.bits + 1):
-        gather.forward(count)
-        if count == 1:
-            gather.keep().wait()
-            work(gather.place(0, 0))
-            gather.wait_core(0)
-            work(gather.place(0, 1))
-        for core in (0, 1):
-            for mask in gather.level(count):
-                if core:
-                    gather.wait_core(mask)
-                work(gather.place(mask, core))
-    grad_dense_ref[...] = acc[...].astype(grad_dense_ref.dtype)
-    product.finish()
-    gather.finish_sends()
-
-
-def dense_back(own, mixed, weight, mlp_rows, grad_pre, n, collective_id):
-    rows, width = own.shape
-    total, depth = mixed.shape
-    return pl.pallas_call(
-        functools.partial(dense_back_kernel, n),
-        out_shape=(
-            jax.ShapeDtypeStruct((total, depth), jnp.bfloat16),
-            jax.ShapeDtypeStruct((depth, width), jnp.bfloat16),
-            jax.ShapeDtypeStruct((mlp_rows.shape[1], grad_pre.shape[1]), jnp.bfloat16),
-        ),
-        in_specs=[VMEM_SPEC, VMEM_SPEC, VMEM_SPEC, HBM_SPEC, HBM_SPEC],
-        out_specs=(VMEM_SPEC, VMEM_SPEC, HBM_SPEC),
-        scratch_shapes=[pltpu.VMEM((total, width), jnp.bfloat16), pltpu.VMEM((depth, width), jnp.float32)]
-        + product_scratch(total, mlp_rows.shape[1], grad_pre.shape[1])
-        + gather_sems(n),
-        compiler_params=comm_params(collective_id),
-        cost_estimate=LINK_COST,
-        name="dense_back",
-    )(own, mixed, weight, mlp_rows, grad_pre)
 
 
 def attend_back_one(slope, proj_ref, grad_ref, start, head, column_ref, row_ref, out_ref, dk_ref, dv_ref, sums_ref, length):
@@ -1073,98 +1026,119 @@
     sums_ref[1:2, own] += column_sum(grad_values.astype(jnp.float32))
 
 
-def shrink_kernel(
-    n, length, slope_ref, a_hbm, w_ref, residual_hbm, bias_ref, proj_hbm, grad_mixed_ref, column_ref, row_ref,
-    hidden_ref, grad_proj_ref, sums_ref, out, residual, proj, dk, dv, fetch_sem, *scratch
+def dense_back_kernel(
+    n, length, slope_ref, own_ref, mixed_ref, w_ref, left_hbm, right_hbm, proj_hbm, column_ref, row_ref,
+    grad_proj_ref, sums_ref, grad_dense_ref, grad_up_hbm, gathered, acc, grad_mixed, proj, dk, dv, fetch_sem, *scratch
 ):
-    fetches = (
-        pltpu.make_async_copy(proj_hbm, proj, fetch_sem.at[0]),
-        pltpu.make_async_copy(residual_hbm, residual, fetch_sem.at[1]),
-    )
-    for fetch in fetches:
-        fetch.start()
-    scatter = Scatter(n, False, a_hbm, w_ref, out, scratch)
-    heads = grad_proj_ref.shape[1] // (3 * HEAD_DIM)
-    units = grad_proj_ref.shape[0] // length * heads
-    per = -(-units // scatter.chunks)
+    fetch = pltpu.make_async_copy(proj_hbm, proj, fetch_sem)
+    fetch.start()
+    product = Product(left_hbm, right_hbm, grad_up_hbm, scratch[:7])
+    gather = Gather(n, own_ref, gathered, scratch[7:])
+    rows = own_ref.shape[0]
+    heads = sums_ref.shape[1] // HEAD_DIM
+    chips = max(1, length // (2 * rows))
+    sequences = max(1, 2 * rows // length)
+
+    def work(at):
+        span = pl.ds(pl.multiple_of(at * rows, rows), rows)
+        grad_mixed[span, :] = lax.dot_general(
+            gathered[span, :], w_ref[...], NT, preferred_element_type=jnp.float32
+        ).astype(grad_mixed.dtype)
+        width = acc.shape[1]
+        part = min(width, 512)
+        for first in range(0, width, part):
+            cols = slice(first, first + part)
+            acc[:, cols] += lax.dot_general(
+                mixed_ref[span, :], gathered[span, cols], TN, preferred_element_type=jnp.float32
+            )
+
+    def attend(mask):
+        first = (gather.place(mask, 0) // 2 // chips) * sequences
+
+        def one(i, carry):
+            s, head = first + i // heads, lax.rem(i, heads)
+            attend_back_one(
+                slope_ref[head], proj, grad_mixed, pl.multiple_of(s * length, length), head, column_ref.at[s],
+                row_ref.at[s], grad_proj_ref, dk, dv, sums_ref, length,
+            )
+            return carry
+
+        lax.fori_loop(0, sequences * heads, one, 0)
+
+    arrived = {}
+
+    def pair(mask):
+        if mask == 0:
+            gather.keep().wait()
+        work(gather.place(mask, 0))
+        gather.wait_core(mask)
+        work(gather.place(mask, 1))
+        group = arrived.setdefault(mask // chips, [])
+        group.append(mask)
+        if len(group) == chips:
+            attend(mask)
+
+    product.start()
+    gather.start()
+    acc[...] = jnp.zeros_like(acc)
     sums_ref[...] = jnp.zeros_like(sums_ref)
-
-    def one(i, carry):
-        s, head = i // heads, lax.rem(i, heads)
-        attend_back_one(
-            slope_ref[head], proj, grad_mixed_ref, pl.multiple_of(s * length, length), head, column_ref.at[s],
-            row_ref.at[s], grad_proj_ref, dk, dv, sums_ref, length,
-        )
-        return carry
-
-    def filler(j):
-        @pl.when(j == 0)
-        def _():
-            fetches[0].wait()
-
-        lax.fori_loop(j * per, jnp.minimum(j * per + per, units), one, 0)
-
-    scatter.run(filler)
-    fetches[1].wait()
-
-    def work(at):
-        hidden_ref[at, :] = (residual[at, :] + out[at, :] + bias_ref[...]).astype(hidden_ref.dtype)
-
-    row_blocks(out.shape[0], 64, work)
-
-
-def shrink(activated, down, residual, bias, slopes, proj, grad_mixed, labels, n, collective_id):
-    rows, width = residual.shape
-    heads_width = grad_mixed.shape[1]
+    product.batch(0, 1)
+    fetch.wait()
+    pair(0)
+    for count in range(1, gather.bits + 1):
+        gather.forward(count)
+        for mask in gather.level(count):
+            pair(mask)
+    grad_dense_ref[...] = acc[...].astype(grad_dense_ref.dtype)
+    product.finish()
+    gather.finish_sends()
+
+
+def dense_back(own, mixed, weight, mlp_rows, grad_pre, proj, slopes, labels, n, collective_id):
+    rows, width = own.shape
+    total, depth = mixed.shape
     length = labels.shape[1]
     return pl.pallas_call(
-        functools.partial(shrink_kernel, n, length),
+        functools.partial(dense_back_kernel, n, length),
         out_shape=(
-            jax.ShapeDtypeStruct((rows, width), jnp.bfloat16),
             jax.ShapeDtypeStruct(proj.shape, jnp.bfloat16),
-            jax.ShapeDtypeStruct((8, heads_width), jnp.float32),
+            jax.ShapeDtypeStruct((8, depth), jnp.float32),
+            jax.ShapeDtypeStruct((depth, width), jnp.bfloat16),
+            jax.ShapeDtypeStruct((mlp_rows.shape[1], grad_pre.shape[1]), jnp.bfloat16),
         ),
-        in_specs=[
-            pl.BlockSpec(memory_space=pltpu.SMEM), HBM_SPEC, VMEM_SPEC, HBM_SPEC, VMEM_SPEC, HBM_SPEC, VMEM_SPEC, VMEM_SPEC,
-            VMEM_SPEC,
-        ],
-        out_specs=(VMEM_SPEC, VMEM_SPEC, VMEM_SPEC),
+        in_specs=[pl.BlockSpec(memory_space=pltpu.SMEM), VMEM_SPEC, VMEM_SPEC, VMEM_SPEC]
+        + [HBM_SPEC] * 3
+        + [VMEM_SPEC] * 2,
+        out_specs=(VMEM_SPEC, VMEM_SPEC, VMEM_SPEC, HBM_SPEC),
         scratch_shapes=[
-            pltpu.VMEM((rows, width), jnp.float32),
-            pltpu.VMEM((rows, width), jnp.float32),
+            pltpu.VMEM((total, width), jnp.bfloat16),
+            pltpu.VMEM((depth, width), jnp.float32),
+            pltpu.VMEM((total, depth), jnp.bfloat16),
             pltpu.VMEM(proj.shape, jnp.bfloat16),
             pltpu.VMEM((length, HEAD_DIM), jnp.float32),
             pltpu.VMEM((length, HEAD_DIM), jnp.float32),
-            pltpu.SemaphoreType.DMA((2,)),
+            pltpu.SemaphoreType.DMA(()),
         ]
-        + scatter_scratch(n, rows, activated.shape[1], width, CHUNKS),
+        + product_scratch(total, mlp_rows.shape[1], grad_pre.shape[1])
+        + gather_sems(n),
         compiler_params=comm_params(collective_id),
         cost_estimate=LINK_COST,
-        name="shrink",
-    )(slopes, activated, down, residual, bias, proj, grad_mixed, labels[:, :, None], labels[:, None, :])
-
-
-def project_back_kernel(
-    n, d, a_hbm, w_ref, input_hbm, grad_hbm, gain_ref, early_ref, up_sum_ref, head_sums_ref,
-    out_ref, sums_ref, biases_ref, inputs, grads, fetch_sem, *scratch
+        name="dense_back",
+    )(slopes, own, mixed, weight, mlp_rows, grad_pre, proj, labels[:, :, None], labels[:, None, :])
+
+
+def shrink_kernel(
+    n, d, a_hbm, w_ref, residual_hbm, bias_ref, early_ref, up_sum_ref, head_sums_ref,
+    hidden_ref, sums_ref, biases_ref, out, residual, fetch_sem, *scratch
 ):
-    fetches = (
-        pltpu.make_async_copy(input_hbm, inputs, fetch_sem.at[0]),
-        pltpu.make_async_copy(grad_hbm, grads, fetch_sem.at[1]),
-    )
-    for fetch in fetches:
-        fetch.start()
-    early, biases, late = (Total(n, d, scratch[6 * i : 6 * i + 6]) for i in range(3))
-    scatter = Scatter(n, True, a_hbm, w_ref, out_ref, scratch[18:])
-    model = out_ref.shape[1]
-    half, quarter = model // 2, model // 4
+    fetch = pltpu.make_async_copy(residual_hbm, residual, fetch_sem)
+    fetch.start()
+    flat, biases = Total(n, d, scratch[:6]), Total(n, d, scratch[6:12])
+    scatter = Scatter(n, False, a_hbm, w_ref, out, scratch[12:])
     heads_width = head_sums_ref.shape[1]
 
-    def pack(i, width):
-        return [(i * (model // width) + k, slice(k * width, (k + 1) * width)) for k in range(model // width)]
-
     def filler(j):
-        for level in range(min(early.levels + 1, scatter.chunks)):
+        for level in range(min(flat.levels + 1, scatter.chunks)):
 
             @pl.when(j == level)
             def _():
@@ -1173,67 +1147,94 @@
                     biases.lines[0, 0:1, :] = up_sum_ref[...]
                     biases.lines[0, 1:3, :heads_width] = head_sums_ref[0:2, :]
                     biases.spread()
-                    for i in range(4):
-                        for row, cols in pack(i, half):
-                            early.pair[0, row : row + 1, :] = early_ref[i : i + 1, cols]
-                early.step(level)
-
-    scatter.run(filler, d)
-    for level in range(scatter.chunks, early.levels + 1):
-        early.step(level)
+                    flat.pair[0] = early_ref[...]
+                flat.step(level)
+
+    def work(at):
+        hidden_ref[at, :] = (residual[at, :] + out[at, :] + bias_ref[...]).astype(hidden_ref.dtype)
+
+    scatter.run(filler, after_chunk(scatter, (fetch,), work), d)
+    for level in range(scatter.chunks, flat.levels + 1):
+        flat.step(level)
+    biases_ref[...] = biases.finish(False)
+    sums_ref[...] = flat.finish()
+
+
+def shrink(activated, down, residual, bias, sums, up_sum, head_sums, n, d, collective_id):
+    rows, width = residual.shape
+    units = up_sum.shape[1]
+    return pl.pallas_call(
+        functools.partial(shrink_kernel, n, d),
+        out_shape=(
+            jax.ShapeDtypeStruct((rows, width), jnp.bfloat16),
+            jax.ShapeDtypeStruct((8, width), jnp.float32),
+            jax.ShapeDtypeStruct((8, units), jnp.float32),
+        ),
+        in_specs=[HBM_SPEC, VMEM_SPEC, HBM_SPEC] + [VMEM_SPEC] * 4,
+        out_specs=(VMEM_SPEC, VMEM_SPEC, VMEM_SPEC),
+        scratch_shapes=[
+            pltpu.VMEM((rows, width), jnp.float32),
+            pltpu.VMEM((rows, width), jnp.float32),
+            pltpu.SemaphoreType.DMA(()),
+        ]
+        + total_scratch(n, d, 8, width)
+        + total_scratch(n, d, 8, units)
+        + scatter_scratch(n, rows, activated.shape[1], width, CHUNKS),
+        compiler_params=comm_params(collective_id),
+        cost_estimate=LINK_COST,
+        name="shrink",
+    )(activated, down, residual, bias, sums, up_sum, head_sums)
+
+
+def project_back_kernel(
+    n, a_hbm, w_ref, input_hbm, grad_hbm, gain_ref, early_ref, left_hbm,
+    out_ref, sums_ref, weight_hbm, inputs, grads, fetch_sem, *scratch
+):
+    fetches = (
+        pltpu.make_async_copy(input_hbm, inputs, fetch_sem.at[0]),
+        pltpu.make_async_copy(grad_hbm, grads, fetch_sem.at[1]),
+    )
     for fetch in fetches:
-        fetch.wait()
-    late.pair[0] = jnp.zeros(late.pair.shape[1:], jnp.float32)
+        fetch.start()
+    product = Product(left_hbm, a_hbm, weight_hbm, scratch[:7])
+    scatter = Scatter(n, True, a_hbm, w_ref, out_ref, scratch[7:])
+    product.start()
+    sums_ref[...] = early_ref[...]
 
     def work(at):
         grad = out_ref[at, :]
         back, terms = back_rows(grad, inputs[at, :].astype(jnp.float32), gain_ref[...])
         out_ref[at, :] = grads[at, :] + back
-        for i, value in enumerate((column_sum(terms), column_sum(grad))):
-            for row, cols in pack(i, quarter):
-                late.pair[0, row : row + 1, :] += value[:, cols]
-
-    row_blocks(out_ref.shape[0], 32, work)
-    late.step(0)
-    biases_ref[...] = biases.finish(False)
-    total = early.finish()
-    for i in range(4):
-        for row, cols in pack(i, half):
-            sums_ref[i : i + 1, cols] = total[row : row + 1, :]
-    for level in range(1, late.levels + 1):
-        late.step(level)
-    total = late.finish()
-    for i in range(2):
-        for row, cols in pack(i, quarter):
-            sums_ref[4 + i : 5 + i, cols] = total[row : row + 1, :]
-    sums_ref[6:8, :] = jnp.zeros((2, model), jnp.float32)
-
-
-def project_back(grad_proj, weight, inputs, grad_residual, gain, early, up_sum, head_sums, n, d, collective_id):
+        sums_ref[4:5, :] += column_sum(terms)
+        sums_ref[5:6, :] += column_sum(grad)
+
+    scatter.run(lambda j: product.batch(j, scatter.chunks), after_chunk(scatter, fetches, work))
+    product.finish()
+
+
+def project_back(grad_proj, weight, inputs, grad_residual, gain, early, attn_rows, n, collective_id):
     rows, width = inputs.shape
-    units = up_sum.shape[1]
+    columns = grad_proj.shape[1]
     return pl.pallas_call(
-        functools.partial(project_back_kernel, n, d),
+        functools.partial(project_back_kernel, n),
         out_shape=(
             jax.ShapeDtypeStruct((rows, width), jnp.float32),
             jax.ShapeDtypeStruct((8, width), jnp.float32),
-            jax.ShapeDtypeStruct((8, units), jnp.float32),
+            jax.ShapeDtypeStruct((width, columns), jnp.bfloat16),
         ),
-        in_specs=[HBM_SPEC, VMEM_SPEC, HBM_SPEC, HBM_SPEC] + [VMEM_SPEC] * 4,
-        out_specs=(VMEM_SPEC, VMEM_SPEC, VMEM_SPEC),
+        in_specs=[HBM_SPEC, VMEM_SPEC, HBM_SPEC, HBM_SPEC, VMEM_SPEC, VMEM_SPEC, HBM_SPEC],
+        out_specs=(VMEM_SPEC, VMEM_SPEC, HBM_SPEC),
         scratch_shapes=[
             pltpu.VMEM((rows, width), inputs.dtype),
             pltpu.VMEM((rows, width), jnp.float32),
             pltpu.SemaphoreType.DMA((2,)),
         ]
-        + total_scratch(n, d, 8, width // 2)
-        + total_scratch(n, d, 8, units)
-        + total_scratch(n, d, 8, width // 4)
-        + scatter_scratch(n, rows, grad_proj.shape[1], width, CHUNKS),
+        + product_scratch(n * rows, width, columns)
+        + scatter_scratch(n, rows, columns, width, CHUNKS),
         compiler_params=comm_params(collective_id),
         cost_estimate=LINK_COST,
         name="project_back",
-    )(grad_proj, weight, inputs, grad_residual, gain, early, up_sum, head_sums)
+    )(grad_proj, weight, inputs, grad_residual, gain, early, attn_rows)
 
 
 HEADS = 16
@@ -1313,19 +1314,18 @@
         grad_pre, expand_full, activated, grad_rows, residual, cotangent, wide(second_gain), n, 4
     )
     grad_down_weight = share(grad_down, 1)
-    grad_mixed, grad_dense, grad_up = dense_back(grad_attn_out, mixed, dense_full, mlp_rows, grad_pre, n, 9)
-    grad_down_weight, activated, grad_mixed = lax.optimization_barrier((grad_down_weight, activated, grad_mixed))
+    grad_proj, head_sums, grad_dense, grad_up = dense_back(
+        grad_attn_out, mixed, dense_full, mlp_rows, grad_pre, proj, slopes, labels, n, 9
+    )
+    grad_down_weight, grad_proj = lax.optimization_barrier((grad_down_weight, grad_proj))
     grad_up_weight = share(grad_up, 0)
-    hidden_output, grad_proj, head_sums = shrink(
-        activated, shrink_full, residual, wide(down_bias), slopes, proj, grad_mixed, labels, n, 3
-    )
-    grad_project = jnp.einsum("td,tc->dc", attn_rows, grad_proj, preferred_element_type=jnp.float32).astype(
-        jnp.bfloat16
+    grad_dense_weight = share(grad_dense, 1)
+    grad_input, sums, grad_project = project_back(
+        grad_proj, project_full, hidden_input, grad_residual, wide(first_gain), early_sums, attn_rows, n, 5
     )
     grad_qkv_weight = share(grad_project, 0)
-    grad_dense_weight = share(grad_dense, 1)
-    grad_input, sums, biases = project_back(
-        grad_proj, project_full, hidden_input, grad_residual, wide(first_gain), early_sums, sum_up_bias, head_sums, n, d, 5
+    hidden_output, sums, biases = shrink(
+        activated, shrink_full, residual, wide(down_bias), sums, sum_up_bias, head_sums, n, d, 3
     )
     heads_width = heads_local * HEAD_DIM
     grad_second_gain, grad_second_shift, grad_dense_bias, grad_down_bias, grad_first_gain, grad_first_shift = (

time: 788 us -> 752 us (0.954)
  matrix products: 20.3 us -> 0 us
  Pallas kernels: 714 us -> 695 us
    dot_general x1 -> x0, matrix products: 20.3 us -> none  [on_device(): jnp.einsum('td,tc->dc', attn_rows, grad_proj, preferred_element_type=jnp....]
    pallas_call x3, Pallas kernels: 278 us -> 268 us  [the longest x1 90.5 us: project_back(): pl.pallas_call(functools.partial(project_back_kernel, n), out_shape=(jax....]
  transfers between devices with their start and end apart: 8 -> 8, of which waited for: 1 -> 1; matrix products, arithmetic and copies ran while one was open for 6% -> 3% of each run, Pallas kernels for 67% -> 68%
where the time goes in v5:
time: 752 us; the launch traced here: 747 us
  Pallas kernels  695 us (92%)
  other arithmetic  20.5 us (3%)
  between operations  14.6 us (2%)
  local copies, waits for them, and re-layouts  10.6 us (1%)
    pallas_call x1, Pallas kernels, expand_back(): pl.pallas_call(functools.partial(expand_back_kernel, n), out_shape=(jax.S...  94.1 us
    pallas_call x1, Pallas kernels, expand(): pl.pallas_call(functools.partial(expand_kernel, n), out_shape=(jax.ShapeD...  92.5 us
    pallas_call x1, Pallas kernels, project_back(): pl.pallas_call(functools.partial(project_back_kernel, n), out_shape=(jax....  90.5 us
    pallas_call x1, Pallas kernels, dense_back(): pl.pallas_call(functools.partial(dense_back_kernel, n, length), out_shape...  90.2 us
    pallas_call x1, Pallas kernels, shrink(): pl.pallas_call(functools.partial(shrink_kernel, n, d), out_shape=(jax.Sha...  87.1 us
    pallas_call x1, Pallas kernels, dense(): pl.pallas_call(functools.partial(dense_kernel, n), out_shape=(jax.ShapeDt...  82.5 us
    pallas_call x1, Pallas kernels, project_attend(): pl.pallas_call(functools.partial(project_kernel, n, labels.shape[1]), out...  79.6 us
    pallas_call x1, Pallas kernels, gather_rows(): pl.pallas_call(functools.partial(gather_kernel, n), out_shape=jax.ShapeDt...  78.5 us
  transfers between devices with their start and end apart: 8, of which 1 were waited for; matrix products, arithmetic and copies ran while one was open for 3% of the time, Pallas kernels for 68%

profile of v5, /device:TPU:0, one launch (start us, length us, event | category | flops | bytes accessed | tf_op | source)
XLA Modules:
  0.0 747.3 jit_solution(11936624338485162106)
XLA Ops:
  8.0 0.7 all-gather.7.cloned.1.call-update
  10.7 0.7 convert_element_type.39
  12.5 2.2 fusion.5.x_ref
  14.7 78.5 %gather_rows.1.rows_hbm.left_hbm = bf16[4096,2048]{1,0:T(8,128)(2,1)} custom-call(bf16[512,2048]{1,0:T(8,128)(2,1)} %fusion.5.x_ref), custom_call_target="tpu_custom_call" | custom-call | bytes 280000000 | tf_op jit(solution)/shard_map/gather_rows/pallas_call | solution.py:179
  93.2 1.9 reshape.166
  99.7 1.6 fusion.6.column_ref
  101.3 79.6 %project_attend.1 = (bf16[4096,2048]{1,0:T(8,128)(2,1)}, bf16[4096,768]{1,0:T(8,128)(2,1)}, bf16[4096,256]{1,0:T(8,128)(2,1)}) custom-call(f32[2]{0:T(128)} %exponential_multiply_fusion.slope_ref, bf16[512,2048]{1,0:T(8,128)(2,1)} %cotangent_hbm.1, bf16[4096,2048]{1,0:T(8,128)(2,1)} %gather_rows.1.rows_hbm.left_hbm, ...), custom_call_target="tpu_custom_call" | custom-call | bytes 280000000 | tf_op jit(solution)/shard_map/project_attend/pallas_call | solution.py:587
  180.9 82.5 %dense.1 = (f32[512,2048]{1,0:T(8,128)}, bf16[512,2048]{1,0:T(8,128)(2,1)}) custom-call(bf16[4096,256]{1,0:T(8,128)(2,1)} %get-tuple-element.40.a_hbm.mixed_ref, bf16[256,2048]{1,0:T(8,128)(2,1)} %all-gather.7.cloned.1.call-done.w_ref, bf16[512,2048]{1,0:T(8,128)(2,1)} %input_hbm.3, f32[1,2048]{1,0:T(1,128)} %bitcast.23, f32[1,2048]{1,0:T(1,128)} %bitcast.20, ...), custom_call_target="tpu_custom_call" | custom-call | bytes 280000000 | tf_op jit(solution)/shard_map/dense/pallas_call | solution.py:943
  263.4 3.0 all-gather.9.cloned.1.call-done.up_ref.w_ref
  266.4 92.5 %expand.1 = (bf16[4096,2048]{1,0:T(8,128)(2,1)}, bf16[4096,1024]{1,0:T(8,128)(2,1)}, bf16[4096,1024]{1,0:T(8,128)(2,1)}, f32[1,1024]{1,0:T(1,128)}) custom-call(bf16[512,2048]{1,0:T(8,128)(2,1)} %get-tuple-element.41.own_ref, bf16[4096,2048]{1,0:T(8,128)(2,1)} %get-tuple-element.42.grad_hbm.rows_hbm, ...), custom_call_target="tpu_custom_call" | custom-call | bytes 280000000 | tf_op jit(solution)/shard_map/expand/pallas_call | solution.py:709
  359.0 94.1 %expand_back.1 = (f32[512,2048]{1,0:T(8,128)}, bf16[512,2048]{1,0:T(8,128)(2,1)}, f32[8,2048]{1,0:T(8,128)}, bf16[1024,2048]{1,0:T(8,128)(2,1)}) custom-call(bf16[4096,1024]{1,0:T(8,128)(2,1)} %get-tuple-element.45.a_hbm.right_hbm, bf16[2048,1024]{1,0:T(8,128)(2,1)} %all-gather.9.cloned.1.call-done.up_ref.w_ref, ...), custom_call_target="tpu_custom_call" | custom-call | bytes 280000000 | tf_op jit(solution)/shard_map/expand_back/pallas_call | solution.py:962
  453.1 90.2 %dense_back.1 = (bf16[4096,768]{1,0:T(8,128)(2,1)}, f32[8,256]{1,0:T(8,128)}, bf16[256,2048]{1,0:T(8,128)(2,1)}, bf16[2048,1024]{1,0:T(8,128)(2,1)}) custom-call(f32[2]{0:T(128)} %exponential_multiply_fusion.slope_ref, bf16[512,2048]{1,0:T(8,128)(2,1)} %get-tuple-element.47.own_ref, bf16[4096,256]{1,0:T(8,128)(2,1)} %get-tuple-element.40.a_hbm.mixed_ref, ...), custom_call_target="tpu_custom_call" | custom-call | bytes 280000000 | tf_op jit(solution)/shard_map/dense_back/pallas_call | solution.py:1101
  543.3 0.7 reduce-scatter.11.cloned.1.call-update
  544.1 2.8 convert_element_type.41
  547.0 90.5 %project_back.1 = (f32[512,2048]{1,0:T(8,128)}, f32[8,2048]{1,0:T(8,128)}, bf16[2048,768]{1,0:T(8,128)(2,1)}) custom-call(bf16[4096,768]{1,0:T(8,128)(2,1)} %get-tuple-element.51.a_hbm, bf16[2048,768]{1,0:T(8,128)(2,1)} %all-gather.5.cloned.1.call-done.w_ref, bf16[512,2048]{1,0:T(8,128)(2,1)} %input_hbm.3, f32[512,2048]{1,0:T(8,128)} %get-tuple-element.52.grad_hbm, ...), custom_call_target="tpu_custom_call" | custom-call | bytes 280000000 | tf_op jit(solution)/shard_map/project_back/pallas_call | solution.py:1218
  638.1 1.8 convert_element_type.43
  639.9 87.1 %shrink.1 = (bf16[512,2048]{1,0:T(8,128)(2,1)}, f32[8,2048]{1,0:T(8,128)}, f32[8,1024]{1,0:T(8,128)}) custom-call(bf16[4096,1024]{1,0:T(8,128)(2,1)} %get-tuple-element.43.act_hbm.a_hbm, bf16[1024,2048]{1,0:T(8,128)(2,1)} %all-gather.11.cloned.1.call-done.down_ref.w_ref, f32[512,2048]{1,0:T(8,128)} %get-tuple-element.44.residual_hbm, f32[1,2048]{1,0:T(1,128)} %bitcast.25, ...), custom_call_target="tpu_custom_call" | custom-call | bytes 280000000 | tf_op jit(solution)/shard_map/shrink/pallas_call | solution.py:1166
  727.0 1.5 slice.34
  728.5 2.8 convert_element_type.44
  731.3 1.3 fusion.8
  732.6 1.7 fusion.7
  734.4 2.5 convert_element_type.42
  736.9 1.3 copy.35
  738.2 2.0 copy.36
  (66 shorter events, 9.2 us)
Async XLA Ops:
  7.2 4.2 copy-start
  7.2 94.1 %all-gather.5.cloned.1.call-start = ((), (), s32[]{:S(2)}) async-start(), calls=%async_computation.4 | async-start | bytes 3932160 | tf_op jit(solution)/shard_map/all_gather | solution.py:1284
  7.9 172.9 %all-gather.7.cloned.1.call-start = ((), (), s32[]{:S(2)}) async-start(), calls=%async_computation.5 | async-start | bytes 1310720 | tf_op jit(solution)/shard_map/all_gather | solution.py:1285
  8.7 254.7 %all-gather.11.cloned.1.call-start = ((), (), s32[]{:S(2)}) async-start(), calls=%async_computation.7 | async-start | bytes 5242880 | tf_op jit(solution)/shard_map/all_gather | solution.py:1287
  9.4 257.0 %all-gather.9.cloned.1.call-start = ((), (), s32[]{:S(2)}) async-start(), calls=%async_computation.6 | async-start | bytes 5242880 | tf_op jit(solution)/shard_map/all_gather | solution.py:1286
  10.0 534.1 %reduce-scatter.5.cloned.1.call-start = ((), (), s32[]{:S(2)}) async-start(), calls=%async_computation.8 | async-start | bytes 5242880 | tf_op jit(solution)/shard_map/reduce_scatter | solution.py:1254
  10.7 3.9 copy-start.3
  14.6 78.6 %copy-start.4 = (s32[4096]{0:T(1024)S(1)}, s32[4096]{0:T(1024)}, u32[]{:S(2)}) copy-start(s32[4096]{0:T(1024)} %param.31) | copy-start | bytes 49156
  14.6 80.5 %copy-start.11 = (bf16[256]{0:T(256)(128)(2,1)S(1)}, bf16[256]{0:T(256)(128)(2,1)}, u32[]{:S(2)}) copy-start(bf16[256]{0:T(256)(128)(2,1)} %param.21) | copy-start | bytes 1540
  14.7 80.5 %copy-start.12 = (bf16[256]{0:T(256)(128)(2,1)S(1)}, bf16[256]{0:T(256)(128)(2,1)}, u32[]{:S(2)}) copy-start(bf16[256]{0:T(256)(128)(2,1)} %param.22) | copy-start | bytes 1540
  14.7 81.3 %copy-start.5 = (bf16[2048]{0:T(1024)(128)(2,1)S(1)}, bf16[2048]{0:T(1024)(128)(2,1)}, u32[]{:S(2)}) copy-start(bf16[2048]{0:T(1024)(128)(2,1)} %param.25) | copy-start | bytes 12292
  14.7 81.9 %copy-start.6 = (bf16[2048]{0:T(1024)(128)(2,1)S(1)}, bf16[2048]{0:T(1024)(128)(2,1)}, u32[]{:S(2)}) copy-start(bf16[2048]{0:T(1024)(128)(2,1)} %param.24) | copy-start | bytes 12292
  14.7 82.5 %copy-start.7 = (bf16[2048]{0:T(1024)(128)(2,1)S(1)}, bf16[2048]{0:T(1024)(128)(2,1)}, u32[]{:S(2)}) copy-start(bf16[2048]{0:T(1024)(128)(2,1)} %param.26) | copy-start | bytes 12292
  14.7 83.1 %copy-start.9 = (bf16[1024]{0:T(1024)(128)(2,1)S(1)}, bf16[1024]{0:T(1024)(128)(2,1)}, u32[]{:S(2)}) copy-start(bf16[1024]{0:T(1024)(128)(2,1)} %param.28) | copy-start | bytes 6148
  14.7 83.7 %copy-start.10 = (s32[4,18]{1,0:T(4,128)S(1)}, s32[4,18]{1,0:T(4,128)}, u32[]{:S(2)}) copy-start(s32[4,18]{1,0:T(4,128)} %param.32) | copy-start | bytes 868
  453.1 185.0 %reduce-scatter.9.cloned.1.call-start = ((), (), s32[]{:S(2)}) async-start(), calls=%async_computation.10 | async-start | bytes 1310720 | tf_op jit(solution)/shard_map/reduce_scatter | solution.py:1254
  543.3 185.2 %reduce-scatter.11.cloned.1.call-start = ((), (), s32[]{:S(2)}) async-start(), calls=%async_computation.11 | async-start | bytes 5242880 | tf_op jit(solution)/shard_map/reduce_scatter | solution.py:1254
  544.0 190.3 %reduce-scatter.7.cloned.1.call-start = ((), (), s32[]{:S(2)}) async-start(), calls=%async_computation.9 | async-start | bytes 3932160 | tf_op jit(solution)/shard_map/reduce_scatter | solution.py:1254
  547.0 90.5 %copy-start.8 = (bf16[2048]{0:T(1024)(128)(2,1)S(1)}, bf16[2048]{0:T(1024)(128)(2,1)}, u32[]{:S(2)}) copy-start(bf16[2048]{0:T(1024)(128)(2,1)} %param.30) | copy-start | bytes 12292
  727.0 9.9 %copy-start.2 = (bf16[512,2048]{1,0:T(8,128)(2,1)S(1)}, bf16[512,2048]{1,0:T(8,128)(2,1)}, u32[]{:S(2)}) copy-start(bf16[512,2048]{1,0:T(8,128)(2,1)} %get-tuple-element.88) | copy-start | bytes 6291460
  734.4 3.9 copy-start.1
Sparse Core Ops, SparseCore 0:
  9.6 66.1 all-gather.4
  77.3 26.6 all-gather.6
  105.6 80.1 all-gather.10
  187.1 79.2 all-gather.8
  453.2 74.3 reduce-scatter.4
  543.4 24.7 reduce-scatter.8
  570.5 75.2 reduce-scatter.10
  648.2 65.9 reduce-scatter.6

commit v6 on v5

--- a/solution.py
+++ b/solution.py
@@ -14,6 +14,19 @@
 
 def flip(index, bit):
     return index + (1 - 2 * ((index // 2**bit) % 2)) * 2**bit
+
+
+def look_up(table, i):
+    if isinstance(i, int):
+        return table[i]
+    value = table[0]
+    for k in range(1, len(table)):
+        value = value + (i >= k).astype(jnp.int32) * (table[k] - table[k - 1])
+    return value
+
+
+def parity(i):
+    return i % 2 if isinstance(i, int) else lax.rem(i, 2)
 
 
 def chip_bits(n):
@@ -66,7 +79,6 @@
         self.parts = column_parts(width, self.bits)
         self.own, self.out = own_ref, out_ref
         self.own_sem, self.chip_send, self.chip_recv, self.core_send, self.core_recv = sems
-        self.sends = []
 
     def slot(self, part, index):
         at = self.me
@@ -82,6 +94,12 @@
                 at = flip(at, 1 + bit)
         return at
 
+    def away(self, codes, t):
+        code, at = look_up(codes, t), self.me
+        for bit in range(self.bits + 1):
+            at = at + (code // 2**bit) % 2 * (1 - 2 * ((self.me // 2**bit) % 2)) * 2**bit
+        return at
+
     def index_of(self, part, mask):
         return sum(2 ** ((bit - part) % self.bits) for bit in range(self.bits) if (mask >> bit) & 1)
 
@@ -97,28 +115,24 @@
         start, size = self.parts[part]
         return self.own.at[:, pl.ds(start, size)] if index == 0 else self.block(part, index)
 
-    def send(self, part, index, step):
+    def chip_copy(self, part, index, step):
         arrives = index + 2**step
-        copy = remote(
+        return remote(
             self.source(part, index),
             self.block(part, index),
             self.chip_send.at[part, arrives],
             self.chip_recv.at[part, arrives],
             flip(self.me, 1 + (part + step) % self.bits),
         )
-        copy.start()
-        self.sends.append(copy)
-
-    def hand_over(self, part, index):
-        copy = remote(
+
+    def core_copy(self, part, index):
+        return remote(
             self.source(part, index),
             self.block(part, index),
             self.core_send.at[part, index],
             self.core_recv.at[part, index],
             flip(self.me, 0),
         )
-        copy.start()
-        self.sends.append(copy)
 
     def keep(self):
         rows = pl.ds(pl.multiple_of(self.me * self.rows, self.rows), self.rows)
@@ -128,9 +142,9 @@
         greet(self.me, self.bits)
         for step in range(self.bits):
             for part in range(self.bits):
-                self.send(part, 0, step)
+                self.chip_copy(part, 0, step).start()
         for part in range(self.bits):
-            self.hand_over(part, 0)
+            self.core_copy(part, 0).start()
         self.keep().start()
 
     def forward(self, count):
@@ -141,8 +155,8 @@
                     arrived, arrived, self.chip_send.at[part, index], self.chip_recv.at[part, index], flip(self.me, 0)
                 ).wait_recv()
                 for step in range(index.bit_length(), self.bits):
-                    self.send(part, index, step)
-                self.hand_over(part, index)
+                    self.chip_copy(part, index, step).start()
+                self.core_copy(part, index).start()
 
     def wait_core(self, mask):
         for part in range(self.bits):
@@ -153,12 +167,20 @@
             ).wait_recv()
 
     def finish_sends(self):
-        for copy in self.sends:
-            copy.wait_send()
-
-
-def gather_kernel(n, x_ref, out_ref, *sems):
-    gather = Gather(n, x_ref, out_ref, sems)
+        for part in range(self.bits):
+            for index in range(2**self.bits):
+                for step in range(index.bit_length(), self.bits):
+                    self.chip_copy(part, index, step).wait_send()
+                self.core_copy(part, index).wait_send()
+
+
+def gather_kernel(n, x_ref, gain_ref, shift_ref, out_ref, own, *sems):
+    def work(at):
+        normed, _ = normal_rows(x_ref[at, :].astype(jnp.float32))
+        own[at, :] = (normed * gain_ref[...] + shift_ref[...]).astype(own.dtype)
+
+    row_blocks(0, own.shape[0], 32, work)
+    gather = Gather(n, own, out_ref, sems)
     gather.start()
     for count in range(1, gather.bits + 1):
         gather.forward(count)
@@ -174,20 +196,20 @@
     return [dma(())] + [dma((bits, 2**bits))] * 4
 
 
-def gather_rows(x, n, collective_id):
+def gather_rows(x, gain, shift, n, collective_id):
     rows, width = x.shape
     return pl.pallas_call(
         functools.partial(gather_kernel, n),
         out_shape=jax.ShapeDtypeStruct((n * rows, width), x.dtype),
-        in_specs=[pl.BlockSpec(memory_space=pltpu.VMEM)],
+        in_specs=[pl.BlockSpec(memory_space=pltpu.VMEM)] * 3,
         out_specs=pl.BlockSpec(memory_space=pl.ANY),
-        scratch_shapes=gather_sems(n),
+        scratch_shapes=[pltpu.VMEM((rows, width), x.dtype)] + gather_sems(n),
         compiler_params=pltpu.CompilerParams(
             collective_id=collective_id, has_side_effects=True, vmem_limit_bytes=VMEM_LIMIT
         ),
         cost_estimate=LINK_COST,
         name="gather_rows",
-    )(x)
+    )(x, gain, shift)
 
 
 class Scatter:
@@ -407,6 +429,12 @@
 TN = (((0,), (0,)), ((), ()))
 
 
+def as_column(row):
+    width = row.shape[1]
+    here = lax.broadcasted_iota(jnp.int32, (width, width), 0) == lax.broadcasted_iota(jnp.int32, (width, width), 1)
+    return jnp.sum(jnp.where(here, row, 0.0), axis=1, keepdims=True)
+
+
 def masked_scores(slope, q, keys, query_labels, key_labels, first):
     raw = lax.dot_general(q, keys, NT, preferred_element_type=jnp.float32)
     rows, width = raw.shape
@@ -491,7 +519,7 @@
     return 256 if width % 256 == 0 else width
 
 
-def attend_one(slope, proj_ref, start, head, column_ref, row_ref, out_ref, length):
+def attend_one(slope, proj_ref, start, head, row_ref, out_ref, length):
     at = pl.multiple_of(head * 3 * HEAD_DIM, HEAD_DIM)
 
     def take(which, first, size):
@@ -500,7 +528,7 @@
     for first in range(0, length, BLOCK):
         last = first + BLOCK
         scores = masked_scores(
-            slope, take(0, first, BLOCK), take(1, 0, last), column_ref[first:last, :], row_ref[:, :last], first
+            slope, take(0, first, BLOCK), take(1, 0, last), as_column(row_ref[:, first:last]), row_ref[:, :last], first
         )
         top = jnp.max(scores, axis=1, keepdims=True)
         expo = jnp.exp2(scores - top)
@@ -512,7 +540,7 @@
 
 
 def project_kernel(
-    n, length, slope_ref, own_ref, rows_hbm, w_ref, bias_ref, column_ref, row_ref, gathered, proj_hbm, mixed_ref,
+    n, length, slope_ref, own_ref, rows_hbm, w_ref, bias_ref, row_ref, gathered, proj_hbm, mixed_ref,
     proj, buf, load_sem, store_sem, *sems
 ):
     gather = Gather(n, own_ref, gathered, sems)
@@ -559,7 +587,6 @@
             proj,
             pl.multiple_of(s * length, length),
             head,
-            column_ref.at[s],
             row_ref.at[s],
             mixed_ref,
             length,
@@ -591,7 +618,7 @@
             jax.ShapeDtypeStruct((total, width), jnp.bfloat16),
             jax.ShapeDtypeStruct((total, heads * HEAD_DIM), jnp.bfloat16),
         ),
-        in_specs=[pl.BlockSpec(memory_space=pltpu.SMEM), vmem, hbm, vmem, vmem, vmem, vmem],
+        in_specs=[pl.BlockSpec(memory_space=pltpu.SMEM), vmem, hbm, vmem, vmem, vmem],
         out_specs=(hbm, hbm, vmem),
         scratch_shapes=[
             pltpu.VMEM((total, width), jnp.bfloat16),
@@ -605,7 +632,7 @@
         ),
         cost_estimate=LINK_COST,
         name="project_attend",
-    )(slopes, own, attn_rows, weight, bias, labels[:, :, None], labels[:, None, :])
+    )(slopes, own, attn_rows, weight, bias, labels[:, None, :])
 
 
 def gelu_both(value):
@@ -619,78 +646,89 @@
 
 def expand_kernel(
     n, own_ref, grad_hbm, up_ref, down_ref, bias_ref, rows_hbm, act_hbm, pre_hbm, sum_ref,
-    gathered, grads, act, pre, load_sem, act_sem, pre_sem, rows_sem, *sems
+    gathered, grads, backs, act, pre, load_sem, act_sem, pre_sem, rows_sem, *sems
 ):
     gather = Gather(n, own_ref, gathered, sems)
     rows, depth = own_ref.shape
     width = up_ref.shape[1]
     tile = tile_of(width)
-    order = [gather.place(mask, core) for mask in (0,) for core in (0, 1)]
-    for count in range(1, gather.bits + 1):
-        for core in (0, 1):
-            order += [gather.place(mask, core) for mask in gather.level(count)]
-
-    def span(at):
-        return pl.ds(pl.multiple_of(at * rows, rows), rows)
+    levels = [gather.level(count) for count in range(gather.bits + 1)]
+    codes = [2 * mask + core for masks in levels for core in (0, 1) for mask in masks]
+
+    def span(i):
+        return pl.ds(pl.multiple_of(gather.away(codes, i) * rows, rows), rows)
 
     def load(i):
-        return pltpu.make_async_copy(grad_hbm.at[span(order[i]), :], grads.at[i % 2], load_sem.at[i % 2])
+        return pltpu.make_async_copy(grad_hbm.at[span(i), :], grads.at[parity(i)], load_sem.at[parity(i)])
 
     def store(i):
+        slot = parity(i)
         return (
-            pltpu.make_async_copy(act.at[i % 2], act_hbm.at[span(order[i]), :], act_sem.at[i % 2]),
-            pltpu.make_async_copy(pre.at[i % 2], pre_hbm.at[span(order[i]), :], pre_sem.at[i % 2]),
+            pltpu.make_async_copy(act.at[slot], act_hbm.at[span(i), :], act_sem.at[slot]),
+            pltpu.make_async_copy(pre.at[slot], pre_hbm.at[span(i), :], pre_sem.at[slot]),
         )
 
     def keep_rows(i):
-        return pltpu.make_async_copy(gathered.at[span(order[i]), :], rows_hbm.at[span(order[i]), :], rows_sem.at[i])
-
-    def work(i):
-        at = order[i]
+        return pltpu.make_async_copy(gathered.at[span(i), :], rows_hbm.at[span(i), :], rows_sem.at[i])
+
+    def cols_of(j):
+        return pl.ds(pl.multiple_of(j * tile, tile), tile)
+
+    def back(i, carry):
+        load(i).wait()
+
+        @pl.when(i + 1 < n)
+        def _():
+            load(i + 1).start()
+
+        def columns(j, carry):
+            value = lax.dot_general(
+                grads[parity(i)], down_ref[cols_of(j), :], NT, preferred_element_type=jnp.float32
+            )
+            backs[i, :, cols_of(j)] = value.astype(backs.dtype)
+            return carry
+
+        lax.fori_loop(0, width // tile, columns, 0)
+        return carry
+
+    def work(i, carry):
+        first = 0
+        for count, masks in enumerate(levels):
+            if count:
+                pl.when(i == first)(functools.partial(gather.forward, count))
+            for k, mask in enumerate(masks):
+                pl.when(i == first + len(masks) + k)(functools.partial(gather.wait_core, mask))
+            first += 2 * len(masks)
         keep_rows(i).start()
-        load(i).wait()
-        if i + 1 < n:
-            load(i + 1).start()
-        if i >= 2:
+
+        @pl.when(i >= 2)
+        def _():
             for copy in store(i - 2):
                 copy.wait()
 
+        here, slot = span(i), parity(i)
+
         def columns(j, carry):
-            cols = pl.ds(pl.multiple_of(j * tile, tile), tile)
-            before = (
-                jnp.dot(gathered[span(at), :], up_ref[:, cols], preferred_element_type=jnp.float32)
-                + bias_ref[:, cols]
-            )
-            back = lax.dot_general(grads[i % 2], down_ref[cols, :], NT, preferred_element_type=jnp.float32)
+            cols = cols_of(j)
+            before = jnp.dot(gathered[here, :], up_ref[:, cols], preferred_element_type=jnp.float32) + bias_ref[:, cols]
             active, slope = gelu_both(before)
-            act[i % 2, :, cols] = active.astype(act.dtype)
-            rounded = (back * slope).astype(pre.dtype)
-            pre[i % 2, :, cols] = rounded
+            act[slot, :, cols] = active.astype(act.dtype)
+            rounded = (backs[i, :, cols].astype(jnp.float32) * slope).astype(pre.dtype)
+            pre[slot, :, cols] = rounded
             sum_ref[:, cols] += jnp.sum(rounded.astype(jnp.float32), axis=0, keepdims=True)
             return carry
 
         lax.fori_loop(0, width // tile, columns, 0)
         for copy in store(i):
             copy.start()
+        return carry
 
     sum_ref[...] = jnp.zeros_like(sum_ref)
     load(0).start()
     gather.start()
+    lax.fori_loop(0, n, back, 0)
     gather.keep().wait()
-    work(0)
-    gather.wait_core(0)
-    work(1)
-    i = 2
-    for count in range(1, gather.bits + 1):
-        masks = gather.level(count)
-        gather.forward(count)
-        for _ in masks:
-            work(i)
-            i += 1
-        for mask in masks:
-            gather.wait_core(mask)
-            work(i)
-            i += 1
+    lax.fori_loop(0, n, work, 0)
     for last in (n - 2, n - 1):
         for copy in store(last):
             copy.wait()
@@ -719,6 +757,7 @@
         scratch_shapes=[
             pltpu.VMEM((total, depth), jnp.bfloat16),
             pltpu.VMEM((2, rows, depth), jnp.bfloat16),
+            pltpu.VMEM((n, rows, width), jnp.bfloat16),
             pltpu.VMEM((2, rows, width), jnp.bfloat16),
             pltpu.VMEM((2, rows, width), jnp.bfloat16),
             dma((2,)),
@@ -982,7 +1021,7 @@
     )(grad_pre, up, activated, grad_rows, residual, cotangent, gain)
 
 
-def attend_back_one(slope, proj_ref, grad_ref, start, head, column_ref, row_ref, out_ref, dk_ref, dv_ref, sums_ref, length):
+def attend_back_one(slope, proj_ref, grad_ref, start, head, row_ref, out_ref, dk_ref, dv_ref, sums_ref, length):
     at = pl.multiple_of(head * 3 * HEAD_DIM, HEAD_DIM)
     own = pl.ds(pl.multiple_of(head * HEAD_DIM, HEAD_DIM), HEAD_DIM)
 
@@ -996,7 +1035,7 @@
     for first in reversed(range(0, length, BLOCK)):
         last = first + BLOCK
         q, g = take(0, first, BLOCK), grad_ref[pl.ds(start + first, BLOCK), own]
-        scores = masked_scores(slope, q, take(1, 0, last), column_ref[first:last, :], row_ref[:, :last], first)
+        scores = masked_scores(slope, q, take(1, 0, last), as_column(row_ref[:, first:last]), row_ref[:, :last], first)
         top = jnp.max(scores, axis=1, keepdims=True)
         expo = jnp.exp2(scores - top)
         probs = expo * (1.0 / jnp.sum(expo, axis=1, keepdims=True))
@@ -1027,7 +1066,7 @@
 
 
 def dense_back_kernel(
-    n, length, slope_ref, own_ref, mixed_ref, w_ref, left_hbm, right_hbm, proj_hbm, column_ref, row_ref,
+    n, length, slope_ref, own_ref, mixed_ref, w_ref, left_hbm, right_hbm, proj_hbm, row_ref,
     grad_proj_ref, sums_ref, grad_dense_ref, grad_up_hbm, gathered, acc, grad_mixed, proj, dk, dv, fetch_sem, *scratch
 ):
     fetch = pltpu.make_async_copy(proj_hbm, proj, fetch_sem)
@@ -1052,31 +1091,37 @@
                 mixed_ref[span, :], gathered[span, cols], TN, preferred_element_type=jnp.float32
             )
 
-    def attend(mask):
-        first = (gather.place(mask, 0) // 2 // chips) * sequences
-
-        def one(i, carry):
-            s, head = first + i // heads, lax.rem(i, heads)
-            attend_back_one(
-                slope_ref[head], proj, grad_mixed, pl.multiple_of(s * length, length), head, column_ref.at[s],
-                row_ref.at[s], grad_proj_ref, dk, dv, sums_ref, length,
-            )
-            return carry
-
-        lax.fori_loop(0, sequences * heads, one, 0)
-
-    arrived = {}
-
-    def pair(mask):
-        if mask == 0:
-            gather.keep().wait()
-        work(gather.place(mask, 0))
-        gather.wait_core(mask)
-        work(gather.place(mask, 1))
-        group = arrived.setdefault(mask // chips, [])
-        group.append(mask)
-        if len(group) == chips:
-            attend(mask)
+    order = [mask for count in range(gather.bits + 1) for mask in gather.level(count)]
+    codes = [2 * mask + core for mask in order for core in (0, 1)]
+    complete = [
+        int(core == 1 and all(other // chips != mask // chips for other in order[k + 1 :]))
+        for k, mask in enumerate(order)
+        for core in (0, 1)
+    ]
+
+    def step(t, carry):
+        for k, mask in enumerate(order):
+            if k and mask.bit_count() > order[k - 1].bit_count():
+                pl.when(t == 2 * k)(functools.partial(gather.forward, mask.bit_count()))
+            pl.when(t == 2 * k + 1)(functools.partial(gather.wait_core, mask))
+        at = gather.away(codes, t)
+        work(at)
+
+        @pl.when(look_up(complete, t) == 1)
+        def _():
+            first = (at // 2 // chips) * sequences
+
+            def one(i, carry):
+                s, head = first + i // heads, lax.rem(i, heads)
+                attend_back_one(
+                    slope_ref[head], proj, grad_mixed, pl.multiple_of(s * length, length), head, row_ref.at[s],
+                    grad_proj_ref, dk, dv, sums_ref, length,
+                )
+                return carry
+
+            lax.fori_loop(0, sequences * heads, one, 0)
+
+        return carry
 
     product.start()
     gather.start()
@@ -1084,11 +1129,8 @@
     sums_ref[...] = jnp.zeros_like(sums_ref)
     product.batch(0, 1)
     fetch.wait()
-    pair(0)
-    for count in range(1, gather.bits + 1):
-        gather.forward(count)
-        for mask in gather.level(count):
-            pair(mask)
+    gather.keep().wait()
+    lax.fori_loop(0, 2 * len(order), step, 0)
     grad_dense_ref[...] = acc[...].astype(grad_dense_ref.dtype)
     product.finish()
     gather.finish_sends()
@@ -1108,7 +1150,7 @@
         ),
         in_specs=[pl.BlockSpec(memory_space=pltpu.SMEM), VMEM_SPEC, VMEM_SPEC, VMEM_SPEC]
         + [HBM_SPEC] * 3
-        + [VMEM_SPEC] * 2,
+        + [VMEM_SPEC],
         out_specs=(VMEM_SPEC, VMEM_SPEC, VMEM_SPEC, HBM_SPEC),
         scratch_shapes=[
             pltpu.VMEM((total, width), jnp.bfloat16),
@@ -1124,7 +1166,7 @@
         compiler_params=comm_params(collective_id),
         cost_estimate=LINK_COST,
         name="dense_back",
-    )(slopes, own, mixed, weight, mlp_rows, grad_pre, proj, labels[:, :, None], labels[:, None, :])
+    )(slopes, own, mixed, weight, mlp_rows, grad_pre, proj, labels[:, None, :])
 
 
 def shrink_kernel(
@@ -1240,18 +1282,51 @@
 HEADS = 16
 
 
-def normalize(rows):
-    center = rows - jnp.mean(rows, axis=1, keepdims=True)
-    factor = lax.rsqrt(jnp.mean(center * center, axis=1, keepdims=True) + 1e-05)
-    return center * factor
-
-
 def wide(vector):
     return vector.astype(jnp.float32)[None]
 
 
 def share(grad, dimension):
-    return lax.psum_scatter(grad, "dp", scatter_dimension=dimension, tiled=True).astype(jnp.float32)
+    return lax.psum_scatter(grad, "dp", scatter_dimension=dimension, tiled=True)
+
+
+def finish_kernel(heads_width, *refs):
+    ins, outs = refs[:8], refs[8:]
+    for source, target in zip(ins[:6], outs[:6]):
+        target[...] = source[...].astype(target.dtype)
+
+    @pl.when(pl.program_id(0) == 0)
+    def _():
+        sums, biases = ins[6:]
+        for i in range(6):
+            outs[6 + i][...] = sums[i : i + 1, :]
+        outs[12][...] = biases[0:1, :]
+        outs[13][...] = biases[1:2, :heads_width]
+        outs[14][...] = biases[2:3, :heads_width]
+
+
+def finish(hidden_output, grad_input, weights, sums, biases, heads_width):
+    steps = 8
+
+    def rows_block(x):
+        return pl.BlockSpec((x.shape[0] // steps, x.shape[1]), lambda i: (i, 0))
+
+    def whole_block(shape):
+        return pl.BlockSpec(shape, lambda i: (0, 0))
+
+    large = (hidden_output, grad_input) + weights
+    small = [(1, sums.shape[1])] * 6 + [(1, biases.shape[1]), (1, heads_width), (1, heads_width)]
+    results = pl.pallas_call(
+        functools.partial(finish_kernel, heads_width),
+        grid=(steps,),
+        out_shape=[jax.ShapeDtypeStruct(hidden_output.shape, hidden_output.dtype)]
+        + [jax.ShapeDtypeStruct(x.shape, jnp.float32) for x in large[1:]]
+        + [jax.ShapeDtypeStruct(shape, jnp.float32) for shape in small],
+        in_specs=[rows_block(x) for x in large] + [whole_block(sums.shape), whole_block(biases.shape)],
+        out_specs=[rows_block(x) for x in large] + [whole_block(shape) for shape in small],
+        name="finish",
+    )(*large, sums, biases)
+    return results[:6], [x.reshape(-1) for x in results[6:]]
 
 
 def on_device(
@@ -1277,9 +1352,7 @@
     d,
 ):
     heads_local = query_bias.shape[0] // HEAD_DIM
-    normed_first = normalize(hidden_input.astype(jnp.float32))
-    attn_input = (normed_first * wide(first_gain) + wide(first_shift)).astype(jnp.bfloat16)
-    attn_rows = gather_rows(attn_input, n, 1)
+    attn_rows = gather_rows(hidden_input, wide(first_gain), wide(first_shift), n, 1)
     project_full, dense_full, expand_full, shrink_full = (
         lax.all_gather(qkv_weight, "dp", axis=0, tiled=True),
         lax.all_gather(dense_weight, "dp", axis=1, tiled=True),
@@ -1295,7 +1368,7 @@
     slopes = jnp.exp2(-8.0 * (heads_index.astype(jnp.float32) + 1.0) / HEADS) * LOG2E
     position = lax.broadcasted_iota(jnp.int32, (sequences, length), 1)
     filled = jnp.sum(document_lengths, axis=1, keepdims=True)
-    labels = jnp.where(position < filled, segments.reshape(sequences, length), length + position)
+    labels = jnp.where(position < filled, segments.reshape(sequences, length), length + position).astype(jnp.float32)
     query_bias32 = query_bias.astype(jnp.float32).reshape(heads_local, HEAD_DIM)
     value_bias32 = value_bias.astype(jnp.float32).reshape(heads_local, HEAD_DIM)
     proj_bias = jnp.stack((query_bias32, jnp.zeros_like(query_bias32), value_bias32), axis=1).reshape(
@@ -1328,10 +1401,17 @@
         activated, shrink_full, residual, wide(down_bias), sums, sum_up_bias, head_sums, n, d, 3
     )
     heads_width = heads_local * HEAD_DIM
-    grad_second_gain, grad_second_shift, grad_dense_bias, grad_down_bias, grad_first_gain, grad_first_shift = (
-        sums[i] for i in range(6)
-    )
-    grad_up_bias, grad_query_bias, grad_value_bias = biases[0], biases[1, :heads_width], biases[2, :heads_width]
+    large, small = finish(
+        hidden_output,
+        grad_input,
+        (grad_qkv_weight, grad_dense_weight, grad_up_weight, grad_down_weight),
+        sums,
+        biases,
+        heads_width,
+    )
+    hidden_output, grad_input, grad_qkv_weight, grad_dense_weight, grad_up_weight, grad_down_weight = large
+    grad_second_gain, grad_second_shift, grad_dense_bias, grad_down_bias, grad_first_gain, grad_first_shift = small[:6]
+    grad_up_bias, grad_query_bias, grad_value_bias = small[6:]
     return (
         hidden_output,
         grad_input,

time: 752 us -> 736 us (0.979)
  local copies, waits for them, and re-layouts: 10.6 us -> 0.68 us
  other arithmetic: 20.5 us -> 11.7 us
    convert_element_type x7 -> x1, other arithmetic: 13.5 us -> 0.69 us  [on_device(): jnp.where(position < filled, segments.reshape(sequences, length), length...]
    pallas_call x0 -> x1, Pallas kernels: none -> 10.3 us  [finish(): pl.pallas_call(functools.partial(finish_kernel, heads_width), grid=(steps...]
  transfers between devices with their start and end apart: 8 -> 8, of which waited for: 1 -> 1; matrix products, arithmetic and copies ran while one was open for 3% -> 2% of each run, Pallas kernels for 68% -> 70%
where the time goes in v6:
time: 736 us; the launch traced here: 734 us
  Pallas kernels  702 us (95%)
  between operations  14.3 us (2%)
  other arithmetic  11.7 us (2%)
    pallas_call x1, Pallas kernels, expand_back(): pl.pallas_call(functools.partial(expand_back_kernel, n), out_shape=(jax.S...  95.6 us
    pallas_call x1, Pallas kernels, project_back(): pl.pallas_call(functools.partial(project_back_kernel, n), out_shape=(jax....  90.3 us
    pallas_call x1, Pallas kernels, dense_back(): pl.pallas_call(functools.partial(dense_back_kernel, n, length), out_shape...  90 us
    pallas_call x1, Pallas kernels, shrink(): pl.pallas_call(functools.partial(shrink_kernel, n, d), out_shape=(jax.Sha...  87.5 us
    pallas_call x1, Pallas kernels, expand(): pl.pallas_call(functools.partial(expand_kernel, n), out_shape=(jax.ShapeD...  85.2 us
    pallas_call x1, Pallas kernels, dense(): pl.pallas_call(functools.partial(dense_kernel, n), out_shape=(jax.ShapeDt...  82.5 us
    pallas_call x1, Pallas kernels, gather_rows(): pl.pallas_call(functools.partial(gather_kernel, n), out_shape=jax.ShapeDt...  82.3 us
    pallas_call x1, Pallas kernels, project_attend(): pl.pallas_call(functools.partial(project_kernel, n, labels.shape[1]), out...  78.9 us
  transfers between devices with their start and end apart: 8, of which 1 were waited for; matrix products, arithmetic and copies ran while one was open for 2% of the time, Pallas kernels for 70%

profile of v6, /device:TPU:0, one launch (start us, length us, event | category | flops | bytes accessed | tf_op | source)
XLA Modules:
  0.0 734.1 jit_solution(13482597859851706413)
XLA Ops:
  7.2 0.7 all-gather.5.cloned.1.call-update
  8.0 0.7 all-gather.7.cloned.1.call-update
  8.7 0.7 all-gather.11.cloned.1.call-update
  10.0 1.3 broadcast_in_dim.54
  11.3 1.3 broadcast_in_dim.55
  12.6 0.7 stack_reshape.16
  13.3 0.7 stack_reshape.17
  14.7 1.3 broadcast_in_dim.57
  15.9 1.3 broadcast_in_dim.56
  17.2 1.3 broadcast_in_dim.58
  18.5 1.3 broadcast_in_dim.59
  19.8 0.8 reduce_sum.9
  20.6 82.3 %gather_rows.1.rows_hbm.left_hbm = bf16[4096,2048]{1,0:T(8,128)(2,1)} custom-call(bf16[512,2048]{1,0:T(8,128)(2,1)} %input_hbm.3, f32[1,2048]{1,0:T(1,128)} %bitcast.20, f32[1,2048]{1,0:T(1,128)} %bitcast.26), custom_call_target="tpu_custom_call" | custom-call | bytes 280000000 | tf_op jit(solution)/shard_map/gather_rows/pallas_call | solution.py:201
  103.5 0.7 fusion.row_ref
  104.2 78.9 %project_attend.1 = (bf16[4096,2048]{1,0:T(8,128)(2,1)}, bf16[4096,768]{1,0:T(8,128)(2,1)}, bf16[4096,256]{1,0:T(8,128)(2,1)}) custom-call(f32[2]{0:T(128)} %exponential_multiply_fusion.slope_ref, bf16[512,2048]{1,0:T(8,128)(2,1)} %cotangent_hbm.1, bf16[4096,2048]{1,0:T(8,128)(2,1)} %gather_rows.1.rows_hbm.left_hbm, ...), custom_call_target="tpu_custom_call" | custom-call | bytes 280000000 | tf_op jit(solution)/shard_map/project_attend/pallas_call | solution.py:614
  183.1 82.5 %dense.1 = (f32[512,2048]{1,0:T(8,128)}, bf16[512,2048]{1,0:T(8,128)(2,1)}) custom-call(bf16[4096,256]{1,0:T(8,128)(2,1)} %get-tuple-element.55.a_hbm.mixed_ref, bf16[256,2048]{1,0:T(8,128)(2,1)} %all-gather.7.cloned.1.call-done.w_ref, bf16[512,2048]{1,0:T(8,128)(2,1)} %input_hbm.3, f32[1,2048]{1,0:T(1,128)} %bitcast.24, f32[1,2048]{1,0:T(1,128)} %bitcast.22, ...), custom_call_target="tpu_custom_call" | custom-call | bytes 280000000 | tf_op jit(solution)/shard_map/dense/pallas_call | solution.py:982
  265.6 0.8 all-gather.9.cloned.1.call-done.up_ref.w_ref
  266.4 85.2 %expand.1 = (bf16[4096,2048]{1,0:T(8,128)(2,1)}, bf16[4096,1024]{1,0:T(8,128)(2,1)}, bf16[4096,1024]{1,0:T(8,128)(2,1)}, f32[1,1024]{1,0:T(1,128)}) custom-call(bf16[512,2048]{1,0:T(8,128)(2,1)} %get-tuple-element.56.own_ref, bf16[4096,2048]{1,0:T(8,128)(2,1)} %get-tuple-element.57.grad_hbm.rows_hbm, ...), custom_call_target="tpu_custom_call" | custom-call | bytes 280000000 | tf_op jit(solution)/shard_map/expand/pallas_call | solution.py:747
  351.6 95.6 %expand_back.1 = (f32[512,2048]{1,0:T(8,128)}, bf16[512,2048]{1,0:T(8,128)(2,1)}, f32[8,2048]{1,0:T(8,128)}, bf16[1024,2048]{1,0:T(8,128)(2,1)}) custom-call(bf16[4096,1024]{1,0:T(8,128)(2,1)} %get-tuple-element.60.a_hbm.right_hbm, bf16[2048,1024]{1,0:T(8,128)(2,1)} %all-gather.9.cloned.1.call-done.up_ref.w_ref, ...), custom_call_target="tpu_custom_call" | custom-call | bytes 280000000 | tf_op jit(solution)/shard_map/expand_back/pallas_call | solution.py:1001
  447.4 90.0 %dense_back.1 = (bf16[4096,768]{1,0:T(8,128)(2,1)}, f32[8,256]{1,0:T(8,128)}, bf16[256,2048]{1,0:T(8,128)(2,1)}, bf16[2048,1024]{1,0:T(8,128)(2,1)}) custom-call(f32[2]{0:T(128)} %exponential_multiply_fusion.slope_ref, bf16[512,2048]{1,0:T(8,128)(2,1)} %get-tuple-element.62.own_ref, bf16[4096,256]{1,0:T(8,128)(2,1)} %get-tuple-element.55.a_hbm.mixed_ref, ...), custom_call_target="tpu_custom_call" | custom-call | bytes 280000000 | tf_op jit(solution)/shard_map/dense_back/pallas_call | solution.py:1143
  537.5 0.7 reduce-scatter.11.cloned.1.call-update
  538.5 90.3 %project_back.1 = (f32[512,2048]{1,0:T(8,128)}, f32[8,2048]{1,0:T(8,128)}, bf16[2048,768]{1,0:T(8,128)(2,1)}) custom-call(bf16[4096,768]{1,0:T(8,128)(2,1)} %get-tuple-element.66.a_hbm, bf16[2048,768]{1,0:T(8,128)(2,1)} %all-gather.5.cloned.1.call-done.w_ref, bf16[512,2048]{1,0:T(8,128)(2,1)} %input_hbm.3, f32[512,2048]{1,0:T(8,128)} %get-tuple-element.67.grad_hbm, ...), custom_call_target="tpu_custom_call" | custom-call | bytes 280000000 | tf_op jit(solution)/shard_map/project_back/pallas_call | solution.py:1260
  629.4 87.5 %shrink.1 = (bf16[512,2048]{1,0:T(8,128)(2,1)}, f32[8,2048]{1,0:T(8,128)}, f32[8,1024]{1,0:T(8,128)}) custom-call(bf16[4096,1024]{1,0:T(8,128)(2,1)} %get-tuple-element.58.act_hbm.a_hbm, bf16[1024,2048]{1,0:T(8,128)(2,1)} %all-gather.11.cloned.1.call-done.down_ref.w_ref, f32[512,2048]{1,0:T(8,128)} %get-tuple-element.59.residual_hbm, f32[1,2048]{1,0:T(1,128)} %bitcast.27, ...), custom_call_target="tpu_custom_call" | custom-call | bytes 280000000 | tf_op jit(solution)/shard_map/shrink/pallas_call | solution.py:1208
  717.0 10.3 %finish.1 = (bf16[512,2048]{1,0:T(8,128)(2,1)}, f32[512,2048]{1,0:T(8,128)}, f32[512,768]{1,0:T(8,128)}, f32[256,512]{1,0:T(8,128)}, f32[512,1024]{1,0:T(8,128)}...) custom-call(bf16[512,2048]{1,0:T(8,128)(2,1)} %get-tuple-element.72., ...), custom_call_target="tpu_custom_call" | custom-call | tf_op jit(solution)/shard_map/finish/pallas_call | solution.py:1319
  (29 shorter events, 3.3 us)
Async XLA Ops:
  7.2 97.0 %all-gather.5.cloned.1.call-start = ((), (), s32[]{:S(2)}) async-start(), calls=%async_computation.4 | async-start | bytes 3932160 | tf_op jit(solution)/shard_map/all_gather | solution.py:1357
  7.9 175.2 %all-gather.7.cloned.1.call-start = ((), (), s32[]{:S(2)}) async-start(), calls=%async_computation.5 | async-start | bytes 1310720 | tf_op jit(solution)/shard_map/all_gather | solution.py:1358
  8.7 257.0 %all-gather.11.cloned.1.call-start = ((), (), s32[]{:S(2)}) async-start(), calls=%async_computation.7 | async-start | bytes 5242880 | tf_op jit(solution)/shard_map/all_gather | solution.py:1360
  9.4 257.0 %all-gather.9.cloned.1.call-start = ((), (), s32[]{:S(2)}) async-start(), calls=%async_computation.6 | async-start | bytes 5242880 | tf_op jit(solution)/shard_map/all_gather | solution.py:1359
  10.0 528.5 %reduce-scatter.5.cloned.1.call-start = ((), (), s32[]{:S(2)}) async-start(), calls=%async_computation.8 | async-start | bytes 5242880 | tf_op jit(solution)/shard_map/reduce_scatter | solution.py:1290
  20.6 82.9 %copy-start = (s32[4096]{0:T(1024)S(1)}, s32[4096]{0:T(1024)}, u32[]{:S(2)}) copy-start(s32[4096]{0:T(1024)} %param.31) | copy-start | bytes 49156
  447.2 269.7 %reduce-scatter.9.cloned.1.call-start = ((), (), s32[]{:S(2)}) async-start(), calls=%async_computation.10 | async-start | bytes 1310720 | tf_op jit(solution)/shard_map/reduce_scatter | solution.py:1290
  537.5 179.5 %reduce-scatter.11.cloned.1.call-start = ((), (), s32[]{:S(2)}) async-start(), calls=%async_computation.11 | async-start | bytes 5242880 | tf_op jit(solution)/shard_map/reduce_scatter | solution.py:1290
  538.2 178.7 %reduce-scatter.7.cloned.1.call-start = ((), (), s32[]{:S(2)}) async-start(), calls=%async_computation.9 | async-start | bytes 3932160 | tf_op jit(solution)/shard_map/reduce_scatter | solution.py:1290
  538.5 90.3 %copy-start.1 = (bf16[2048]{0:T(1024)(128)(2,1)S(1)}, bf16[2048]{0:T(1024)(128)(2,1)}, u32[]{:S(2)}) copy-start(bf16[2048]{0:T(1024)(128)(2,1)} %param.30) | copy-start | bytes 12292
Sparse Core Ops, SparseCore 0:
  9.6 66.1 all-gather.4
  77.3 26.6 all-gather.6
  105.6 80.0 all-gather.10
  187.1 79.2 all-gather.8
  447.3 75.9 reduce-scatter.4
  537.6 25.8 reduce-scatter.8
  565.8 75.3 reduce-scatter.10
  643.4 65.0 reduce-scatter.6

commit v7 on v6

--- a/solution.py
+++ b/solution.py
@@ -43,7 +43,7 @@
     return {"tensor": index}
 
 
-def greet(me, bits, d=1):
+def greet(me, bits, d=1, meanwhile=None):
     barrier = pltpu.get_barrier_semaphore()
     for bit in range(bits + 1):
         pl.semaphore_signal(
@@ -53,6 +53,8 @@
         pl.semaphore_signal(
             barrier, inc=1, device_id=ahead_on_dp(ahead, d), device_id_type=pl.DeviceIdType.MESH
         )
+    if meanwhile is not None:
+        meanwhile()
     pl.semaphore_wait(barrier, bits + d)
 
 
@@ -138,8 +140,8 @@
         rows = pl.ds(pl.multiple_of(self.me * self.rows, self.rows), self.rows)
         return pltpu.make_async_copy(self.own, self.out.at[rows, :], self.own_sem)
 
-    def start(self):
-        greet(self.me, self.bits)
+    def start(self, meanwhile=None):
+        greet(self.me, self.bits, meanwhile=meanwhile)
         for step in range(self.bits):
             for part in range(self.bits):
                 self.chip_copy(part, 0, step).start()
@@ -174,14 +176,29 @@
                 self.core_copy(part, index).wait_send()
 
 
-def gather_kernel(n, x_ref, gain_ref, shift_ref, out_ref, own, *sems):
+def gather_kernel(n, x_ref, *refs):
+    flat_refs, (out_ref, vectors_ref, own, *sems) = refs[:9], refs[9:]
+
+    def put(row, start, ref):
+        size = ref.shape[0]
+        vectors_ref[row, :, start : start + size] = ref[...].astype(jnp.float32).reshape(1, size)
+
+    put(FIRST_GAIN, 0, flat_refs[FIRST_GAIN])
+    put(FIRST_SHIFT, 0, flat_refs[FIRST_SHIFT])
+
     def work(at):
         normed, _ = normal_rows(x_ref[at, :].astype(jnp.float32))
-        own[at, :] = (normed * gain_ref[...] + shift_ref[...]).astype(own.dtype)
-
-    row_blocks(0, own.shape[0], 32, work)
+        own[at, :] = (normed * vectors_ref[FIRST_GAIN] + vectors_ref[FIRST_SHIFT]).astype(own.dtype)
+
     gather = Gather(n, own, out_ref, sems)
-    gather.start()
+    gather.start(lambda: row_blocks(0, own.shape[0], 32, work))
+    for row in range(FIRST_SHIFT + 1, UP_BIAS):
+        put(row, 0, flat_refs[row])
+    vectors_ref[UP_BIAS] = jnp.zeros(vectors_ref.shape[1:], jnp.float32)
+    vectors_ref[HEAD_BIASES] = jnp.zeros(vectors_ref.shape[1:], jnp.float32)
+    put(UP_BIAS, 0, flat_refs[UP_BIAS])
+    put(HEAD_BIASES, 0, flat_refs[7])
+    put(HEAD_BIASES, flat_refs[7].shape[0], flat_refs[8])
     for count in range(1, gather.bits + 1):
         gather.forward(count)
     for mask in range(2**gather.bits):
@@ -196,20 +213,23 @@
     return [dma(())] + [dma((bits, 2**bits))] * 4
 
 
-def gather_rows(x, gain, shift, n, collective_id):
+def gather_rows(x, vectors, n, collective_id):
     rows, width = x.shape
     return pl.pallas_call(
         functools.partial(gather_kernel, n),
-        out_shape=jax.ShapeDtypeStruct((n * rows, width), x.dtype),
-        in_specs=[pl.BlockSpec(memory_space=pltpu.VMEM)] * 3,
-        out_specs=pl.BlockSpec(memory_space=pl.ANY),
+        out_shape=(
+            jax.ShapeDtypeStruct((n * rows, width), x.dtype),
+            jax.ShapeDtypeStruct((8, 1, width), jnp.float32),
+        ),
+        in_specs=[VMEM_SPEC] * 10,
+        out_specs=(HBM_SPEC, VMEM_SPEC),
         scratch_shapes=[pltpu.VMEM((rows, width), x.dtype)] + gather_sems(n),
         compiler_params=pltpu.CompilerParams(
             collective_id=collective_id, has_side_effects=True, vmem_limit_bytes=VMEM_LIMIT
         ),
         cost_estimate=LINK_COST,
         name="gather_rows",
-    )(x, gain, shift)
+    )(x, *vectors)
 
 
 class Scatter:
@@ -422,6 +442,8 @@
 
 
 HEAD_DIM = 128
+HEADS = 16
+FIRST_GAIN, FIRST_SHIFT, DENSE_BIAS, SECOND_GAIN, SECOND_SHIFT, DOWN_BIAS, UP_BIAS, HEAD_BIASES = range(8)
 LOG2E = 1.4426950408889634
 SCALE = 1.0 / math.sqrt(HEAD_DIM)
 BLOCK = 256
@@ -540,8 +562,8 @@
 
 
 def project_kernel(
-    n, length, slope_ref, own_ref, rows_hbm, w_ref, bias_ref, row_ref, gathered, proj_hbm, mixed_ref,
-    proj, buf, load_sem, store_sem, *sems
+    n, length, slope_ref, own_ref, rows_hbm, w_ref, vectors_ref, row_ref, gathered, proj_hbm, mixed_ref,
+    proj, buf, bias, load_sem, store_sem, *sems
 ):
     gather = Gather(n, own_ref, gathered, sems)
     rows = own_ref.shape[0]
@@ -555,6 +577,11 @@
         return pltpu.make_async_copy(rows_hbm.at[at, :], buf.at[lax.rem(i, 2)], load_sem.at[lax.rem(i, 2)])
 
     load(0).start()
+    bias[...] = jnp.zeros_like(bias)
+    for head in range(heads):
+        for which, first in ((0, 0), (2, heads * HEAD_DIM)):
+            at = (3 * head + which) * HEAD_DIM
+            bias[:, at : at + HEAD_DIM] = vectors_ref[HEAD_BIASES, :, first + head * HEAD_DIM : first + (head + 1) * HEAD_DIM]
     gather.start()
 
     def store(i):
@@ -572,7 +599,7 @@
         for first in range(0, width, tile):
             cols = slice(first, first + tile)
             proj[at, cols] = (
-                jnp.dot(buf[lax.rem(i, 2)], w_ref[:, cols], preferred_element_type=jnp.float32) + bias_ref[:, cols]
+                jnp.dot(buf[lax.rem(i, 2)], w_ref[:, cols], preferred_element_type=jnp.float32) + bias[:, cols]
             ).astype(proj.dtype)
         store(i).start()
         return carry
@@ -604,7 +631,7 @@
     gather.keep().wait()
 
 
-def project_attend(attn_rows, weight, bias, slopes, labels, own, n, collective_id):
+def project_attend(attn_rows, weight, vectors, slopes, labels, own, n, collective_id):
     total, depth = attn_rows.shape
     rows, width = own.shape[0], weight.shape[1]
     heads = width // (3 * HEAD_DIM)
@@ -623,6 +650,7 @@
         scratch_shapes=[
             pltpu.VMEM((total, width), jnp.bfloat16),
             pltpu.VMEM((2, rows, depth), jnp.bfloat16),
+            pltpu.VMEM((1, width), jnp.float32),
             dma((2,)),
             dma((n,)),
         ]
@@ -632,7 +660,7 @@
         ),
         cost_estimate=LINK_COST,
         name="project_attend",
-    )(slopes, own, attn_rows, weight, bias, labels[:, None, :])
+    )(slopes, own, attn_rows, weight, vectors, labels[:, None, :])
 
 
 def gelu_both(value):
@@ -645,7 +673,7 @@
 
 
 def expand_kernel(
-    n, own_ref, grad_hbm, up_ref, down_ref, bias_ref, rows_hbm, act_hbm, pre_hbm, sum_ref,
+    n, own_ref, grad_hbm, up_ref, down_ref, vectors_ref, rows_hbm, act_hbm, pre_hbm, sum_ref,
     gathered, grads, backs, act, pre, load_sem, act_sem, pre_sem, rows_sem, *sems
 ):
     gather = Gather(n, own_ref, gathered, sems)
@@ -710,7 +738,8 @@
 
         def columns(j, carry):
             cols = cols_of(j)
-            before = jnp.dot(gathered[here, :], up_ref[:, cols], preferred_element_type=jnp.float32) + bias_ref[:, cols]
+            before = jnp.dot(gathered[here, :], up_ref[:, cols], preferred_element_type=jnp.float32)
+            before = before + vectors_ref[UP_BIAS, :, cols]
             active, slope = gelu_both(before)
             act[slot, :, cols] = active.astype(act.dtype)
             rounded = (backs[i, :, cols].astype(jnp.float32) * slope).astype(pre.dtype)
@@ -737,7 +766,7 @@
     gather.finish_sends()
 
 
-def expand(own, grad_rows, up, down, bias, n, collective_id):
+def expand(own, grad_rows, up, down, vectors, n, collective_id):
     rows, depth = own.shape
     width = up.shape[1]
     total = n * rows
@@ -771,7 +800,7 @@
         ),
         cost_estimate=LINK_COST,
         name="expand",
-    )(own, grad_rows, up, down, bias)
+    )(own, grad_rows, up, down, vectors)
 
 
 class Product:
@@ -906,17 +935,17 @@
 
 
 def dense_kernel(
-    n, a_hbm, w_ref, input_hbm, bias_ref, gain_ref, shift_ref, out_ref, next_ref, inputs, input_sem, *scratch
+    n, a_hbm, w_ref, input_hbm, vectors_ref, out_ref, next_ref, inputs, input_sem, *scratch
 ):
     fetch = pltpu.make_async_copy(input_hbm, inputs, input_sem)
     fetch.start()
     scatter = Scatter(n, False, a_hbm, w_ref, out_ref, scratch)
 
     def work(at):
-        residual = inputs[at, :].astype(jnp.float32) + out_ref[at, :] + bias_ref[...]
+        residual = inputs[at, :].astype(jnp.float32) + out_ref[at, :] + vectors_ref[DENSE_BIAS]
         out_ref[at, :] = residual
         normed, _ = normal_rows(residual)
-        next_ref[at, :] = (normed * gain_ref[...] + shift_ref[...]).astype(next_ref.dtype)
+        next_ref[at, :] = (normed * vectors_ref[SECOND_GAIN] + vectors_ref[SECOND_SHIFT]).astype(next_ref.dtype)
 
     scatter.run(after=after_chunk(scatter, (fetch,), work))
 
@@ -938,7 +967,7 @@
 
 
 def expand_back_kernel(
-    n, a_hbm, w_ref, act_hbm, rows_hbm, residual_hbm, cotangent_hbm, gain_ref,
+    n, a_hbm, w_ref, act_hbm, rows_hbm, residual_hbm, cotangent_hbm, vectors_ref,
     out_ref, next_ref, sums_ref, grad_hbm, residual, cotangent, fetch_sem, *scratch
 ):
     fetches = (
@@ -955,7 +984,7 @@
     def work(at):
         grad = out_ref[at, :]
         other = cotangent[at, :].astype(jnp.float32)
-        back, terms = back_rows(grad, residual[at, :], gain_ref[...])
+        back, terms = back_rows(grad, residual[at, :], vectors_ref[SECOND_GAIN])
         result = other + back
         out_ref[at, :] = result
         next_ref[at, :] = result.astype(next_ref.dtype)
@@ -974,10 +1003,10 @@
 
 VMEM_SPEC = pl.BlockSpec(memory_space=pltpu.VMEM)
 HBM_SPEC = pl.BlockSpec(memory_space=pl.ANY)
-CHUNKS = 4
-
-
-def dense(mixed, weight, inputs, bias, gain, shift, n, collective_id):
+CHUNKS = 8
+
+
+def dense(mixed, weight, inputs, vectors, n, collective_id):
     rows, width = inputs.shape
     return pl.pallas_call(
         functools.partial(dense_kernel, n),
@@ -985,17 +1014,17 @@
             jax.ShapeDtypeStruct((rows, width), jnp.float32),
             jax.ShapeDtypeStruct((rows, width), jnp.bfloat16),
         ),
-        in_specs=[HBM_SPEC, VMEM_SPEC, HBM_SPEC, VMEM_SPEC, VMEM_SPEC, VMEM_SPEC],
+        in_specs=[HBM_SPEC, VMEM_SPEC, HBM_SPEC, VMEM_SPEC],
         out_specs=(VMEM_SPEC, VMEM_SPEC),
         scratch_shapes=[pltpu.VMEM((rows, width), inputs.dtype), pltpu.SemaphoreType.DMA(())]
         + scatter_scratch(n, rows, mixed.shape[1], width, CHUNKS),
         compiler_params=comm_params(collective_id),
         cost_estimate=LINK_COST,
         name="dense",
-    )(mixed, weight, inputs, bias, gain, shift)
-
-
-def expand_back(grad_pre, up, activated, grad_rows, residual, cotangent, gain, n, collective_id):
+    )(mixed, weight, inputs, vectors)
+
+
+def expand_back(grad_pre, up, activated, grad_rows, residual, cotangent, vectors, n, collective_id):
     rows, width = residual.shape
     units = activated.shape[1]
     return pl.pallas_call(
@@ -1018,7 +1047,7 @@
         compiler_params=comm_params(collective_id),
         cost_estimate=LINK_COST,
         name="expand_back",
-    )(grad_pre, up, activated, grad_rows, residual, cotangent, gain)
+    )(grad_pre, up, activated, grad_rows, residual, cotangent, vectors)
 
 
 def attend_back_one(slope, proj_ref, grad_ref, start, head, row_ref, out_ref, dk_ref, dv_ref, sums_ref, length):
@@ -1170,7 +1199,7 @@
 
 
 def shrink_kernel(
-    n, d, a_hbm, w_ref, residual_hbm, bias_ref, early_ref, up_sum_ref, head_sums_ref,
+    n, d, a_hbm, w_ref, residual_hbm, vectors_ref, early_ref, up_sum_ref, head_sums_ref,
     hidden_ref, sums_ref, biases_ref, out, residual, fetch_sem, *scratch
 ):
     fetch = pltpu.make_async_copy(residual_hbm, residual, fetch_sem)
@@ -1193,7 +1222,7 @@
                 flat.step(level)
 
     def work(at):
-        hidden_ref[at, :] = (residual[at, :] + out[at, :] + bias_ref[...]).astype(hidden_ref.dtype)
+        hidden_ref[at, :] = (residual[at, :] + out[at, :] + vectors_ref[DOWN_BIAS]).astype(hidden_ref.dtype)
 
     scatter.run(filler, after_chunk(scatter, (fetch,), work), d)
     for level in range(scatter.chunks, flat.levels + 1):
@@ -1202,7 +1231,7 @@
     sums_ref[...] = flat.finish()
 
 
-def shrink(activated, down, residual, bias, sums, up_sum, head_sums, n, d, collective_id):
+def shrink(activated, down, residual, vectors, sums, up_sum, head_sums, n, d, collective_id):
     rows, width = residual.shape
     units = up_sum.shape[1]
     return pl.pallas_call(
@@ -1225,11 +1254,11 @@
         compiler_params=comm_params(collective_id),
         cost_estimate=LINK_COST,
         name="shrink",
-    )(activated, down, residual, bias, sums, up_sum, head_sums)
+    )(activated, down, residual, vectors, sums, up_sum, head_sums)
 
 
 def project_back_kernel(
-    n, a_hbm, w_ref, input_hbm, grad_hbm, gain_ref, early_ref, left_hbm,
+    n, a_hbm, w_ref, input_hbm, grad_hbm, vectors_ref, early_ref, left_hbm,
     out_ref, sums_ref, weight_hbm, inputs, grads, fetch_sem, *scratch
 ):
     fetches = (
@@ -1245,7 +1274,7 @@
 
     def work(at):
         grad = out_ref[at, :]
-        back, terms = back_rows(grad, inputs[at, :].astype(jnp.float32), gain_ref[...])
+        back, terms = back_rows(grad, inputs[at, :].astype(jnp.float32), vectors_ref[FIRST_GAIN])
         out_ref[at, :] = grads[at, :] + back
         sums_ref[4:5, :] += column_sum(terms)
         sums_ref[5:6, :] += column_sum(grad)
@@ -1254,7 +1283,7 @@
     product.finish()
 
 
-def project_back(grad_proj, weight, inputs, grad_residual, gain, early, attn_rows, n, collective_id):
+def project_back(grad_proj, weight, inputs, grad_residual, vectors, early, attn_rows, n, collective_id):
     rows, width = inputs.shape
     columns = grad_proj.shape[1]
     return pl.pallas_call(
@@ -1276,14 +1305,7 @@
         compiler_params=comm_params(collective_id),
         cost_estimate=LINK_COST,
         name="project_back",
-    )(grad_proj, weight, inputs, grad_residual, gain, early, attn_rows)
-
-
-HEADS = 16
-
-
-def wide(vector):
-    return vector.astype(jnp.float32)[None]
+    )(grad_proj, weight, inputs, grad_residual, vectors, early, attn_rows)
 
 
 def share(grad, dimension):
@@ -1306,7 +1328,7 @@
 
 
 def finish(hidden_output, grad_input, weights, sums, biases, heads_width):
-    steps = 8
+    steps = 2
 
     def rows_block(x):
         return pl.BlockSpec((x.shape[0] // steps, x.shape[1]), lambda i: (i, 0))
@@ -1352,7 +1374,22 @@
     d,
 ):
     heads_local = query_bias.shape[0] // HEAD_DIM
-    attn_rows = gather_rows(hidden_input, wide(first_gain), wide(first_shift), n, 1)
+    attn_rows, vectors = gather_rows(
+        hidden_input,
+        (
+            first_gain,
+            first_shift,
+            dense_bias,
+            second_gain,
+            second_shift,
+            down_bias,
+            up_bias,
+            query_bias,
+            value_bias,
+        ),
+        n,
+        1,
+    )
     project_full, dense_full, expand_full, shrink_full = (
         lax.all_gather(qkv_weight, "dp", axis=0, tiled=True),
         lax.all_gather(dense_weight, "dp", axis=1, tiled=True),
@@ -1369,22 +1406,17 @@
     position = lax.broadcasted_iota(jnp.int32, (sequences, length), 1)
     filled = jnp.sum(document_lengths, axis=1, keepdims=True)
     labels = jnp.where(position < filled, segments.reshape(sequences, length), length + position).astype(jnp.float32)
-    query_bias32 = query_bias.astype(jnp.float32).reshape(heads_local, HEAD_DIM)
-    value_bias32 = value_bias.astype(jnp.float32).reshape(heads_local, HEAD_DIM)
-    proj_bias = jnp.stack((query_bias32, jnp.zeros_like(query_bias32), value_bias32), axis=1).reshape(
-        heads_local * 3 * HEAD_DIM
-    )
     grad_rows, proj, mixed = project_attend(
-        attn_rows, project_full, proj_bias[None], slopes, labels, cotangent, n, 6
+        attn_rows, project_full, vectors, slopes, labels, cotangent, n, 6
     )
     residual, mlp_input = dense(
-        mixed, dense_full, hidden_input, wide(dense_bias), wide(second_gain), wide(second_shift), n, 2
+        mixed, dense_full, hidden_input, vectors, n, 2
     )
     mlp_rows, activated, grad_pre, sum_up_bias = expand(
-        mlp_input, grad_rows, expand_full, shrink_full, wide(up_bias), n, 7
+        mlp_input, grad_rows, expand_full, shrink_full, vectors, n, 7
     )
     grad_residual, grad_attn_out, early_sums, grad_down = expand_back(
-        grad_pre, expand_full, activated, grad_rows, residual, cotangent, wide(second_gain), n, 4
+        grad_pre, expand_full, activated, grad_rows, residual, cotangent, vectors, n, 4
     )
     grad_down_weight = share(grad_down, 1)
     grad_proj, head_sums, grad_dense, grad_up = dense_back(
@@ -1394,11 +1426,11 @@
     grad_up_weight = share(grad_up, 0)
     grad_dense_weight = share(grad_dense, 1)
     grad_input, sums, grad_project = project_back(
-        grad_proj, project_full, hidden_input, grad_residual, wide(first_gain), early_sums, attn_rows, n, 5
+        grad_proj, project_full, hidden_input, grad_residual, vectors, early_sums, attn_rows, n, 5
     )
     grad_qkv_weight = share(grad_project, 0)
     hidden_output, sums, biases = shrink(
-        activated, shrink_full, residual, wide(down_bias), sums, sum_up_bias, head_sums, n, d, 3
+        activated, shrink_full, residual, vectors, sums, sum_up_bias, head_sums, n, d, 3
     )
     heads_width = heads_local * HEAD_DIM
     large, small = finish(

time: 736 us -> 731 us (level)
  waiting for transfers between devices: 4.22 us -> 15.1 us
  other arithmetic: 11.7 us -> 2.02 us
    all_gather x1, waiting for transfers between devices: 0.02 us -> 11.7 us  [on_device(): lax.all_gather(down_weight, 'dp', axis=1, tiled=True)]
    broadcast_in_dim x7 -> x0, other arithmetic: 8.31 us -> none  [wide(): return vector.astype(jnp.float32)[None]]
  transfers between devices with their start and end apart: 8 -> 8, of which waited for: 1 -> 1; matrix products, arithmetic and copies ran while one was open for 2% -> 0% of each run, Pallas kernels for 70% -> 69%
where the time goes in v7:
time: 731 us; the launch traced here: 730 us
  Pallas kernels  698 us (95%)
  waiting for transfers between devices  15.1 us (2%)
  between operations  14.3 us (2%)
    pallas_call x1, Pallas kernels, expand_back(): pl.pallas_call(functools.partial(expand_back_kernel, n), out_shape=(jax.S...  98.4 us
    pallas_call x1, Pallas kernels, project_back(): pl.pallas_call(functools.partial(project_back_kernel, n), out_shape=(jax....  89.9 us
    pallas_call x1, Pallas kernels, dense_back(): pl.pallas_call(functools.partial(dense_back_kernel, n, length), out_shape...  89.4 us
    pallas_call x1, Pallas kernels, expand(): pl.pallas_call(functools.partial(expand_kernel, n), out_shape=(jax.ShapeD...  85.1 us
    pallas_call x1, Pallas kernels, shrink(): pl.pallas_call(functools.partial(shrink_kernel, n, d), out_shape=(jax.Sha...  84.8 us
    pallas_call x1, Pallas kernels, dense(): pl.pallas_call(functools.partial(dense_kernel, n), out_shape=(jax.ShapeDt...  81.9 us
    pallas_call x1, Pallas kernels, gather_rows(): pl.pallas_call(functools.partial(gather_kernel, n), out_shape=(jax.ShapeD...  81.8 us
    pallas_call x1, Pallas kernels, project_attend(): pl.pallas_call(functools.partial(project_kernel, n, labels.shape[1]), out...  78.9 us
  transfers between devices with their start and end apart: 8, of which 1 were waited for; matrix products, arithmetic and copies ran while one was open for 0% of the time, Pallas kernels for 69%

profile of v7, /device:TPU:0, one launch (start us, length us, event | category | flops | bytes accessed | tf_op | source)
XLA Modules:
  0.0 730.0 jit_solution(10607590380123327877)
XLA Ops:
  7.2 0.7 all-gather.5.cloned.1.call-update
  8.0 0.7 all-gather.7.cloned.1.call-update
  8.7 0.0 all-gather.9.cloned.1.call-start
  8.7 0.7 all-gather.9.cloned.1.call-update
  9.4 0.0 all-gather.11.cloned.1.call-start
  9.5 0.5 all-gather.11.cloned.1.call-update
  10.0 0.0 reduce-scatter.5.cloned.1.call-start
  10.0 0.8 reduce_sum.9
  10.8 81.8 %gather_rows.1 = (bf16[4096,2048]{1,0:T(8,128)(2,1)}, f32[8,1,2048]{2,1,0:T(1,128)}) custom-call(bf16[512,2048]{1,0:T(8,128)(2,1)} %input_hbm.3, bf16[2048]{0:T(1024)(128)(2,1)} %refs_0_.1, bf16[2048]{0:T(1024)(128)(2,1)} %refs_1_.1, bf16[2048]{0:T(1024)(128)(2,1)} %refs_2_.1, bf16[2048]{0:T(1024)(128)(2,1)} %refs_3_.1, bf16[2048]{0:T(1024)(128)(2,1)} %refs_4_.1, ...), custom_call_target="tpu_custom_call" | custom-call | bytes 280000000 | tf_op jit(solution)/shard_map/gather_rows/pallas_call | solution.py:218
  92.6 0.5 exponential_multiply_fusion.slope_ref
  93.2 0.7 fusion.row_ref
  93.9 78.9 %project_attend.1 = (bf16[4096,2048]{1,0:T(8,128)(2,1)}, bf16[4096,768]{1,0:T(8,128)(2,1)}, bf16[4096,256]{1,0:T(8,128)(2,1)}) custom-call(f32[2]{0:T(128)} %exponential_multiply_fusion.slope_ref, bf16[512,2048]{1,0:T(8,128)(2,1)} %cotangent_hbm.1, bf16[4096,2048]{1,0:T(8,128)(2,1)} %get-tuple-element.57.rows_hbm.left_hbm, ...), custom_call_target="tpu_custom_call" | custom-call | bytes 280000000 | tf_op jit(solution)/shard_map/project_attend/pallas_call | solution.py:641
  172.8 81.9 %dense.1 = (f32[512,2048]{1,0:T(8,128)}, bf16[512,2048]{1,0:T(8,128)(2,1)}) custom-call(bf16[4096,256]{1,0:T(8,128)(2,1)} %get-tuple-element.59.a_hbm.mixed_ref, bf16[256,2048]{1,0:T(8,128)(2,1)} %all-gather.7.cloned.1.call-done.w_ref, bf16[512,2048]{1,0:T(8,128)(2,1)} %input_hbm.3, f32[8,1,2048]{2,1,0:T(1,128)} %get-tuple-element.58.vectors_ref), custom_call_target="tpu_custom_call" | custom-call | bytes 280000000 | tf_op jit(solution)/shard_map/dense/pallas_call | solution.py:1011
  254.8 11.7 %all-gather.11.cloned.1.call-done.down_ref.w_ref = bf16[1024,2048]{1,0:T(8,128)(2,1)} async-done(((bf16[1024,512]{1,0:T(8,128)(2,1)}), bf16[1024,2048]{1,0:T(8,128)(2,1)}) %all-gather.11.cloned.1.call-update) | async-done | bytes 4194320 | tf_op jit(solution)/shard_map/all_gather | solution.py:1397
  266.5 85.1 %expand.1 = (bf16[4096,2048]{1,0:T(8,128)(2,1)}, bf16[4096,1024]{1,0:T(8,128)(2,1)}, bf16[4096,1024]{1,0:T(8,128)(2,1)}, f32[1,1024]{1,0:T(1,128)}) custom-call(bf16[512,2048]{1,0:T(8,128)(2,1)} %get-tuple-element.60.own_ref, bf16[4096,2048]{1,0:T(8,128)(2,1)} %get-tuple-element.61.grad_hbm.rows_hbm, ...), custom_call_target="tpu_custom_call" | custom-call | bytes 280000000 | tf_op jit(solution)/shard_map/expand/pallas_call | solution.py:776
  351.6 98.4 %expand_back.1 = (f32[512,2048]{1,0:T(8,128)}, bf16[512,2048]{1,0:T(8,128)(2,1)}, f32[8,2048]{1,0:T(8,128)}, bf16[1024,2048]{1,0:T(8,128)(2,1)}) custom-call(bf16[4096,1024]{1,0:T(8,128)(2,1)} %get-tuple-element.64.a_hbm.right_hbm, bf16[2048,1024]{1,0:T(8,128)(2,1)} %all-gather.9.cloned.1.call-done.up_ref.w_ref, ...), custom_call_target="tpu_custom_call" | custom-call | bytes 280000000 | tf_op jit(solution)/shard_map/expand_back/pallas_call | solution.py:1030
  450.0 0.2 reduce-scatter.9.cloned.1.call-start
  450.2 89.4 %dense_back.1 = (bf16[4096,768]{1,0:T(8,128)(2,1)}, f32[8,256]{1,0:T(8,128)}, bf16[256,2048]{1,0:T(8,128)(2,1)}, bf16[2048,1024]{1,0:T(8,128)(2,1)}) custom-call(f32[2]{0:T(128)} %exponential_multiply_fusion.slope_ref, bf16[512,2048]{1,0:T(8,128)(2,1)} %get-tuple-element.66.own_ref, bf16[4096,256]{1,0:T(8,128)(2,1)} %get-tuple-element.59.a_hbm.mixed_ref, ...), custom_call_target="tpu_custom_call" | custom-call | bytes 280000000 | tf_op jit(solution)/shard_map/dense_back/pallas_call | solution.py:1172
  539.6 0.0 reduce-scatter.11.cloned.1.call-start
  539.7 0.7 reduce-scatter.11.cloned.1.call-update
  540.4 0.0 reduce-scatter.7.cloned.1.call-start
  540.4 89.9 %project_back.1 = (f32[512,2048]{1,0:T(8,128)}, f32[8,2048]{1,0:T(8,128)}, bf16[2048,768]{1,0:T(8,128)(2,1)}) custom-call(bf16[4096,768]{1,0:T(8,128)(2,1)} %get-tuple-element.70.a_hbm, bf16[2048,768]{1,0:T(8,128)(2,1)} %all-gather.5.cloned.1.call-done.w_ref, bf16[512,2048]{1,0:T(8,128)(2,1)} %input_hbm.3, f32[512,2048]{1,0:T(8,128)} %get-tuple-element.71.grad_hbm, ...), custom_call_target="tpu_custom_call" | custom-call | bytes 280000000 | tf_op jit(solution)/shard_map/project_back/pallas_call | solution.py:1289
  630.4 84.8 %shrink.1 = (bf16[512,2048]{1,0:T(8,128)(2,1)}, f32[8,2048]{1,0:T(8,128)}, f32[8,1024]{1,0:T(8,128)}) custom-call(bf16[4096,1024]{1,0:T(8,128)(2,1)} %get-tuple-element.62.act_hbm.a_hbm, bf16[1024,2048]{1,0:T(8,128)(2,1)} %all-gather.11.cloned.1.call-done.down_ref.w_ref, f32[512,2048]{1,0:T(8,128)} %get-tuple-element.63.residual_hbm, ...), custom_call_target="tpu_custom_call" | custom-call | bytes 280000000 | tf_op jit(solution)/shard_map/shrink/pallas_call | solution.py:1237
  715.2 7.9 %finish.1 = (bf16[512,2048]{1,0:T(8,128)(2,1)}, f32[512,2048]{1,0:T(8,128)}, f32[512,768]{1,0:T(8,128)}, f32[256,512]{1,0:T(8,128)}, f32[512,1024]{1,0:T(8,128)}...) custom-call(bf16[512,2048]{1,0:T(8,128)(2,1)} %get-tuple-element.76., ...), custom_call_target="tpu_custom_call" | custom-call | tf_op jit(solution)/shard_map/finish/pallas_call | solution.py:1341
  (15 shorter events, 0.3 us)
Async XLA Ops:
  7.2 86.0 %copy-start = (s32[4096]{0:T(1024)S(1)}, s32[4096]{0:T(1024)}, u32[]{:S(2)}) copy-start(s32[4096]{0:T(1024)} %param.31) | copy-start | bytes 49156
  7.2 86.7 %all-gather.5.cloned.1.call-start = ((), (), s32[]{:S(2)}) async-start(), calls=%async_computation.4 | async-start | bytes 3932160 | tf_op jit(solution)/shard_map/all_gather | solution.py:1394
  7.9 164.9 %all-gather.7.cloned.1.call-start = ((), (), s32[]{:S(2)}) async-start(), calls=%async_computation.5 | async-start | bytes 1310720 | tf_op jit(solution)/shard_map/all_gather | solution.py:1395
  8.7 246.1 %all-gather.9.cloned.1.call-start = ((), (), s32[]{:S(2)}) async-start(), calls=%async_computation.6 | async-start | bytes 5242880 | tf_op jit(solution)/shard_map/all_gather | solution.py:1396
  9.4 257.0 %all-gather.11.cloned.1.call-start = ((), (), s32[]{:S(2)}) async-start(), calls=%async_computation.7 | async-start | bytes 5242880 | tf_op jit(solution)/shard_map/all_gather | solution.py:1397
  10.0 530.5 %reduce-scatter.5.cloned.1.call-start = ((), (), s32[]{:S(2)}) async-start(), calls=%async_computation.8 | async-start | bytes 5242880 | tf_op jit(solution)/shard_map/reduce_scatter | solution.py:1312
  450.0 265.2 %reduce-scatter.9.cloned.1.call-start = ((), (), s32[]{:S(2)}) async-start(), calls=%async_computation.10 | async-start | bytes 1310720 | tf_op jit(solution)/shard_map/reduce_scatter | solution.py:1312
  539.6 175.6 %reduce-scatter.11.cloned.1.call-start = ((), (), s32[]{:S(2)}) async-start(), calls=%async_computation.11 | async-start | bytes 5242880 | tf_op jit(solution)/shard_map/reduce_scatter | solution.py:1312
  540.4 174.9 %reduce-scatter.7.cloned.1.call-start = ((), (), s32[]{:S(2)}) async-start(), calls=%async_computation.9 | async-start | bytes 3932160 | tf_op jit(solution)/shard_map/reduce_scatter | solution.py:1312
Sparse Core Ops, SparseCore 0:
  9.6 66.1 all-gather.4
  77.3 26.6 all-gather.6
  105.6 80.1 all-gather.8
  187.1 79.2 all-gather.10
  450.1 74.4 reduce-scatter.4
  539.7 25.0 reduce-scatter.8
  567.1 75.2 reduce-scatter.10
  644.7 65.5 reduce-scatter.6

commit v8 on v7

--- a/solution.py
+++ b/solution.py
@@ -140,8 +140,8 @@
         rows = pl.ds(pl.multiple_of(self.me * self.rows, self.rows), self.rows)
         return pltpu.make_async_copy(self.own, self.out.at[rows, :], self.own_sem)
 
-    def start(self, meanwhile=None):
-        greet(self.me, self.bits, meanwhile=meanwhile)
+    def start(self, meanwhile=None, d=1):
+        greet(self.me, self.bits, d, meanwhile)
         for step in range(self.bits):
             for part in range(self.bits):
                 self.chip_copy(part, 0, step).start()
@@ -176,8 +176,53 @@
                 self.core_copy(part, index).wait_send()
 
 
-def gather_kernel(n, x_ref, *refs):
-    flat_refs, (out_ref, vectors_ref, own, *sems) = refs[:9], refs[9:]
+class Spread:
+    def __init__(self, d, shard, full, sems):
+        self.d, self.shard, self.full = d, shard, full
+        self.own_sem, self.send_sem, self.recv_sem = sems
+        self.z = lax.axis_index("dp")
+
+    def columns(self, z):
+        width = self.shard.shape[1]
+        return self.full.at[:, pl.ds(pl.multiple_of(z * width, width), width)]
+
+    def copy(self, ahead):
+        return pltpu.make_async_remote_copy(
+            src_ref=self.shard,
+            dst_ref=self.columns(self.z),
+            send_sem=self.send_sem.at[ahead],
+            recv_sem=self.recv_sem.at[ahead],
+            device_id=ahead_on_dp(ahead, self.d),
+            device_id_type=pl.DeviceIdType.MESH,
+        )
+
+    def keep(self):
+        return pltpu.make_async_copy(self.shard, self.columns(self.z), self.own_sem)
+
+    def start(self):
+        for ahead in range(1, self.d):
+            self.copy(ahead).start()
+        self.keep().start()
+
+    def finish(self):
+        for ahead in range(1, self.d):
+            arrived = self.columns(lax.rem(self.z + self.d - ahead, self.d))
+            pltpu.make_async_remote_copy(
+                src_ref=self.shard,
+                dst_ref=arrived,
+                send_sem=self.send_sem.at[ahead],
+                recv_sem=self.recv_sem.at[ahead],
+                device_id=ahead_on_dp(ahead, self.d),
+                device_id_type=pl.DeviceIdType.MESH,
+            ).wait_recv()
+            self.copy(ahead).wait_send()
+        self.keep().wait()
+
+
+def gather_kernel(n, d, x_ref, *refs):
+    flat_refs, (shard_ref, out_ref, vectors_ref, full_ref, own, *sems) = refs[:9], refs[9:]
+    spread = Spread(d, shard_ref, full_ref, sems[:3])
+    sems = sems[3:]
 
     def put(row, start, ref):
         size = ref.shape[0]
@@ -191,7 +236,8 @@
         own[at, :] = (normed * vectors_ref[FIRST_GAIN] + vectors_ref[FIRST_SHIFT]).astype(own.dtype)
 
     gather = Gather(n, own, out_ref, sems)
-    gather.start(lambda: row_blocks(0, own.shape[0], 32, work))
+    gather.start(lambda: row_blocks(0, own.shape[0], 32, work), d)
+    spread.start()
     for row in range(FIRST_SHIFT + 1, UP_BIAS):
         put(row, 0, flat_refs[row])
     vectors_ref[UP_BIAS] = jnp.zeros(vectors_ref.shape[1:], jnp.float32)
@@ -204,6 +250,7 @@
     for mask in range(2**gather.bits):
         gather.wait_core(mask)
     gather.finish_sends()
+    spread.finish()
     gather.keep().wait()
 
 
@@ -213,23 +260,30 @@
     return [dma(())] + [dma((bits, 2**bits))] * 4
 
 
-def gather_rows(x, vectors, n, collective_id):
+def gather_rows(x, vectors, shard, n, d, collective_id):
     rows, width = x.shape
     return pl.pallas_call(
-        functools.partial(gather_kernel, n),
+        functools.partial(gather_kernel, n, d),
         out_shape=(
             jax.ShapeDtypeStruct((n * rows, width), x.dtype),
             jax.ShapeDtypeStruct((8, 1, width), jnp.float32),
+            jax.ShapeDtypeStruct((shard.shape[0], d * shard.shape[1]), shard.dtype),
         ),
-        in_specs=[VMEM_SPEC] * 10,
-        out_specs=(HBM_SPEC, VMEM_SPEC),
-        scratch_shapes=[pltpu.VMEM((rows, width), x.dtype)] + gather_sems(n),
+        in_specs=[VMEM_SPEC] * 11,
+        out_specs=(HBM_SPEC, VMEM_SPEC, HBM_SPEC),
+        scratch_shapes=[
+            pltpu.VMEM((rows, width), x.dtype),
+            pltpu.SemaphoreType.DMA(()),
+            pltpu.SemaphoreType.DMA((d,)),
+            pltpu.SemaphoreType.DMA((d,)),
+        ]
+        + gather_sems(n),
         compiler_params=pltpu.CompilerParams(
             collective_id=collective_id, has_side_effects=True, vmem_limit_bytes=VMEM_LIMIT
         ),
         cost_estimate=LINK_COST,
         name="gather_rows",
-    )(x, *vectors)
+    )(x, *vectors, shard)
 
 
 class Scatter:
@@ -1004,6 +1058,7 @@
 VMEM_SPEC = pl.BlockSpec(memory_space=pltpu.VMEM)
 HBM_SPEC = pl.BlockSpec(memory_space=pl.ANY)
 CHUNKS = 8
+FILLED_CHUNKS = 4
 
 
 def dense(mixed, weight, inputs, vectors, n, collective_id):
@@ -1043,7 +1098,7 @@
             pltpu.SemaphoreType.DMA((2,)),
         ]
         + product_scratch(n * rows, units, width)
-        + scatter_scratch(n, rows, units, width, CHUNKS),
+        + scatter_scratch(n, rows, units, width, FILLED_CHUNKS),
         compiler_params=comm_params(collective_id),
         cost_estimate=LINK_COST,
         name="expand_back",
@@ -1374,7 +1429,7 @@
     d,
 ):
     heads_local = query_bias.shape[0] // HEAD_DIM
-    attn_rows, vectors = gather_rows(
+    attn_rows, vectors, dense_full = gather_rows(
         hidden_input,
         (
             first_gain,
@@ -1387,12 +1442,13 @@
             query_bias,
             value_bias,
         ),
+        dense_weight,
         n,
+        d,
         1,
     )
-    project_full, dense_full, expand_full, shrink_full = (
+    project_full, expand_full, shrink_full = (
         lax.all_gather(qkv_weight, "dp", axis=0, tiled=True),
-        lax.all_gather(dense_weight, "dp", axis=1, tiled=True),
         lax.all_gather(up_weight, "dp", axis=0, tiled=True),
         lax.all_gather(down_weight, "dp", axis=1, tiled=True),
     )

time: 731 us -> 718 us (0.982)
  waiting for transfers between devices: 15.1 us -> 5.19 us
    all_gather x1, waiting for transfers between devices: 11.7 us -> 1.84 us  [on_device(): lax.all_gather(down_weight, 'dp', axis=1, tiled=True)]
  transfers between devices with their start and end apart: 8 -> 7, of which waited for: 1 -> 2; matrix products, arithmetic and copies ran while one was open for 0% -> 0% of each run, Pallas kernels for 69% -> 71%
where the time goes in v8:
time: 718 us; the launch traced here: 717 us
  Pallas kernels  695 us (97%)
  between operations  14.3 us (2%)
    pallas_call x1, Pallas kernels, expand_back(): pl.pallas_call(functools.partial(expand_back_kernel, n), out_shape=(jax.S...  95.4 us
    pallas_call x1, Pallas kernels, project_back(): pl.pallas_call(functools.partial(project_back_kernel, n), out_shape=(jax....  90.5 us
    pallas_call x1, Pallas kernels, dense_back(): pl.pallas_call(functools.partial(dense_back_kernel, n, length), out_shape...  89.7 us
    pallas_call x1, Pallas kernels, expand(): pl.pallas_call(functools.partial(expand_kernel, n), out_shape=(jax.ShapeD...  85.2 us
    pallas_call x1, Pallas kernels, shrink(): pl.pallas_call(functools.partial(shrink_kernel, n, d), out_shape=(jax.Sha...  84.1 us
    pallas_call x1, Pallas kernels, gather_rows(): pl.pallas_call(functools.partial(gather_kernel, n, d), out_shape=(jax.Sha...  82 us
    pallas_call x1, Pallas kernels, dense(): pl.pallas_call(functools.partial(dense_kernel, n), out_shape=(jax.ShapeDt...  81 us
    pallas_call x1, Pallas kernels, project_attend(): pl.pallas_call(functools.partial(project_kernel, n, labels.shape[1]), out...  79.5 us
  transfers between devices with their start and end apart: 7, of which 2 were waited for; matrix products, arithmetic and copies ran while one was open for 0% of the time, Pallas kernels for 71%

profile of v8, /device:TPU:0, one launch (start us, length us, event | category | flops | bytes accessed | tf_op | source)
XLA Modules:
  0.0 717.3 jit_solution(17597313152422980154)
XLA Ops:
  7.2 0.7 all-gather.4.cloned.1.call-update
  7.9 0.0 all-gather.6.cloned.1.call-start
  8.0 0.7 all-gather.6.cloned.1.call-update
  8.7 0.0 all-gather.8.cloned.1.call-start
  8.7 0.7 all-gather.8.cloned.1.call-update
  9.4 0.0 reduce-scatter.5.cloned.1.call-start
  9.5 0.8 reduce_sum.9
  10.3 82.0 %gather_rows.1 = (bf16[4096,2048]{1,0:T(8,128)(2,1)}, f32[8,1,2048]{2,1,0:T(1,128)}, bf16[256,2048]{1,0:T(8,128)(2,1)}) custom-call(bf16[512,2048]{1,0:T(8,128)(2,1)} %input_hbm.3, bf16[2048]{0:T(1024)(128)(2,1)} %refs_0_.1, bf16[2048]{0:T(1024)(128)(2,1)} %refs_1_.1, bf16[2048]{0:T(1024)(128)(2,1)} %refs_2_.1, bf16[2048]{0:T(1024)(128)(2,1)} %refs_3_.1, ...), custom_call_target="tpu_custom_call" | custom-call | bytes 280000000 | tf_op jit(solution)/shard_map/gather_rows/pallas_call | solution.py:265
  92.2 0.5 exponential_multiply_fusion.slope_ref
  92.8 0.7 fusion.row_ref
  93.4 0.6 all-gather.4.cloned.1.call-done.w_ref
  94.1 79.5 %project_attend.1 = (bf16[4096,2048]{1,0:T(8,128)(2,1)}, bf16[4096,768]{1,0:T(8,128)(2,1)}, bf16[4096,256]{1,0:T(8,128)(2,1)}) custom-call(f32[2]{0:T(128)} %exponential_multiply_fusion.slope_ref, bf16[512,2048]{1,0:T(8,128)(2,1)} %cotangent_hbm.1, bf16[4096,2048]{1,0:T(8,128)(2,1)} %get-tuple-element.58.rows_hbm.left_hbm, ...), custom_call_target="tpu_custom_call" | custom-call | bytes 280000000 | tf_op jit(solution)/shard_map/project_attend/pallas_call | solution.py:695
  173.6 81.0 %dense.1 = (f32[512,2048]{1,0:T(8,128)}, bf16[512,2048]{1,0:T(8,128)(2,1)}) custom-call(bf16[4096,256]{1,0:T(8,128)(2,1)} %get-tuple-element.60.a_hbm.mixed_ref, bf16[256,2048]{1,0:T(8,128)(2,1)} %get-tuple-element.61.w_ref, bf16[512,2048]{1,0:T(8,128)(2,1)} %input_hbm.3, f32[8,1,2048]{2,1,0:T(1,128)} %get-tuple-element.59.vectors_ref), custom_call_target="tpu_custom_call" | custom-call | bytes 280000000 | tf_op jit(solution)/shard_map/dense/pallas_call | solution.py:1066
  254.6 1.8 all-gather.8.cloned.1.call-done.down_ref.w_ref
  256.4 85.2 %expand.1 = (bf16[4096,2048]{1,0:T(8,128)(2,1)}, bf16[4096,1024]{1,0:T(8,128)(2,1)}, bf16[4096,1024]{1,0:T(8,128)(2,1)}, f32[1,1024]{1,0:T(1,128)}) custom-call(bf16[512,2048]{1,0:T(8,128)(2,1)} %get-tuple-element.62.own_ref, bf16[4096,2048]{1,0:T(8,128)(2,1)} %get-tuple-element.63.grad_hbm.rows_hbm, ...), custom_call_target="tpu_custom_call" | custom-call | bytes 280000000 | tf_op jit(solution)/shard_map/expand/pallas_call | solution.py:830
  341.7 95.4 %expand_back.1 = (f32[512,2048]{1,0:T(8,128)}, bf16[512,2048]{1,0:T(8,128)(2,1)}, f32[8,2048]{1,0:T(8,128)}, bf16[1024,2048]{1,0:T(8,128)(2,1)}) custom-call(bf16[4096,1024]{1,0:T(8,128)(2,1)} %get-tuple-element.66.a_hbm.right_hbm, bf16[2048,1024]{1,0:T(8,128)(2,1)} %all-gather.6.cloned.1.call-done.up_ref.w_ref, ...), custom_call_target="tpu_custom_call" | custom-call | bytes 280000000 | tf_op jit(solution)/shard_map/expand_back/pallas_call | solution.py:1085
  437.1 0.2 reduce-scatter.9.cloned.1.call-start
  437.4 89.7 %dense_back.1 = (bf16[4096,768]{1,0:T(8,128)(2,1)}, f32[8,256]{1,0:T(8,128)}, bf16[256,2048]{1,0:T(8,128)(2,1)}, bf16[2048,1024]{1,0:T(8,128)(2,1)}) custom-call(f32[2]{0:T(128)} %exponential_multiply_fusion.slope_ref, bf16[512,2048]{1,0:T(8,128)(2,1)} %get-tuple-element.68.own_ref, bf16[4096,256]{1,0:T(8,128)(2,1)} %get-tuple-element.60.a_hbm.mixed_ref, ...), custom_call_target="tpu_custom_call" | custom-call | bytes 280000000 | tf_op jit(solution)/shard_map/dense_back/pallas_call | solution.py:1227
  527.2 0.0 reduce-scatter.11.cloned.1.call-start
  527.2 0.5 reduce-scatter.11.cloned.1.call-update
  527.7 0.0 reduce-scatter.7.cloned.1.call-start
  527.8 90.5 %project_back.1 = (f32[512,2048]{1,0:T(8,128)}, f32[8,2048]{1,0:T(8,128)}, bf16[2048,768]{1,0:T(8,128)(2,1)}) custom-call(bf16[4096,768]{1,0:T(8,128)(2,1)} %get-tuple-element.72.a_hbm, bf16[2048,768]{1,0:T(8,128)(2,1)} %all-gather.4.cloned.1.call-done.w_ref, bf16[512,2048]{1,0:T(8,128)(2,1)} %input_hbm.3, f32[512,2048]{1,0:T(8,128)} %get-tuple-element.73.grad_hbm, ...), custom_call_target="tpu_custom_call" | custom-call | bytes 280000000 | tf_op jit(solution)/shard_map/project_back/pallas_call | solution.py:1344
  618.3 84.1 %shrink.1 = (bf16[512,2048]{1,0:T(8,128)(2,1)}, f32[8,2048]{1,0:T(8,128)}, f32[8,1024]{1,0:T(8,128)}) custom-call(bf16[4096,1024]{1,0:T(8,128)(2,1)} %get-tuple-element.64.act_hbm.a_hbm, bf16[1024,2048]{1,0:T(8,128)(2,1)} %all-gather.8.cloned.1.call-done.down_ref.w_ref, f32[512,2048]{1,0:T(8,128)} %get-tuple-element.65.residual_hbm, ...), custom_call_target="tpu_custom_call" | custom-call | bytes 280000000 | tf_op jit(solution)/shard_map/shrink/pallas_call | solution.py:1292
  702.5 7.9 %finish.1 = (bf16[512,2048]{1,0:T(8,128)(2,1)}, f32[512,2048]{1,0:T(8,128)}, f32[512,768]{1,0:T(8,128)}, f32[256,512]{1,0:T(8,128)}, f32[512,1024]{1,0:T(8,128)}...) custom-call(bf16[512,2048]{1,0:T(8,128)(2,1)} %get-tuple-element.78., ...), custom_call_target="tpu_custom_call" | custom-call | tf_op jit(solution)/shard_map/finish/pallas_call | solution.py:1396
  (12 shorter events, 0.2 us)
Async XLA Ops:
  7.2 85.6 %copy-start = (s32[4096]{0:T(1024)S(1)}, s32[4096]{0:T(1024)}, u32[]{:S(2)}) copy-start(s32[4096]{0:T(1024)} %param.31) | copy-start | bytes 49156
  7.2 86.9 %all-gather.4.cloned.1.call-start = ((), (), s32[]{:S(2)}) async-start(), calls=%async_computation.4 | async-start | bytes 3932160 | tf_op jit(solution)/shard_map/all_gather | solution.py:1451
  7.9 246.7 %all-gather.6.cloned.1.call-start = ((), (), s32[]{:S(2)}) async-start(), calls=%async_computation.5 | async-start | bytes 5242880 | tf_op jit(solution)/shard_map/all_gather | solution.py:1452
  8.7 247.8 %all-gather.8.cloned.1.call-start = ((), (), s32[]{:S(2)}) async-start(), calls=%async_computation.6 | async-start | bytes 5242880 | tf_op jit(solution)/shard_map/all_gather | solution.py:1453
  9.4 518.4 %reduce-scatter.5.cloned.1.call-start = ((), (), s32[]{:S(2)}) async-start(), calls=%async_computation.7 | async-start | bytes 5242880 | tf_op jit(solution)/shard_map/reduce_scatter | solution.py:1367
  437.1 265.2 %reduce-scatter.9.cloned.1.call-start = ((), (), s32[]{:S(2)}) async-start(), calls=%async_computation.9 | async-start | bytes 1310720 | tf_op jit(solution)/shard_map/reduce_scatter | solution.py:1367
  527.2 175.3 %reduce-scatter.11.cloned.1.call-start = ((), (), s32[]{:S(2)}) async-start(), calls=%async_computation.10 | async-start | bytes 5242880 | tf_op jit(solution)/shard_map/reduce_scatter | solution.py:1367
  527.7 174.7 %reduce-scatter.7.cloned.1.call-start = ((), (), s32[]{:S(2)}) async-start(), calls=%async_computation.8 | async-start | bytes 3932160 | tf_op jit(solution)/shard_map/reduce_scatter | solution.py:1367
Sparse Core Ops, SparseCore 0:
  9.6 84.4 all-gather.3
  95.6 79.8 all-gather.5
  177.1 79.2 all-gather.7
  437.3 74.8 reduce-scatter.4
  527.3 24.9 reduce-scatter.8
  554.5 75.3 reduce-scatter.10
  632.1 65.6 reduce-scatter.6

commit v9 on v8

--- a/solution.py
+++ b/solution.py
@@ -236,7 +236,7 @@
         own[at, :] = (normed * vectors_ref[FIRST_GAIN] + vectors_ref[FIRST_SHIFT]).astype(own.dtype)
 
     gather = Gather(n, own, out_ref, sems)
-    gather.start(lambda: row_blocks(0, own.shape[0], 32, work), d)
+    gather.start(lambda: row_blocks(0, own.shape[0], 64, work), d)
     spread.start()
     for row in range(FIRST_SHIFT + 1, UP_BIAS):
         put(row, 0, flat_refs[row])
@@ -352,7 +352,7 @@
 
     def tiles(self, part, lhs, put):
         start, size = self.parts[part]
-        tile = 256 if size % 256 == 0 and start % 256 == 0 else 128
+        tile = next(tile for tile in (512, 256, 128) if size % tile == 0 and start % tile == 0)
 
         def one(i, carry):
             cols = pl.ds(pl.multiple_of(start + i * tile, tile), tile)

time: 718 us -> 710 us (0.989)
  Pallas kernels: 695 us -> 683 us
  transfers between devices with their start and end apart: 7 -> 7, of which waited for: 2 -> 2; matrix products, arithmetic and copies ran while one was open for 0% -> 0% of each run, Pallas kernels for 71% -> 70%
where the time goes in v9:
time: 710 us; the launch traced here: 708 us
  Pallas kernels  683 us (96%)
  between operations  14.3 us (2%)
  waiting for transfers between devices  8.91 us (1%)
    pallas_call x1, Pallas kernels, expand_back(): pl.pallas_call(functools.partial(expand_back_kernel, n), out_shape=(jax.S...  91.3 us
    pallas_call x1, Pallas kernels, dense_back(): pl.pallas_call(functools.partial(dense_back_kernel, n, length), out_shape...  89.7 us
    pallas_call x1, Pallas kernels, expand(): pl.pallas_call(functools.partial(expand_kernel, n), out_shape=(jax.ShapeD...  85.2 us
    pallas_call x1, Pallas kernels, project_back(): pl.pallas_call(functools.partial(project_back_kernel, n), out_shape=(jax....  85.1 us
    pallas_call x1, Pallas kernels, shrink(): pl.pallas_call(functools.partial(shrink_kernel, n, d), out_shape=(jax.Sha...  82.9 us
    pallas_call x1, Pallas kernels, gather_rows(): pl.pallas_call(functools.partial(gather_kernel, n, d), out_shape=(jax.Sha...  81.4 us
    pallas_call x1, Pallas kernels, dense(): pl.pallas_call(functools.partial(dense_kernel, n), out_shape=(jax.ShapeDt...  80.1 us
    pallas_call x1, Pallas kernels, project_attend(): pl.pallas_call(functools.partial(project_kernel, n, labels.shape[1]), out...  79.2 us
  transfers between devices with their start and end apart: 7, of which 2 were waited for; matrix products, arithmetic and copies ran while one was open for 0% of the time, Pallas kernels for 70%

profile of v9, /device:TPU:0, one launch (start us, length us, event | category | flops | bytes accessed | tf_op | source)
XLA Modules:
  0.0 708.4 jit_solution(4148348723332389964)
XLA Ops:
  7.2 0.7 all-gather.4.cloned.1.call-update
  7.9 0.0 all-gather.6.cloned.1.call-start
  8.0 0.7 all-gather.6.cloned.1.call-update
  8.7 0.0 all-gather.8.cloned.1.call-start
  8.7 0.7 all-gather.8.cloned.1.call-update
  9.4 0.0 reduce-scatter.5.cloned.1.call-start
  9.5 0.8 reduce_sum.9
  10.3 81.4 %gather_rows.1 = (bf16[4096,2048]{1,0:T(8,128)(2,1)}, f32[8,1,2048]{2,1,0:T(1,128)}, bf16[256,2048]{1,0:T(8,128)(2,1)}) custom-call(bf16[512,2048]{1,0:T(8,128)(2,1)} %input_hbm.3, bf16[2048]{0:T(1024)(128)(2,1)} %refs_0_.1, bf16[2048]{0:T(1024)(128)(2,1)} %refs_1_.1, bf16[2048]{0:T(1024)(128)(2,1)} %refs_2_.1, bf16[2048]{0:T(1024)(128)(2,1)} %refs_3_.1, ...), custom_call_target="tpu_custom_call" | custom-call | bytes 280000000 | tf_op jit(solution)/shard_map/gather_rows/pallas_call | solution.py:265
  91.7 0.5 exponential_multiply_fusion.slope_ref
  92.2 0.7 fusion.row_ref
  92.9 79.2 %project_attend.1 = (bf16[4096,2048]{1,0:T(8,128)(2,1)}, bf16[4096,768]{1,0:T(8,128)(2,1)}, bf16[4096,256]{1,0:T(8,128)(2,1)}) custom-call(f32[2]{0:T(128)} %exponential_multiply_fusion.slope_ref, bf16[512,2048]{1,0:T(8,128)(2,1)} %cotangent_hbm.1, bf16[4096,2048]{1,0:T(8,128)(2,1)} %get-tuple-element.58.rows_hbm.left_hbm, ...), custom_call_target="tpu_custom_call" | custom-call | bytes 280000000 | tf_op jit(solution)/shard_map/project_attend/pallas_call | solution.py:695
  172.1 80.1 %dense.1 = (f32[512,2048]{1,0:T(8,128)}, bf16[512,2048]{1,0:T(8,128)(2,1)}) custom-call(bf16[4096,256]{1,0:T(8,128)(2,1)} %get-tuple-element.60.a_hbm.mixed_ref, bf16[256,2048]{1,0:T(8,128)(2,1)} %get-tuple-element.61.w_ref, bf16[512,2048]{1,0:T(8,128)(2,1)} %input_hbm.3, f32[8,1,2048]{2,1,0:T(1,128)} %get-tuple-element.59.vectors_ref), custom_call_target="tpu_custom_call" | custom-call | bytes 280000000 | tf_op jit(solution)/shard_map/dense/pallas_call | solution.py:1066
  252.2 2.7 all-gather.8.cloned.1.call-done.down_ref.w_ref
  255.0 85.2 %expand.1 = (bf16[4096,2048]{1,0:T(8,128)(2,1)}, bf16[4096,1024]{1,0:T(8,128)(2,1)}, bf16[4096,1024]{1,0:T(8,128)(2,1)}, f32[1,1024]{1,0:T(1,128)}) custom-call(bf16[512,2048]{1,0:T(8,128)(2,1)} %get-tuple-element.62.own_ref, bf16[4096,2048]{1,0:T(8,128)(2,1)} %get-tuple-element.63.grad_hbm.rows_hbm, ...), custom_call_target="tpu_custom_call" | custom-call | bytes 280000000 | tf_op jit(solution)/shard_map/expand/pallas_call | solution.py:830
  340.1 91.3 %expand_back.1 = (f32[512,2048]{1,0:T(8,128)}, bf16[512,2048]{1,0:T(8,128)(2,1)}, f32[8,2048]{1,0:T(8,128)}, bf16[1024,2048]{1,0:T(8,128)(2,1)}) custom-call(bf16[4096,1024]{1,0:T(8,128)(2,1)} %get-tuple-element.66.a_hbm.right_hbm, bf16[2048,1024]{1,0:T(8,128)(2,1)} %all-gather.6.cloned.1.call-done.up_ref.w_ref, ...), custom_call_target="tpu_custom_call" | custom-call | bytes 280000000 | tf_op jit(solution)/shard_map/expand_back/pallas_call | solution.py:1085
  431.4 0.2 reduce-scatter.9.cloned.1.call-start
  431.7 89.7 %dense_back.1 = (bf16[4096,768]{1,0:T(8,128)(2,1)}, f32[8,256]{1,0:T(8,128)}, bf16[256,2048]{1,0:T(8,128)(2,1)}, bf16[2048,1024]{1,0:T(8,128)(2,1)}) custom-call(f32[2]{0:T(128)} %exponential_multiply_fusion.slope_ref, bf16[512,2048]{1,0:T(8,128)(2,1)} %get-tuple-element.68.own_ref, bf16[4096,256]{1,0:T(8,128)(2,1)} %get-tuple-element.60.a_hbm.mixed_ref, ...), custom_call_target="tpu_custom_call" | custom-call | bytes 280000000 | tf_op jit(solution)/shard_map/dense_back/pallas_call | solution.py:1227
  521.4 0.0 reduce-scatter.11.cloned.1.call-start
  521.5 0.5 reduce-scatter.11.cloned.1.call-update
  522.0 0.0 reduce-scatter.7.cloned.1.call-start
  522.1 85.1 %project_back.1 = (f32[512,2048]{1,0:T(8,128)}, f32[8,2048]{1,0:T(8,128)}, bf16[2048,768]{1,0:T(8,128)(2,1)}) custom-call(bf16[4096,768]{1,0:T(8,128)(2,1)} %get-tuple-element.72.a_hbm, bf16[2048,768]{1,0:T(8,128)(2,1)} %all-gather.4.cloned.1.call-done.w_ref, bf16[512,2048]{1,0:T(8,128)(2,1)} %input_hbm.3, f32[512,2048]{1,0:T(8,128)} %get-tuple-element.73.grad_hbm, ...), custom_call_target="tpu_custom_call" | custom-call | bytes 280000000 | tf_op jit(solution)/shard_map/project_back/pallas_call | solution.py:1344
  607.2 82.9 %shrink.1 = (bf16[512,2048]{1,0:T(8,128)(2,1)}, f32[8,2048]{1,0:T(8,128)}, f32[8,1024]{1,0:T(8,128)}) custom-call(bf16[4096,1024]{1,0:T(8,128)(2,1)} %get-tuple-element.64.act_hbm.a_hbm, bf16[1024,2048]{1,0:T(8,128)(2,1)} %all-gather.8.cloned.1.call-done.down_ref.w_ref, f32[512,2048]{1,0:T(8,128)} %get-tuple-element.65.residual_hbm, ...), custom_call_target="tpu_custom_call" | custom-call | bytes 280000000 | tf_op jit(solution)/shard_map/shrink/pallas_call | solution.py:1292
  690.2 3.5 reduce-scatter.7.cloned.1.call-done.refs_2_
  693.6 7.9 %finish.1 = (bf16[512,2048]{1,0:T(8,128)(2,1)}, f32[512,2048]{1,0:T(8,128)}, f32[512,768]{1,0:T(8,128)}, f32[256,512]{1,0:T(8,128)}, f32[512,1024]{1,0:T(8,128)}...) custom-call(bf16[512,2048]{1,0:T(8,128)(2,1)} %get-tuple-element.78., ...), custom_call_target="tpu_custom_call" | custom-call | tf_op jit(solution)/shard_map/finish/pallas_call | solution.py:1396
  (12 shorter events, 0.2 us)
Async XLA Ops:
  7.2 85.0 %copy-start = (s32[4096]{0:T(1024)S(1)}, s32[4096]{0:T(1024)}, u32[]{:S(2)}) copy-start(s32[4096]{0:T(1024)} %param.31) | copy-start | bytes 49156
  7.2 85.7 %all-gather.4.cloned.1.call-start = ((), (), s32[]{:S(2)}) async-start(), calls=%async_computation.4 | async-start | bytes 3932160 | tf_op jit(solution)/shard_map/all_gather | solution.py:1451
  7.9 244.3 %all-gather.6.cloned.1.call-start = ((), (), s32[]{:S(2)}) async-start(), calls=%async_computation.5 | async-start | bytes 5242880 | tf_op jit(solution)/shard_map/all_gather | solution.py:1452
  8.7 246.3 %all-gather.8.cloned.1.call-start = ((), (), s32[]{:S(2)}) async-start(), calls=%async_computation.6 | async-start | bytes 5242880 | tf_op jit(solution)/shard_map/all_gather | solution.py:1453
  9.4 512.7 %reduce-scatter.5.cloned.1.call-start = ((), (), s32[]{:S(2)}) async-start(), calls=%async_computation.7 | async-start | bytes 5242880 | tf_op jit(solution)/shard_map/reduce_scatter | solution.py:1367
  431.4 258.7 %reduce-scatter.9.cloned.1.call-start = ((), (), s32[]{:S(2)}) async-start(), calls=%async_computation.9 | async-start | bytes 1310720 | tf_op jit(solution)/shard_map/reduce_scatter | solution.py:1367
  521.4 168.7 %reduce-scatter.11.cloned.1.call-start = ((), (), s32[]{:S(2)}) async-start(), calls=%async_computation.10 | async-start | bytes 5242880 | tf_op jit(solution)/shard_map/reduce_scatter | solution.py:1367
  522.0 171.6 %reduce-scatter.7.cloned.1.call-start = ((), (), s32[]{:S(2)}) async-start(), calls=%async_computation.8 | async-start | bytes 3932160 | tf_op jit(solution)/shard_map/reduce_scatter | solution.py:1367
Sparse Core Ops, SparseCore 0:
  9.6 82.9 all-gather.3
  94.1 79.9 all-gather.5
  175.7 79.2 all-gather.7
  431.6 74.8 reduce-scatter.4
  521.5 25.0 reduce-scatter.8
  548.8 77.4 reduce-scatter.10
  628.6 65.0 reduce-scatter.6
